TPU v7x, 32 devices: a whole 2x2x4 slice. The times are simulated.
32 devices in a mesh: doc: 4 (over y, x), seq: 8 (over z, core).
Axes of the slice: x: 2, y: 2, z: 4, core: 2. Of those that a mesh axis runs over, the one named last changes fastest.
Arguments:
- queries: bfloat16 [12288, 2048], P(('doc', 'seq')), parts along dimension 0, may hold values from -120 to 120
- keys: bfloat16 [12288, 2048], P(('doc', 'seq')), parts along dimension 0, may hold values from -4.1 to 4.1
- values: bfloat16 [12288, 2048], P(('doc', 'seq')), parts along dimension 0, may hold values from -6 to 6
- global_positions: int32 [256], P('doc'), parts along dimension 0, may hold values from 0 to 3070, as said below
- score_weight: float32 [2048], replicated, may hold values from -0.125 to 0.125
Outputs:
- token_scores: float32 [12288], P(('doc', 'seq')), parts along dimension 0
There are 4 independent parts, one for each index of `doc`. A program takes and returns all parts, laid end to end along the dimension named above; an argument that names none is the same for every part. Nothing has to cross between parts.
Inputs may be any that keep to these rules, and one draw needn't show every extreme that they name: `global_positions`: 64 distinct positions in increasing order; the first is 0 and the last is 3070.
All inputs are finite; a program needn't handle non-finite values.
Results may differ from a plain program's by a relative error of at most 0.0023.
Values may be sent and summed in bfloat16 or wider, within the bound.
No kernel may reach another device: no remote copies, remote signals or barrier semaphores. Data moves between devices by JAX's collectives and lax.ppermute only.
A program may use at most 64 MiB of HBM per device.

v0:
```python
import functools
import math

import jax
import jax.numpy as jnp
from jax import lax
from jax.experimental import pallas as pl
from jax.experimental.pallas import tpu as pltpu
from jax.sharding import PartitionSpec as P

HEADS = 16
BLK = 64
CORES = 2
LANES = 128
NEG = -1e30
LOG2E = math.log2(math.e)
STAT_ROWS = 16


def pieces(x):
    hi = x.astype(jnp.bfloat16)
    rest = x - hi.astype(jnp.float32)
    mid = rest.astype(jnp.bfloat16)
    low = (rest - mid.astype(jnp.float32)).astype(jnp.bfloat16)
    return hi, mid, low


def dot_t(a, b):
    return lax.dot_general(a, b, (((1,), (1,)), ((), ())), preferred_element_type=jnp.float32)


def dot_n(a, b):
    return lax.dot_general(a, b, (((1,), (0,)), ((), ())), preferred_element_type=jnp.float32)


def put_message(out_ref, pair, out, peak, total):
    rows = out.shape[0]
    out_ref[pair, :rows, :] = out.astype(jnp.bfloat16)
    stats = [p.astype(jnp.float32) for p in (*pieces(peak), *pieces(total))]
    row = lax.broadcasted_iota(jnp.int32, (STAT_ROWS, LANES), 0)
    block = jnp.zeros((STAT_ROWS, LANES), jnp.float32)
    for i, stat in enumerate(stats):
        block = jnp.where(row == i, jnp.broadcast_to(stat, block.shape), block)
    out_ref[pair, rows:, :] = block.astype(jnp.bfloat16)


def get_message(ref, pair, head_size):
    out = ref[pair, :head_size, :].astype(jnp.float32)
    stats = ref[pair, head_size:, :].astype(jnp.float32)
    peak = stats[0:1] + stats[1:2] + stats[2:3]
    total = stats[3:4] + stats[4:5] + stats[5:6]
    return out, peak, total


def merged(a, b, scale2):
    out_a, peak_a, total_a = a
    out_b, peak_b, total_b = b
    peak = jnp.maximum(peak_a, peak_b)
    weight_a = jnp.exp2((peak_a - peak) * scale2) * total_a
    weight_b = jnp.exp2((peak_b - peak) * scale2) * total_b
    total = weight_a + weight_b
    inv = 1.0 / total
    return out_a * (weight_a * inv) + out_b * (weight_b * inv), peak, total


def device_place():
    index = lax.axis_index("seq")
    return index % CORES, index // CORES


def column_of(row):
    wide = jnp.concatenate([row, row], axis=1).astype(jnp.float32)
    return jnp.transpose(jnp.broadcast_to(wide, (LANES, LANES)))[: row.shape[1]]


def pick(x_ref, hit, out_ref, at, cols):
    contract = (((0,), (0,)), ((), ()))
    picked = lax.dot_general(hit, x_ref[:, cols], contract, preferred_element_type=jnp.float32)
    out_ref[at : at + hit.shape[1], :] = picked.astype(jnp.bfloat16)


def own_positions(pos_ref, rows):
    core, chip = device_place()
    row = (chip * CORES + core) * rows + lax.broadcasted_iota(jnp.int32, (rows, pos_ref.shape[1]), 0)
    return jnp.where(row == pos_ref[...], 1.0, 0.0).astype(jnp.bfloat16)


def select_q_kernel(half, pos_hbm, q_hbm, own_ref, sib_ref, pos_ref, q_ref, sems):
    core, _ = device_place()
    copies = [pltpu.make_async_copy(pos_hbm, pos_ref, sems.at[2])]
    for slot, which in ((0, 1 - core), (1, core)):
        cols = pl.ds(pl.multiple_of(which * half, half), half)
        copies.append(pltpu.make_async_copy(q_hbm.at[:, cols], q_ref.at[slot], sems.at[slot]))
    for copy in copies:
        copy.start()
    copies[0].wait()
    hit = own_positions(pos_ref, q_ref.shape[1])
    for slot, out_ref in ((0, sib_ref), (1, own_ref)):
        copies[1 + slot].wait()
        pick(q_ref.at[slot], hit, out_ref, 0, slice(None))


def select_kv_kernel(half, pos_ref, k_ref, v_ref, q_ref, own_ref, edge_ref, sib_ref):
    rows = k_ref.shape[0]
    glob = pos_ref.shape[1]
    hit = own_positions(pos_ref, rows)
    core, _ = device_place()
    block = pl.ds(pl.multiple_of(core * (rows - BLK), BLK), BLK)
    mine = pl.ds(pl.multiple_of(core * half, half), half)
    theirs = pl.ds(pl.multiple_of((1 - core) * half, half), half)
    start = 2 * glob + 2 * BLK
    for i, x_ref in enumerate((k_ref, v_ref)):
        pick(x_ref, hit, sib_ref, i * glob, theirs)
        sib_ref[2 * glob + i * BLK : 2 * glob + (i + 1) * BLK, :] = x_ref[block, theirs]
        sib_ref[start + i * rows : start + (i + 1) * rows, :] = x_ref[:, theirs]
        pick(x_ref, hit, own_ref, i * glob, mine)
        edge_ref[i * BLK : (i + 1) * BLK, :] = x_ref[block, mine]
    sib_ref[start + 2 * rows :, :] = q_ref[:, theirs]


def split_kernel(a_ref, b_ref, sum_ref, rest_ref):
    count = sum_ref.shape[0]
    sum_ref[...] = a_ref[...] + b_ref[:count, :]
    rest_ref[...] = b_ref[count : count + rest_ref.shape[0], :]


def add_kernel(a_ref, b_ref, out_ref):
    count = out_ref.shape[0]
    out_ref[...] = a_ref[:count, :] + b_ref[:count, :]


def prepare_kernel(q_own_ref, k_own_ref, v_own_ref, sib_ref, k_ref, v_t_ref, q_t_ref, v_all):
    rows = k_own_ref.shape[0]
    half = k_ref.shape[1]
    core, _ = device_place()
    cols = pl.ds(pl.multiple_of(core * half, half), half)
    own = pl.multiple_of(core * rows, BLK)
    sib = pl.multiple_of((1 - core) * rows, BLK)
    start = sib_ref.shape[0] - 3 * rows
    zero = jnp.zeros((BLK, half), jnp.bfloat16)
    for i, (ref, own_ref) in enumerate(((k_ref, k_own_ref), (v_all, v_own_ref))):
        ref[:BLK, :] = zero
        ref[BLK + CORES * rows :, :] = zero
        ref[pl.ds(pl.multiple_of(own + BLK, BLK), rows), :] = own_ref[:, cols]
        ref[pl.ds(pl.multiple_of(sib + BLK, BLK), rows), :] = sib_ref[start + i * rows : start + (i + 1) * rows, :]

    def turn(head, carry):
        lanes = pl.ds(pl.multiple_of(head * LANES, LANES), LANES)
        v_t_ref[lanes, :] = jnp.transpose(v_all[:, lanes])
        source = pl.ds(pl.multiple_of(core * half + head * LANES, LANES), LANES)
        q_t_ref[lanes, pl.ds(pl.multiple_of(own, LANES), rows)] = jnp.transpose(q_own_ref[:, source])
        q_t_ref[lanes, pl.ds(pl.multiple_of(sib, LANES), rows)] = jnp.transpose(sib_ref[start + 2 * rows :, lanes])
        return carry

    lax.fori_loop(0, half // LANES, turn, 0)


def global_kernel(scale2, q_a_ref, q_b_ref, k_ref, v_t_ref, out_ref, s_buf, e_buf):
    glob, half = q_a_ref.shape
    head_size = LANES
    pairs = half // (2 * head_size)
    tokens = k_ref.shape[0] - 2 * BLK
    row = lax.broadcasted_iota(jnp.int32, (2 * glob, 2 * head_size), 0)
    col = lax.broadcasted_iota(jnp.int32, (2 * glob, 2 * head_size), 1)
    keep = (row < glob) == (col < head_size)
    lane = lax.broadcasted_iota(jnp.int32, (head_size, LANES), 1)
    for pair in range(pairs):
        cols = slice(2 * pair * head_size, 2 * (pair + 1) * head_size)
        q = q_a_ref[:, cols] + q_b_ref[:, cols]
        doubled = jnp.concatenate([q, q], axis=0)
        diag = jnp.where(keep, doubled, jnp.zeros_like(doubled))
        s_buf[pair] = dot_t(k_ref[BLK : BLK + tokens, cols], diag)
    stats = []
    for pair in range(pairs):
        s = s_buf[pair]
        peak = jnp.max(s, axis=0, keepdims=True)
        e = jnp.exp2((s - peak) * scale2)
        stats.append((peak, jnp.sum(e, axis=0, keepdims=True)))
        zero = jnp.zeros((BLK, LANES), jnp.bfloat16)
        e_buf[pair, :BLK] = zero
        e_buf[pair, BLK + tokens :] = zero
        e_buf[pair, BLK : BLK + tokens] = e.astype(jnp.bfloat16)
    for pair in range(pairs):
        rows = slice(2 * pair * head_size, 2 * (pair + 1) * head_size)
        acc = dot_n(v_t_ref[rows, :], e_buf[pair])
        peak, total = stats[pair]
        out = jnp.where(lane < glob, acc[:head_size], acc[head_size:]) / total
        put_message(out_ref, pair, out, peak, total)


def merge_kernel(scale2, a_ref, b_ref, out_ref):
    head_size = a_ref.shape[1] - STAT_ROWS
    for pair in range(a_ref.shape[0]):
        a = get_message(a_ref, pair, head_size)
        b = get_message(b_ref, pair, head_size)
        put_message(out_ref, pair, *merged(a, b, scale2))


def final_kernel(scale2, a_ref, b_ref, w_ref, pos_ref, win_ref, own_ref, sib_ref):
    pairs = a_ref.shape[0]
    head_size = a_ref.shape[1] - STAT_ROWS
    glob = pos_ref.shape[1]
    core, chip = device_place()
    upper = lax.broadcasted_iota(jnp.int32, (LANES, head_size), 0) < glob
    lin = jnp.zeros((1, LANES), jnp.float32)
    sq = jnp.zeros((1, LANES), jnp.float32)
    for pair in range(pairs):
        a = get_message(a_ref, pair, head_size)
        b = get_message(b_ref, pair, head_size)
        out, _, _ = merged(a, b, scale2)
        w_a = w_ref[pl.ds(core * 2 * pairs + 2 * pair, 1), :]
        w_b = w_ref[pl.ds(core * 2 * pairs + 2 * pair + 1, 1), :]
        w = jnp.transpose(jnp.where(upper, w_a, w_b))
        lin = lin + jnp.sum(out * w, axis=0, keepdims=True)
        sq = sq + jnp.sum(out * out, axis=0, keepdims=True)
    lin = lin + pltpu.roll(lin, glob, 1)
    sq = sq + pltpu.roll(sq, glob, 1)
    parts = [p.astype(jnp.float32) for p in (*pieces(lin), *pieces(sq))] + [jnp.ones((1, LANES), jnp.float32)]
    row = lax.broadcasted_iota(jnp.int32, (16, LANES), 0)
    table = jnp.zeros((16, LANES), jnp.float32)
    for i, part in enumerate(parts):
        table = jnp.where(row == i, jnp.broadcast_to(part, table.shape), table)
    table = table.astype(jnp.bfloat16)[:, :glob]
    pos = column_of(pos_ref[...])
    n_pairs = win_ref.shape[1]
    each = n_pairs // CORES
    for out_ref, which in ((own_ref, core), (sib_ref, 1 - core)):
        for j in range(each):
            pair = which * each + j
            token = (chip * n_pairs + pair) * LANES + lax.broadcasted_iota(jnp.int32, (glob, LANES), 1)
            hit = jnp.where(pos == token.astype(jnp.float32), 1.0, 0.0).astype(jnp.bfloat16)
            placed = dot_n(table, hit)
            is_glob = placed[6:7] > 0.5
            for i in (0, 1):
                value = placed[3 * i : 3 * i + 1] + placed[3 * i + 1 : 3 * i + 2] + placed[3 * i + 2 : 3 * i + 3]
                out_ref[i, j : j + 1, :] = jnp.where(is_glob, value, win_ref[i, pl.ds(pair, 1), :])


def near_kernel(scale2, q_t_ref, k_ref, v_t_ref, edge_a_ref, edge_b_ref, acc_ref, stat_ref, s_buf, e_buf, edges):
    half, tokens = q_t_ref.shape
    n_pairs = tokens // LANES
    core, chip = device_place()
    chips = lax.axis_size("seq") // CORES
    left = lax.broadcasted_iota(jnp.int32, (BLK, LANES), 1) < BLK
    wide_left = lax.broadcasted_iota(jnp.int32, (LANES, LANES), 1) < BLK
    first_bias = jnp.where(left & (chip == 0), NEG, 0.0)
    last_bias = jnp.where((~left) & (chip == chips - 1), NEG, 0.0)

    @pl.when(core == 1)
    def _():
        edges[0] = edge_a_ref[...]
        edges[1] = edge_b_ref[...]

    @pl.when(core == 0)
    def _():
        edges[0] = edge_b_ref[...]
        edges[1] = edge_a_ref[...]

    def one_head(head, carry):
        cols = pl.ds(pl.multiple_of(head * LANES, LANES), LANES)
        for j in range(n_pairs):
            if j == 0:
                k = jnp.concatenate([edges[0, :BLK, cols], k_ref[BLK : 4 * BLK, cols]], axis=0)
            elif j == n_pairs - 1:
                k = jnp.concatenate([k_ref[j * LANES : j * LANES + 3 * BLK, cols], edges[1, :BLK, cols]], axis=0)
            else:
                k = k_ref[j * LANES : (j + 2) * LANES, cols]
            s_buf[j] = dot_n(k, q_t_ref[cols, j * LANES : (j + 1) * LANES])
        peaks, totals = [], []
        for j in range(n_pairs):
            ends = jnp.where(left, s_buf[j, :BLK], s_buf[j, 3 * BLK :])
            if j == 0:
                ends = ends + first_bias
            if j == n_pairs - 1:
                ends = ends + last_bias
            mid = s_buf[j, BLK : 3 * BLK]
            peak = jnp.max(jnp.maximum(ends, jnp.maximum(mid[:BLK], mid[BLK:])), axis=0, keepdims=True)
            e_ends = jnp.exp2((ends - peak) * scale2)
            e_mid = jnp.exp2((mid - peak) * scale2)
            zero = jnp.zeros_like(e_ends)
            e_buf[j, :BLK] = jnp.where(left, e_ends, zero).astype(jnp.bfloat16)
            e_buf[j, BLK : 3 * BLK] = e_mid.astype(jnp.bfloat16)
            e_buf[j, 3 * BLK :] = jnp.where(left, zero, e_ends).astype(jnp.bfloat16)
            peaks.append(peak)
            totals.append(jnp.sum(e_ends + e_mid[:BLK] + e_mid[BLK:], axis=0, keepdims=True))
        stat_ref[head, 0] = jnp.concatenate(peaks, axis=0)
        stat_ref[head, 1] = jnp.concatenate(totals, axis=0)
        turned = jnp.transpose(jnp.concatenate([edges[0, BLK:, cols], edges[1, BLK:, cols]], axis=0))
        for j in range(n_pairs):
            v_0 = v_t_ref[cols, j * LANES : (j + 1) * LANES]
            v_1 = v_t_ref[cols, (j + 1) * LANES : (j + 2) * LANES]
            if j == 0:
                v_0 = jnp.where(wide_left, turned, v_0)
            if j == n_pairs - 1:
                v_1 = jnp.where(wide_left, v_1, turned)
            acc_ref[head, j] = dot_n(jnp.concatenate([v_0, v_1], axis=1), e_buf[j])
        return carry

    lax.fori_loop(0, half // LANES, one_head, 0)


def far_kernel(
    scale2, q_t_ref, acc_ref, stat_ref, kv_a_ref, kv_b_ref, w_ref, pos_ref, out_ref, s_buf, e_buf, bias, w_cols
):
    half, tokens = q_t_ref.shape
    glob = pos_ref.shape[1]
    heads = half // LANES
    n_pairs = tokens // LANES
    core, chip = device_place()
    glob_block = column_of(pos_ref[...] // BLK)
    for j in range(n_pairs):
        block = (chip * n_pairs + j) * (LANES // BLK) + lax.broadcasted_iota(jnp.int32, (glob, LANES), 1) // BLK
        bias[j] = jnp.where(jnp.abs(glob_block - block.astype(jnp.float32)) > 1.5, 0.0, NEG)
    for head in range(heads):
        row = w_ref[pl.ds(core * heads + head, 1), :]
        w_cols[head] = jnp.transpose(jnp.broadcast_to(row, (LANES, LANES)))

    def one_head(head, carry):
        cols = pl.ds(pl.multiple_of(head * LANES, LANES), LANES)
        kg = kv_a_ref[:glob, cols] + kv_b_ref[:glob, cols]
        for j in range(n_pairs):
            s_buf[j] = dot_n(kg, q_t_ref[cols, j * LANES : (j + 1) * LANES])
        near_peaks = stat_ref[head, 0]
        near_totals = stat_ref[head, 1]
        near_weights, inverses = [], []
        for j in range(n_pairs):
            far = s_buf[j] + bias[j]
            near_peak = near_peaks[j : j + 1]
            peak = jnp.maximum(jnp.max(far, axis=0, keepdims=True), near_peak)
            e_far = jnp.exp2((far - peak) * scale2)
            e_buf[j] = e_far.astype(jnp.bfloat16)
            near_weight = jnp.exp2((near_peak - peak) * scale2)
            total = near_totals[j : j + 1] * near_weight + jnp.sum(e_far, axis=0, keepdims=True)
            near_weights.append(near_weight)
            inverses.append(1.0 / total)
        vg_t = jnp.transpose(kv_a_ref[glob:, cols] + kv_b_ref[glob:, cols])
        w = w_cols[head]
        lins, sqs = [], []
        for j in range(n_pairs):
            acc = acc_ref[head, j] * near_weights[j] + dot_n(vg_t, e_buf[j])
            lins.append(jnp.sum(acc * w, axis=0, keepdims=True) * inverses[j])
            sqs.append(jnp.sum(acc * acc, axis=0, keepdims=True) * (inverses[j] * inverses[j]))
        lin, sq = carry
        return lin + jnp.concatenate(lins, axis=0), sq + jnp.concatenate(sqs, axis=0)

    none = jnp.zeros((n_pairs, LANES), jnp.float32)
    lin, sq = lax.fori_loop(0, heads, one_head, (none, none))
    out_ref[0] = lin
    out_ref[1] = sq


def call(kernel, name, outs, args, scratch=(), micros=0.0, from_hbm=False):
    spec = pl.BlockSpec(memory_space=pltpu.VMEM)
    source = pltpu.HBM if from_hbm else pltpu.VMEM
    single = not isinstance(outs, list)
    shapes = [outs] if single else outs
    result = pl.pallas_call(
        kernel,
        in_specs=[pl.BlockSpec(memory_space=source)] * len(args),
        out_specs=[spec] * len(shapes),
        out_shape=[pltpu.VMEM(shape, dtype) for shape, dtype in shapes],
        scratch_shapes=[pltpu.VMEM(*x) if isinstance(x, tuple) else x for x in scratch],
        compiler_params=pltpu.CompilerParams(vmem_limit_bytes=16 * 1024 * 1024),
        cost_estimate=pl.CostEstimate(flops=int(micros * 1e9) + 1, transcendentals=0, bytes_accessed=1),
        name=name,
    )(*[pltpu.with_memory_space_constraint(x, source) for x in args])
    return result[0] if single else result


def on_device(queries, keys, values, global_positions, score_weight):
    rows, model_width = queries.shape
    head_size = model_width // HEADS
    half = model_width // CORES
    half_heads = HEADS // CORES
    glob = global_positions.shape[0]
    seq_count = lax.axis_size("seq")
    chips = seq_count // CORES
    scale2 = head_size ** (-0.5) * LOG2E
    bf16 = jnp.bfloat16
    f32 = jnp.float32
    rounds = int(math.log2(chips))
    tokens = CORES * rows
    n_pairs = tokens // LANES

    def swap(x, mask):
        return lax.ppermute(x, "seq", [(i, i ^ mask) for i in range(seq_count)])

    def shift(x, even, odd):
        moves = [(i, i + (odd if i % CORES else even) * CORES) for i in range(seq_count)]
        return lax.ppermute(x, "seq", [(i, to) for i, to in moves if 0 <= to < seq_count])

    def after(arrays, *others):
        return lax.optimization_barrier((*arrays, *others))[: len(arrays)]

    row_positions = global_positions.reshape(1, glob)
    small = ((glob, half), bf16)
    pair_of = ((2 * glob, half), bf16)
    edge = ((2 * BLK, half), bf16)
    q_own, q_sib = call(
        functools.partial(select_q_kernel, half),
        "select_queries",
        [small, small],
        [row_positions, queries],
        [((1, glob), jnp.int32), ((CORES, rows, half), bf16), pltpu.SemaphoreType.DMA((3,))],
        from_hbm=True,
    )
    keys, values, queries = after((keys, values, queries), q_sib)
    kv_own, edge_own, kv_sib = call(
        functools.partial(select_kv_kernel, half),
        "select_keys_values",
        [pair_of, edge, ((2 * glob + 2 * BLK + 3 * rows, half), bf16)],
        [row_positions, keys, values, queries],
    )
    q_near = call(add_kernel, "add_queries", small, [q_own, swap(q_sib, 1)])
    kv_sib = after((kv_sib,), q_near)[0]
    sib_recv = swap(kv_sib, 1)
    for r in range(1, rounds):
        q_near = call(add_kernel, "add_queries", small, [q_near, swap(q_near, 1 << r)])
    q_far = swap(q_near, 1 << rounds)

    k_all, v_t, q_t = call(
        prepare_kernel,
        "prepare",
        [((tokens + 2 * BLK, half), bf16), ((half, tokens + 2 * BLK), bf16), ((half, tokens), bf16)],
        [queries, keys, values, sib_recv],
        [((tokens + 2 * BLK, half), bf16)],
        micros=1.6,
    )
    kv_own, edge_own, sib_recv = after((kv_own, edge_own, sib_recv), k_all, q_near)
    edge_a = shift(edge_own, -1, 1)
    kv_near, edge_recv = call(split_kernel, "join_keys_values", [pair_of, edge], [kv_own, sib_recv])
    edge_b = shift(edge_recv, 1, -1)
    for r in range(1, rounds):
        kv_near = call(add_kernel, "add_keys_values", pair_of, [kv_near, swap(kv_near, 1 << r)])
    kv_far = swap(kv_near, 1 << rounds)

    part = ((half_heads // 2, head_size + STAT_ROWS, LANES), bf16)
    message = call(
        functools.partial(global_kernel, scale2),
        "global_partial",
        part,
        [q_near, q_far, k_all, v_t],
        [((half_heads // 2, tokens, LANES), f32), ((half_heads // 2, tokens + 2 * BLK, LANES), bf16)],
    )
    for r in range(1, rounds):
        message = call(
            functools.partial(merge_kernel, scale2), "merge_partial", part, [message, swap(message, 1 << r)]
        )
    message_far = swap(message, 1 << rounds)

    weights = score_weight.reshape(HEADS, head_size)
    near_acc, near_stat = call(
        functools.partial(near_kernel, scale2),
        "near_attention",
        [((half_heads, n_pairs, head_size, LANES), f32), ((half_heads, 2, n_pairs, LANES), f32)],
        [q_t, k_all, v_t, edge_a, edge_b],
        [((n_pairs, 4 * BLK, LANES), f32), ((n_pairs, 4 * BLK, LANES), bf16), ((2, 2 * BLK, half), bf16)],
        micros=4.0,
    )
    window = call(
        functools.partial(far_kernel, scale2),
        "far_attention",
        ((2, n_pairs, LANES), f32),
        [q_t, near_acc, near_stat, kv_near, kv_far, weights, row_positions],
        [
            ((n_pairs, glob, LANES), f32),
            ((n_pairs, glob, LANES), bf16),
            ((n_pairs, glob, LANES), f32),
            ((half_heads, LANES, LANES), f32),
        ],
        micros=2.0,
    )
    share = ((2, n_pairs // CORES, LANES), f32)
    mine, theirs = call(
        functools.partial(final_kernel, scale2),
        "place_global",
        [share, share],
        [message, message_far, weights, row_positions, window],
    )
    theirs = swap(theirs, 1)
    lin = mine[0] + theirs[0]
    sq = mine[1] + theirs[1]
    return (lin * lax.rsqrt(sq * (1.0 / model_width) + 1e-06)).reshape(rows)


def solution(mesh):
    placed = (
        P(("doc", "seq"), None),
        P(("doc", "seq"), None),
        P(("doc", "seq"), None),
        P("doc"),
        P(),
    )
    return jax.shard_map(
        on_device, mesh=mesh, in_specs=placed, out_specs=P(("doc", "seq")), check_vma=False
    )
```

profile of v0, /device:TPU:0, one launch (start us, length us, event | category | flops | bytes accessed | tf_op | source)
XLA Modules:
  0.0 61.7 jit_solution(5355139567134496184)
XLA Ops:
  0.0 0.0 copy-start
  0.0 1.8 %select_queries.1 = (bf16[64,1024]{1,0:T(8,128)(2,1)S(1)}, bf16[64,1024]{1,0:T(8,128)(2,1)S(1)}) custom-call(s32[1,64]{1,0:T(1,128)} %bitcast.6, bf16[384,2048]{1,0:T(8,128)(2,1)} %q_own_ref), custom_call_target="tpu_custom_call" | custom-call | flops 1 | bytes 1 | tf_op jit(solution)/shard_map/select_queries/pallas_call | solution.py:357
  1.8 0.5 collective-permute-start
  2.4 0.0 copy-done
  2.4 0.0 copy-start.1
  2.4 1.4 %copy-done.1 = bf16[384,2048]{1,0:T(8,128)(2,1)S(1)} copy-done((bf16[384,2048]{1,0:T(8,128)(2,1)S(1)}, bf16[384,2048]{1,0:T(8,128)(2,1)}, u32[]{:S(2)}) %copy-start.1) | copy-done | bytes 1572888
  3.8 0.0 copy-start.3
  3.8 1.4 %copy-done.3 = bf16[384,2048]{1,0:T(8,128)(2,1)S(1)} copy-done((bf16[384,2048]{1,0:T(8,128)(2,1)S(1)}, bf16[384,2048]{1,0:T(8,128)(2,1)}, u32[]{:S(2)}) %copy-start.3) | copy-done | bytes 1572888
  5.2 0.0 copy-start.6
  5.2 0.7 %copy-done.6 = s32[64]{0:T(128)S(1)} copy-done((s32[64]{0:T(128)S(1)}, s32[64]{0:T(128)}, u32[]{:S(2)}) %copy-start.6) | copy-done | bytes 280
  5.8 0.0 copy-start.2
  5.8 0.0 copy-start.4
  5.8 0.8 %select_keys_values.1 = (bf16[128,1024]{1,0:T(8,128)(2,1)S(1)}, bf16[128,1024]{1,0:T(8,128)(2,1)S(1)}, bf16[1408,1024]{1,0:T(8,128)(2,1)S(1)}) custom-call(s32[1,64]{1,0:T(1,128)S(1)} %bitcast.7, bf16[384,2048]{1,0:T(8,128)(2,1)S(1)} %copy-done.1, bf16[384,2048]{1,0:T(8,128)(2,1)S(1)} %copy-done.3, bf16[384,2048]{1,0:T(8,128)(2,1)S(1)} %copy-done), custom_call_target="tpu_custom_call" | custom-call | flops 1 | bytes 1 | tf_op jit(solution)/shard_map/select_keys_values/pallas_call | solution.py:357
  6.7 0.0 collective-permute-done.b_ref
  6.7 0.1 collective-permute-start.3
  6.8 3.0 %collective-permute-start.1 = (bf16[64,1024]{1,0:T(8,128)(2,1)S(1)}, bf16[64,1024]{1,0:T(8,128)(2,1)S(1)}, u32[]{:S(2)}, u32[]{:S(2)}) collective-permute-start(bf16[64,1024]{1,0:T(8,128)(2,1)S(1)} %add_queries.2.a_ref), channel_id=1, source_target_pairs={{0,2},{1,3},{2,0},{3,1},{4,6},{5,7},{6,4},{7,5},{8,10},{9,11},{10,... | collective-permute-start | bytes 393224 | tf_op jit(solution)/shard_map/ppermute | solution.py:386
  9.9 3.7 %collective-permute-done.1.b_ref = bf16[64,1024]{1,0:T(8,128)(2,1)S(1)} collective-permute-done((bf16[64,1024]{1,0:T(8,128)(2,1)S(1)}, bf16[64,1024]{1,0:T(8,128)(2,1)S(1)}, u32[]{:S(2)}, u32[]{:S(2)}) %collective-permute-start.1) | collective-permute-done | bytes 131104 | tf_op jit(solution)/shard_map/ppermute | solution.py:386
  13.6 2.8 %collective-permute-start.2 = (bf16[64,1024]{1,0:T(8,128)(2,1)S(1)}, bf16[64,1024]{1,0:T(8,128)(2,1)S(1)}, u32[]{:S(2)}, u32[]{:S(2)}) collective-permute-start(bf16[64,1024]{1,0:T(8,128)(2,1)S(1)} %add_queries.3.q_a_ref), channel_id=1, source_target_pairs={{0,4},{1,5},{2,6},{3,7},{4,0},{5,1},{6,2},{7,3},{8,12},{9,13},{10,... | collective-permute-start | bytes 393224 | tf_op jit(solution)/shard_map/ppermute | solution.py:386
  16.4 0.0 collective-permute-done.3.sib_ref.b_ref
  16.4 0.0 copy-done.2
  16.4 0.0 copy-done.4
  16.4 1.6 %prepare.1 = (bf16[896,1024]{1,0:T(8,128)(2,1)S(1)}, bf16[1024,896]{1,0:T(8,128)(2,1)S(1)}, bf16[1024,768]{1,0:T(8,128)(2,1)S(1)}) custom-call(bf16[384,2048]{1,0:T(8,128)(2,1)S(1)} %copy-done, bf16[384,2048]{1,0:T(8,128)(2,1)S(1)} %copy-done.2, bf16[384,2048]{1,0:T(8,128)(2,1)S(1)} %copy-done.4, bf16[1408,1024]{1,0:T(8,128)(2,1)S(1)} %collective-permute-done.3.sib_ref.b_ref), custom_call_target="tpu_custom_call" | custom-call | flops 1600000000 | bytes 1 | tf_op jit(solution)/shard_map/prepare/pallas_call | solution.py:357
  18.1 1.6 %collective-permute-start.8 = (bf16[128,1024]{1,0:T(8,128)(2,1)S(1)}, bf16[128,1024]{1,0:T(8,128)(2,1)S(1)}, u32[]{:S(2)}, u32[]{:S(2)}) collective-permute-start(bf16[128,1024]{1,0:T(8,128)(2,1)S(1)} %get-tuple-element.44.a_ref), channel_id=1, source_target_pairs={{0,2},{1,3},{2,0},{3,1},{4,6},{5,7},{6,4},{7,5},{8,10},{9,11},{10,... | collective-permute-start | bytes 786440 | tf_op jit(solution)/shard_map/ppermute | solution.py:386
  19.8 1.3 %collective-permute-start.6 = (bf16[128,1024]{1,0:T(8,128)(2,1)S(1)}, bf16[128,1024]{1,0:T(8,128)(2,1)S(1)}, u32[]{:S(2)}, u32[]{:S(2)}) collective-permute-start(bf16[128,1024]{1,0:T(8,128)(2,1)S(1)} %get-tuple-element.38), channel_id=1, source_target_pairs={{1,3},{2,0},{3,5},{4,2},{5,7},{6,4},{9,11},{10,8},{11,13},{12,10},... | collective-permute-start | bytes 786440 | tf_op jit(solution)/shard_map/ppermute | solution.py:390
  21.1 4.6 %collective-permute-start.7 = (bf16[128,1024]{1,0:T(8,128)(2,1)S(1)}, bf16[128,1024]{1,0:T(8,128)(2,1)S(1)}, u32[]{:S(2)}, u32[]{:S(2)}) collective-permute-start(bf16[128,1024]{1,0:T(8,128)(2,1)S(1)} %get-tuple-element.41), channel_id=1, source_target_pairs={{0,2},{2,4},{3,1},{4,6},{5,3},{7,5},{8,10},{10,12},{11,9},{12,14},... | collective-permute-start | bytes 786440 | tf_op jit(solution)/shard_map/ppermute | solution.py:390
  25.6 0.0 collective-permute-done.2.q_b_ref
  25.7 1.4 %global_partial.1.a_ref = bf16[4,144,128]{2,1,0:T(8,128)(2,1)S(1)} custom-call(bf16[64,1024]{1,0:T(8,128)(2,1)S(1)} %add_queries.3.q_a_ref, bf16[64,1024]{1,0:T(8,128)(2,1)S(1)} %collective-permute-done.2.q_b_ref, bf16[896,1024]{1,0:T(8,128)(2,1)S(1)} %get-tuple-element.33.k_ref, bf16[1024,896]{1,0:T(8,128)(2,1)S(1)} %get-tuple-element.34.v_t_ref), custom_call_target="tpu_custom_call" | custom-call | flops 1 | bytes 1 | tf_op jit(solution)/shard_map/global_partial/pallas_call | solution.py:357
  27.0 0.5 collective-permute-start.4
  27.5 8.3 %collective-permute-done.4.b_ref = bf16[4,144,128]{2,1,0:T(8,128)(2,1)S(1)} collective-permute-done((bf16[4,144,128]{2,1,0:T(8,128)(2,1)S(1)}, bf16[4,144,128]{2,1,0:T(8,128)(2,1)S(1)}, u32[]{:S(2)}, u32[]{:S(2)}) %collective-permute-start.4) | collective-permute-done | bytes 147488 | tf_op jit(solution)/shard_map/ppermute | solution.py:386
  35.8 0.1 merge_partial.1.a_ref
  35.9 1.0 %collective-permute-start.5 = (bf16[4,144,128]{2,1,0:T(8,128)(2,1)S(1)}, bf16[4,144,128]{2,1,0:T(8,128)(2,1)S(1)}, u32[]{:S(2)}, u32[]{:S(2)}) collective-permute-start(bf16[4,144,128]{2,1,0:T(8,128)(2,1)S(1)} %merge_partial.1.a_ref), channel_id=1, source_target_pairs={{0,4},{1,5},{2,6},{3,7},{4,0},{5,1},{6,2},{7,3},{8,12},{9,13},{10,... | collective-permute-start | bytes 442376 | tf_op jit(solution)/shard_map/ppermute | solution.py:386
  36.9 0.0 collective-permute-done.8.b_ref
  36.9 2.1 %collective-permute-start.9 = (bf16[128,1024]{1,0:T(8,128)(2,1)S(1)}, bf16[128,1024]{1,0:T(8,128)(2,1)S(1)}, u32[]{:S(2)}, u32[]{:S(2)}) collective-permute-start(bf16[128,1024]{1,0:T(8,128)(2,1)S(1)} %add_keys_values.1.kv_a_ref), channel_id=1, source_target_pairs={{0,4},{1,5},{2,6},{3,7},{4,0},{5,1},{6,2},{7,3},{8,12},{9,13},{10,... | collective-permute-start | bytes 786440 | tf_op jit(solution)/shard_map/ppermute | solution.py:386
  39.0 0.0 collective-permute-done.6.edge_a_ref
  39.0 0.0 collective-permute-done.7.edge_b_ref
  39.0 0.0 copy-start.5
  39.0 0.0 copy-start.7
  39.0 4.3 %near_attention.1 = (f32[8,6,128,128]{3,2,1,0:T(8,128)S(1)}, f32[8,2,6,128]{3,2,1,0:T(8,128)S(1)}) custom-call(bf16[1024,768]{1,0:T(8,128)(2,1)S(1)} %get-tuple-element.35.q_t_ref, bf16[896,1024]{1,0:T(8,128)(2,1)S(1)} %get-tuple-element.33.k_ref, bf16[1024,896]{1,0:T(8,128)(2,1)S(1)} %get-tuple-element.34.v_t_ref, ...), custom_call_target="tpu_custom_call" | custom-call | flops 4000000000 | bytes 1 | tf_op jit(solution)/shard_map/near_attention/pallas_call | solution.py:357
  43.4 12.5 %collective-permute-done.9.kv_b_ref = bf16[128,1024]{1,0:T(8,128)(2,1)S(1)} collective-permute-done((bf16[128,1024]{1,0:T(8,128)(2,1)S(1)}, bf16[128,1024]{1,0:T(8,128)(2,1)S(1)}, u32[]{:S(2)}, u32[]{:S(2)}) %collective-permute-start.9) | collective-permute-done | bytes 262176 | tf_op jit(solution)/shard_map/ppermute | solution.py:386
  55.9 0.0 copy-done.5
  55.9 0.0 copy-done.7
  55.9 3.6 %far_attention.1.win_ref = f32[2,6,128]{2,1,0:T(8,128)S(1)} custom-call(bf16[1024,768]{1,0:T(8,128)(2,1)S(1)} %get-tuple-element.35.q_t_ref, f32[8,6,128,128]{3,2,1,0:T(8,128)S(1)} %get-tuple-element.42.acc_ref, f32[8,2,6,128]{3,2,1,0:T(8,128)S(1)} %get-tuple-element.43.stat_ref, bf16[128,1024]{1,0:T(8,128)(2,1)S(1)} %add_keys_values.1.kv_a_ref, ...), custom_call_target="tpu_custom_call" | custom-call | flops 2000000000 | bytes 1 | tf_op jit(solution)/shard_map/far_attention/pallas_call | solution.py:357
  59.5 0.0 collective-permute-done.5.b_ref
  59.5 0.4 place_global.1
  59.9 0.1 collective-permute-start.10
  60.0 1.2 %collective-permute-done.10 = f32[2,3,128]{2,1,0:T(4,128)S(1)} collective-permute-done((f32[2,3,128]{2,1,0:T(4,128)S(1)}, f32[2,3,128]{2,1,0:T(4,128)S(1)}, u32[]{:S(2)}, u32[]{:S(2)}) %collective-permute-start.10) | collective-permute-done | bytes 3104 | tf_op jit(solution)/shard_map/ppermute | solution.py:386
  61.1 0.6 fusion.4
  (4 shorter events, 0.1 us)
Async XLA Ops:
  0.0 2.4 %copy-start = (bf16[384,2048]{1,0:T(8,128)(2,1)S(1)}, bf16[384,2048]{1,0:T(8,128)(2,1)}, u32[]{:S(2)}) copy-start(bf16[384,2048]{1,0:T(8,128)(2,1)} %q_own_ref) | copy-start | bytes 4718596
  1.8 4.8 %collective-permute-start = (bf16[64,1024]{1,0:T(8,128)(2,1)S(1)}, bf16[64,1024]{1,0:T(8,128)(2,1)S(1)}, u32[]{:S(2)}, u32[]{:S(2)}) collective-permute-start(bf16[64,1024]{1,0:T(8,128)(2,1)S(1)} %get-tuple-element.27), channel_id=1, source_target_pairs={{0,1},{1,0},{2,3},{3,2},{4,5},{5,4},{6,7},{7,6},{8,9},{9,8},{10,11... | collective-permute-start | bytes 393224 | tf_op jit(solution)/shard_map/ppermute | solution.py:386
  2.4 1.4 %copy-start.1 = (bf16[384,2048]{1,0:T(8,128)(2,1)S(1)}, bf16[384,2048]{1,0:T(8,128)(2,1)}, u32[]{:S(2)}) copy-start(bf16[384,2048]{1,0:T(8,128)(2,1)} %k_own_ref) | copy-start | bytes 4718596
  3.8 1.4 %copy-start.3 = (bf16[384,2048]{1,0:T(8,128)(2,1)S(1)}, bf16[384,2048]{1,0:T(8,128)(2,1)}, u32[]{:S(2)}) copy-start(bf16[384,2048]{1,0:T(8,128)(2,1)} %v_own_ref) | copy-start | bytes 4718596
  5.2 0.7 %copy-start.6 = (s32[64]{0:T(128)S(1)}, s32[64]{0:T(128)}, u32[]{:S(2)}) copy-start(s32[64]{0:T(128)} %param.8) | copy-start | bytes 772
  5.8 10.6 %copy-start.2 = (bf16[384,2048]{1,0:T(8,128)(2,1)S(1)}, bf16[384,2048]{1,0:T(8,128)(2,1)}, u32[]{:S(2)}) copy-start(bf16[384,2048]{1,0:T(8,128)(2,1)} %k_own_ref) | copy-start | bytes 4718596
  5.8 10.6 %copy-start.4 = (bf16[384,2048]{1,0:T(8,128)(2,1)S(1)}, bf16[384,2048]{1,0:T(8,128)(2,1)}, u32[]{:S(2)}) copy-start(bf16[384,2048]{1,0:T(8,128)(2,1)} %v_own_ref) | copy-start | bytes 4718596
  6.7 9.7 %collective-permute-start.3 = (bf16[1408,1024]{1,0:T(8,128)(2,1)S(1)}, bf16[1408,1024]{1,0:T(8,128)(2,1)S(1)}, u32[]{:S(2)}, u32[]{:S(2)}) collective-permute-start(bf16[1408,1024]{1,0:T(8,128)(2,1)S(1)} %get-tuple-element.32), channel_id=1, source_target_pairs={{0,1},{1,0},{2,3},{3,2},{4,5},{5,4},{6,7},{7,6},{8,9},{9,8},{10,11... | collective-permute-start | bytes 8650760 | tf_op jit(solution)/shard_map/ppermute | solution.py:386
  6.8 6.8 %collective-permute-start.1 = (bf16[64,1024]{1,0:T(8,128)(2,1)S(1)}, bf16[64,1024]{1,0:T(8,128)(2,1)S(1)}, u32[]{:S(2)}, u32[]{:S(2)}) collective-permute-start(bf16[64,1024]{1,0:T(8,128)(2,1)S(1)} %add_queries.2.a_ref), channel_id=1, source_target_pairs={{0,2},{1,3},{2,0},{3,1},{4,6},{5,7},{6,4},{7,5},{8,10},{9,11},{10,... | collective-permute-start | bytes 393224 | tf_op jit(solution)/shard_map/ppermute | solution.py:386
  13.6 12.0 %collective-permute-start.2 = (bf16[64,1024]{1,0:T(8,128)(2,1)S(1)}, bf16[64,1024]{1,0:T(8,128)(2,1)S(1)}, u32[]{:S(2)}, u32[]{:S(2)}) collective-permute-start(bf16[64,1024]{1,0:T(8,128)(2,1)S(1)} %add_queries.3.q_a_ref), channel_id=1, source_target_pairs={{0,4},{1,5},{2,6},{3,7},{4,0},{5,1},{6,2},{7,3},{8,12},{9,13},{10,... | collective-permute-start | bytes 393224 | tf_op jit(solution)/shard_map/ppermute | solution.py:386
  18.1 18.7 %collective-permute-start.8 = (bf16[128,1024]{1,0:T(8,128)(2,1)S(1)}, bf16[128,1024]{1,0:T(8,128)(2,1)S(1)}, u32[]{:S(2)}, u32[]{:S(2)}) collective-permute-start(bf16[128,1024]{1,0:T(8,128)(2,1)S(1)} %get-tuple-element.44.a_ref), channel_id=1, source_target_pairs={{0,2},{1,3},{2,0},{3,1},{4,6},{5,7},{6,4},{7,5},{8,10},{9,11},{10,... | collective-permute-start | bytes 786440 | tf_op jit(solution)/shard_map/ppermute | solution.py:386
  19.8 19.2 %collective-permute-start.6 = (bf16[128,1024]{1,0:T(8,128)(2,1)S(1)}, bf16[128,1024]{1,0:T(8,128)(2,1)S(1)}, u32[]{:S(2)}, u32[]{:S(2)}) collective-permute-start(bf16[128,1024]{1,0:T(8,128)(2,1)S(1)} %get-tuple-element.38), channel_id=1, source_target_pairs={{1,3},{2,0},{3,5},{4,2},{5,7},{6,4},{9,11},{10,8},{11,13},{12,10},... | collective-permute-start | bytes 786440 | tf_op jit(solution)/shard_map/ppermute | solution.py:390
  21.1 17.9 %collective-permute-start.7 = (bf16[128,1024]{1,0:T(8,128)(2,1)S(1)}, bf16[128,1024]{1,0:T(8,128)(2,1)S(1)}, u32[]{:S(2)}, u32[]{:S(2)}) collective-permute-start(bf16[128,1024]{1,0:T(8,128)(2,1)S(1)} %get-tuple-element.41), channel_id=1, source_target_pairs={{0,2},{2,4},{3,1},{4,6},{5,3},{7,5},{8,10},{10,12},{11,9},{12,14},... | collective-permute-start | bytes 786440 | tf_op jit(solution)/shard_map/ppermute | solution.py:390
  27.0 8.8 %collective-permute-start.4 = (bf16[4,144,128]{2,1,0:T(8,128)(2,1)S(1)}, bf16[4,144,128]{2,1,0:T(8,128)(2,1)S(1)}, u32[]{:S(2)}, u32[]{:S(2)}) collective-permute-start(bf16[4,144,128]{2,1,0:T(8,128)(2,1)S(1)} %global_partial.1.a_ref), channel_id=1, source_target_pairs={{0,2},{1,3},{2,0},{3,1},{4,6},{5,7},{6,4},{7,5},{8,10},{9,11},{10,... | collective-permute-start | bytes 442376 | tf_op jit(solution)/shard_map/ppermute | solution.py:386
  35.9 23.6 %collective-permute-start.5 = (bf16[4,144,128]{2,1,0:T(8,128)(2,1)S(1)}, bf16[4,144,128]{2,1,0:T(8,128)(2,1)S(1)}, u32[]{:S(2)}, u32[]{:S(2)}) collective-permute-start(bf16[4,144,128]{2,1,0:T(8,128)(2,1)S(1)} %merge_partial.1.a_ref), channel_id=1, source_target_pairs={{0,4},{1,5},{2,6},{3,7},{4,0},{5,1},{6,2},{7,3},{8,12},{9,13},{10,... | collective-permute-start | bytes 442376 | tf_op jit(solution)/shard_map/ppermute | solution.py:386
  36.9 19.0 %collective-permute-start.9 = (bf16[128,1024]{1,0:T(8,128)(2,1)S(1)}, bf16[128,1024]{1,0:T(8,128)(2,1)S(1)}, u32[]{:S(2)}, u32[]{:S(2)}) collective-permute-start(bf16[128,1024]{1,0:T(8,128)(2,1)S(1)} %add_keys_values.1.kv_a_ref), channel_id=1, source_target_pairs={{0,4},{1,5},{2,6},{3,7},{4,0},{5,1},{6,2},{7,3},{8,12},{9,13},{10,... | collective-permute-start | bytes 786440 | tf_op jit(solution)/shard_map/ppermute | solution.py:386
  39.0 16.9 %copy-start.5 = (f32[2048]{0:T(1024)S(1)}, f32[2048]{0:T(1024)}, u32[]{:S(2)}) copy-start(f32[2048]{0:T(1024)} %param.9) | copy-start | bytes 24580
  39.0 16.9 %copy-start.7 = (s32[64]{0:T(128)S(1)}, s32[64]{0:T(128)}, u32[]{:S(2)}) copy-start(s32[64]{0:T(128)} %param.8) | copy-start | bytes 772
  59.9 1.2 %collective-permute-start.10 = (f32[2,3,128]{2,1,0:T(4,128)S(1)}, f32[2,3,128]{2,1,0:T(4,128)S(1)}, u32[]{:S(2)}, u32[]{:S(2)}) collective-permute-start(f32[2,3,128]{2,1,0:T(4,128)S(1)} %get-tuple-element.46), channel_id=1, source_target_pairs={{0,1},{1,0},{2,3},{3,2},{4,5},{5,4},{6,7},{7,6},{8,9},{9,8},{10,11... | collective-permute-start | bytes 9224 | tf_op jit(solution)/shard_map/ppermute | solution.py:386
where the time goes:
time: 61.9 us; the launch traced here: 61.7 us
  waiting for transfers between devices  25.7 us (42%)
  starting transfers between devices  17.6 us (28%)
  Pallas kernels  14.2 us (23%)
  local copies, waits for them, and re-layouts  3.49 us (6%)
    ppermute x9, waiting for transfers between devices, swap(): return lax.ppermute(x, 'seq', [(i, i ^ mask) for i in range(seq_count)])  25.7 us
    pallas_call x12, Pallas kernels, call(): pl.pallas_call(kernel, in_specs=[pl.BlockSpec(memory_space=source)] * len...  14.2 us
    ppermute x9, starting transfers between devices, swap(): return lax.ppermute(x, 'seq', [(i, i ^ mask) for i in range(seq_count)])  11.8 us
    ppermute x2, starting transfers between devices, shift(): lax.ppermute(x, 'seq', [(i, to) for i, to in moves if 0 <= to < seq_count])  5.84 us
    unnamed x16, local copies, waits for them, and re-layouts  3.49 us
  transfers between devices with their start and end apart: 11, of which 4 were waited for; matrix products, arithmetic and copies ran while one was open for 0% of the time, Pallas kernels for 19%

commit v1 on v0

--- a/solution.py
+++ b/solution.py
@@ -100,7 +100,7 @@
         pick(q_ref.at[slot], hit, out_ref, 0, slice(None))
 
 
-def select_kv_kernel(half, pos_ref, k_ref, v_ref, q_ref, own_ref, edge_ref, sib_ref):
+def select_kv_kernel(half, pos_ref, k_ref, v_ref, q_ref, own_ref, edge_ref, sib_ref, bulk_ref):
     rows = k_ref.shape[0]
     glob = pos_ref.shape[1]
     hit = own_positions(pos_ref, rows)
@@ -108,25 +108,31 @@
     block = pl.ds(pl.multiple_of(core * (rows - BLK), BLK), BLK)
     mine = pl.ds(pl.multiple_of(core * half, half), half)
     theirs = pl.ds(pl.multiple_of((1 - core) * half, half), half)
-    start = 2 * glob + 2 * BLK
     for i, x_ref in enumerate((k_ref, v_ref)):
         pick(x_ref, hit, sib_ref, i * glob, theirs)
         sib_ref[2 * glob + i * BLK : 2 * glob + (i + 1) * BLK, :] = x_ref[block, theirs]
-        sib_ref[start + i * rows : start + (i + 1) * rows, :] = x_ref[:, theirs]
+        bulk_ref[i * rows : (i + 1) * rows, :] = x_ref[:, theirs]
         pick(x_ref, hit, own_ref, i * glob, mine)
         edge_ref[i * BLK : (i + 1) * BLK, :] = x_ref[block, mine]
-    sib_ref[start + 2 * rows :, :] = q_ref[:, theirs]
+    bulk_ref[2 * rows :, :] = q_ref[:, theirs]
 
 
 def split_kernel(a_ref, b_ref, sum_ref, rest_ref):
     count = sum_ref.shape[0]
     sum_ref[...] = a_ref[...] + b_ref[:count, :]
-    rest_ref[...] = b_ref[count : count + rest_ref.shape[0], :]
+    rest_ref[...] = b_ref[count:, :]
 
 
 def add_kernel(a_ref, b_ref, out_ref):
-    count = out_ref.shape[0]
-    out_ref[...] = a_ref[:count, :] + b_ref[:count, :]
+    out_ref[...] = a_ref[...] + b_ref[...]
+
+
+def on_line():
+    return lax.axis_size("seq") // CORES == 4
+
+
+def is_inner(chip):
+    return (chip == 1) | (chip == 2)
 
 
 def prepare_kernel(q_own_ref, k_own_ref, v_own_ref, sib_ref, k_ref, v_t_ref, q_t_ref, v_all):
@@ -136,20 +142,19 @@
     cols = pl.ds(pl.multiple_of(core * half, half), half)
     own = pl.multiple_of(core * rows, BLK)
     sib = pl.multiple_of((1 - core) * rows, BLK)
-    start = sib_ref.shape[0] - 3 * rows
     zero = jnp.zeros((BLK, half), jnp.bfloat16)
     for i, (ref, own_ref) in enumerate(((k_ref, k_own_ref), (v_all, v_own_ref))):
         ref[:BLK, :] = zero
         ref[BLK + CORES * rows :, :] = zero
         ref[pl.ds(pl.multiple_of(own + BLK, BLK), rows), :] = own_ref[:, cols]
-        ref[pl.ds(pl.multiple_of(sib + BLK, BLK), rows), :] = sib_ref[start + i * rows : start + (i + 1) * rows, :]
+        ref[pl.ds(pl.multiple_of(sib + BLK, BLK), rows), :] = sib_ref[i * rows : (i + 1) * rows, :]
 
     def turn(head, carry):
         lanes = pl.ds(pl.multiple_of(head * LANES, LANES), LANES)
         v_t_ref[lanes, :] = jnp.transpose(v_all[:, lanes])
         source = pl.ds(pl.multiple_of(core * half + head * LANES, LANES), LANES)
         q_t_ref[lanes, pl.ds(pl.multiple_of(own, LANES), rows)] = jnp.transpose(q_own_ref[:, source])
-        q_t_ref[lanes, pl.ds(pl.multiple_of(sib, LANES), rows)] = jnp.transpose(sib_ref[start + 2 * rows :, lanes])
+        q_t_ref[lanes, pl.ds(pl.multiple_of(sib, LANES), rows)] = jnp.transpose(sib_ref[2 * rows :, lanes])
         return carry
 
     lax.fori_loop(0, half // LANES, turn, 0)
@@ -196,10 +201,22 @@
         put_message(out_ref, pair, *merged(a, b, scale2))
 
 
-def final_kernel(scale2, a_ref, b_ref, w_ref, pos_ref, win_ref, own_ref, sib_ref):
+def inward_kernel(scale2, a_ref, b_ref, out_ref):
+    _, chip = device_place()
+
+    @pl.when(is_inner(chip))
+    def _():
+        merge_kernel(scale2, a_ref, b_ref, out_ref)
+
+    @pl.when(jnp.logical_not(is_inner(chip)))
+    def _():
+        out_ref[...] = a_ref[...]
+
+
+def sums_kernel(scale2, a_ref, b_ref, w_ref, out_ref):
     pairs = a_ref.shape[0]
     head_size = a_ref.shape[1] - STAT_ROWS
-    glob = pos_ref.shape[1]
+    glob = LANES // 2
     core, chip = device_place()
     upper = lax.broadcasted_iota(jnp.int32, (LANES, head_size), 0) < glob
     lin = jnp.zeros((1, LANES), jnp.float32)
@@ -207,15 +224,26 @@
     for pair in range(pairs):
         a = get_message(a_ref, pair, head_size)
         b = get_message(b_ref, pair, head_size)
+        if on_line():
+            b = tuple(jnp.where(is_inner(chip), y, x) for x, y in zip(a, b))
         out, _, _ = merged(a, b, scale2)
         w_a = w_ref[pl.ds(core * 2 * pairs + 2 * pair, 1), :]
         w_b = w_ref[pl.ds(core * 2 * pairs + 2 * pair + 1, 1), :]
         w = jnp.transpose(jnp.where(upper, w_a, w_b))
         lin = lin + jnp.sum(out * w, axis=0, keepdims=True)
         sq = sq + jnp.sum(out * out, axis=0, keepdims=True)
-    lin = lin + pltpu.roll(lin, glob, 1)
-    sq = sq + pltpu.roll(sq, glob, 1)
-    parts = [p.astype(jnp.float32) for p in (*pieces(lin), *pieces(sq))] + [jnp.ones((1, LANES), jnp.float32)]
+    out_ref[...] = jnp.zeros_like(out_ref)
+    out_ref[0:1, :] = lin + pltpu.roll(lin, glob, 1)
+    out_ref[1:2, :] = sq + pltpu.roll(sq, glob, 1)
+
+
+def place_kernel(own_sums_ref, far_sums_ref, pos_ref, win_ref, own_ref, sib_ref):
+    glob = pos_ref.shape[1]
+    core, chip = device_place()
+    sums = own_sums_ref[...]
+    if on_line():
+        sums = jnp.where(is_inner(chip), sums, far_sums_ref[...])
+    parts = [p.astype(jnp.float32) for p in (*pieces(sums[0:1]), *pieces(sums[1:2]))] + [jnp.ones((1, LANES), jnp.float32)]
     row = lax.broadcasted_iota(jnp.int32, (16, LANES), 0)
     table = jnp.zeros((16, LANES), jnp.float32)
     for i, part in enumerate(parts):
@@ -224,7 +252,7 @@
     pos = column_of(pos_ref[...])
     n_pairs = win_ref.shape[1]
     each = n_pairs // CORES
-    for out_ref, which in ((own_ref, core), (sib_ref, 1 - core)):
+    for out_ref, which in ((sib_ref, 1 - core), (own_ref, core)):
         for j in range(each):
             pair = which * each + j
             token = (chip * n_pairs + pair) * LANES + lax.broadcasted_iota(jnp.int32, (glob, LANES), 1)
@@ -317,7 +345,11 @@
 
     def one_head(head, carry):
         cols = pl.ds(pl.multiple_of(head * LANES, LANES), LANES)
-        kg = kv_a_ref[:glob, cols] + kv_b_ref[:glob, cols]
+        kv_a = kv_a_ref[:, cols]
+        if on_line():
+            kv_a = jnp.where(is_inner(chip), kv_a, jnp.zeros_like(kv_a))
+        kv = kv_a + kv_b_ref[:, cols]
+        kg = kv[:glob]
         for j in range(n_pairs):
             s_buf[j] = dot_n(kg, q_t_ref[cols, j * LANES : (j + 1) * LANES])
         near_peaks = stat_ref[head, 0]
@@ -333,7 +365,7 @@
             total = near_totals[j : j + 1] * near_weight + jnp.sum(e_far, axis=0, keepdims=True)
             near_weights.append(near_weight)
             inverses.append(1.0 / total)
-        vg_t = jnp.transpose(kv_a_ref[glob:, cols] + kv_b_ref[glob:, cols])
+        vg_t = jnp.transpose(kv[glob:])
         w = w_cols[head]
         lins, sqs = [], []
         for j in range(n_pairs):
@@ -389,6 +421,13 @@
         moves = [(i, i + (odd if i % CORES else even) * CORES) for i in range(seq_count)]
         return lax.ppermute(x, "seq", [(i, to) for i, to in moves if 0 <= to < seq_count])
 
+    def move(x, pairs):
+        return lax.ppermute(x, "seq", [(a * CORES + c, b * CORES + c) for a, b in pairs for c in range(CORES)])
+
+    inward = ((0, 1), (3, 2))
+    across = ((1, 2), (2, 1))
+    outward = ((1, 0), (2, 3))
+
     def after(arrays, *others):
         return lax.optimization_barrier((*arrays, *others))[: len(arrays)]
 
@@ -404,36 +443,42 @@
         [((1, glob), jnp.int32), ((CORES, rows, half), bf16), pltpu.SemaphoreType.DMA((3,))],
         from_hbm=True,
     )
-    keys, values, queries = after((keys, values, queries), q_sib)
-    kv_own, edge_own, kv_sib = call(
+    later_positions = after((row_positions,), q_sib)[0]
+    kv_own, edge_own, kv_sib, bulk_sib = call(
         functools.partial(select_kv_kernel, half),
         "select_keys_values",
-        [pair_of, edge, ((2 * glob + 2 * BLK + 3 * rows, half), bf16)],
-        [row_positions, keys, values, queries],
+        [pair_of, edge, ((2 * glob + 2 * BLK, half), bf16), ((3 * rows, half), bf16)],
+        [later_positions, keys, values, queries],
     )
     q_near = call(add_kernel, "add_queries", small, [q_own, swap(q_sib, 1)])
-    kv_sib = after((kv_sib,), q_near)[0]
-    sib_recv = swap(kv_sib, 1)
+    kv_near, edge_recv = call(split_kernel, "join_keys_values", [pair_of, edge], [kv_own, swap(kv_sib, 1)])
+    bulk_sib = after((bulk_sib,), q_near, kv_near)[0]
+    bulk_recv = swap(bulk_sib, 1)
+    kv_near = after((kv_near,), q_near)[0]
     for r in range(1, rounds):
         q_near = call(add_kernel, "add_queries", small, [q_near, swap(q_near, 1 << r)])
     q_far = swap(q_near, 1 << rounds)
+
+    edge_own, edge_recv = after((edge_own, edge_recv), q_near)
+    edge_a = shift(edge_own, -1, 1)
+    edge_b = shift(edge_recv, 1, -1)
+    if chips == 4:
+        kv_near = call(add_kernel, "add_keys_values", pair_of, [kv_near, move(kv_near, inward)])
+        kv_near = call(add_kernel, "add_keys_values", pair_of, [kv_near, move(kv_near, across)])
+        kv_far = move(kv_near, outward)
+    else:
+        for r in range(1, rounds):
+            kv_near = call(add_kernel, "add_keys_values", pair_of, [kv_near, swap(kv_near, 1 << r)])
+        kv_far = swap(kv_near, 1 << rounds)
 
     k_all, v_t, q_t = call(
         prepare_kernel,
         "prepare",
         [((tokens + 2 * BLK, half), bf16), ((half, tokens + 2 * BLK), bf16), ((half, tokens), bf16)],
-        [queries, keys, values, sib_recv],
+        [queries, keys, values, bulk_recv],
         [((tokens + 2 * BLK, half), bf16)],
         micros=1.6,
     )
-    kv_own, edge_own, sib_recv = after((kv_own, edge_own, sib_recv), k_all, q_near)
-    edge_a = shift(edge_own, -1, 1)
-    kv_near, edge_recv = call(split_kernel, "join_keys_values", [pair_of, edge], [kv_own, sib_recv])
-    edge_b = shift(edge_recv, 1, -1)
-    for r in range(1, rounds):
-        kv_near = call(add_kernel, "add_keys_values", pair_of, [kv_near, swap(kv_near, 1 << r)])
-    kv_far = swap(kv_near, 1 << rounds)
-
     part = ((half_heads // 2, head_size + STAT_ROWS, LANES), bf16)
     message = call(
         functools.partial(global_kernel, scale2),
@@ -442,13 +487,23 @@
         [q_near, q_far, k_all, v_t],
         [((half_heads // 2, tokens, LANES), f32), ((half_heads // 2, tokens + 2 * BLK, LANES), bf16)],
     )
-    for r in range(1, rounds):
+    weights = score_weight.reshape(HEADS, head_size)
+    if chips == 4:
         message = call(
-            functools.partial(merge_kernel, scale2), "merge_partial", part, [message, swap(message, 1 << r)]
+            functools.partial(inward_kernel, scale2), "merge_partial", part, [message, move(message, inward)]
         )
-    message_far = swap(message, 1 << rounds)
-
-    weights = score_weight.reshape(HEADS, head_size)
+        message_far = move(message, across)
+    else:
+        for r in range(1, rounds):
+            message = call(
+                functools.partial(merge_kernel, scale2), "merge_partial", part, [message, swap(message, 1 << r)]
+            )
+        message_far = swap(message, 1 << rounds)
+    sums = call(
+        functools.partial(sums_kernel, scale2), "global_sums", ((8, LANES), f32), [message, message_far, weights]
+    )
+    sums_far = move(sums, outward) if chips == 4 else sums
+
     near_acc, near_stat = call(
         functools.partial(near_kernel, scale2),
         "near_attention",
@@ -472,10 +527,7 @@
     )
     share = ((2, n_pairs // CORES, LANES), f32)
     mine, theirs = call(
-        functools.partial(final_kernel, scale2),
-        "place_global",
-        [share, share],
-        [message, message_far, weights, row_positions, window],
+        place_kernel, "place_global", [share, share], [sums, sums_far, row_positions, window]
     )
     theirs = swap(theirs, 1)
     lin = mine[0] + theirs[0]

time: 61.9 us -> 58.4 us (0.943)
  waiting for transfers between devices: 25.7 us -> 16.5 us
  starting transfers between devices: 17.6 us -> 22.9 us
    ppermute x9 -> x6, waiting for transfers between devices: 25.7 us -> 11.6 us  [swap(): return lax.ppermute(x, 'seq', [(i, i ^ mask) for i in range(seq_count)])]
    ppermute x0 -> x6, starting transfers between devices: none -> 12.3 us  [move(): lax.ppermute(x, 'seq', [(a * CORES + c, b * CORES + c) for a, b in pairs...]
    ppermute x9 -> x6, starting transfers between devices: 11.8 us -> 4.74 us  [swap(): return lax.ppermute(x, 'seq', [(i, i ^ mask) for i in range(seq_count)])]
    ppermute x0 -> x6, waiting for transfers between devices: none -> 4.93 us  [move(): lax.ppermute(x, 'seq', [(a * CORES + c, b * CORES + c) for a, b in pairs...]
    pallas_call x12 -> x14, Pallas kernels: 14.2 us -> 14.2 us  [call(): pl.pallas_call(kernel, in_specs=[pl.BlockSpec(memory_space=source)] * len...]
  transfers between devices with their start and end apart: 11 -> 14, of which waited for: 4 -> 6; matrix products, arithmetic and copies ran while one was open for 0% -> 0% of each run, Pallas kernels for 19% -> 19%
where the time goes in v1:
time: 58.4 us; the launch traced here: 58 us
  starting transfers between devices  22.9 us (39%)
  waiting for transfers between devices  16.5 us (28%)
  Pallas kernels  14.2 us (24%)
  local copies, waits for them, and re-layouts  3.54 us (6%)
  other arithmetic  0.59 us (1%)
    pallas_call x14, Pallas kernels, call(): pl.pallas_call(kernel, in_specs=[pl.BlockSpec(memory_space=source)] * len...  14.2 us
    ppermute x6, starting transfers between devices, move(): lax.ppermute(x, 'seq', [(a * CORES + c, b * CORES + c) for a, b in pairs...  12.3 us
    ppermute x6, waiting for transfers between devices, swap(): return lax.ppermute(x, 'seq', [(i, i ^ mask) for i in range(seq_count)])  11.6 us
    ppermute x2, starting transfers between devices, shift(): lax.ppermute(x, 'seq', [(i, to) for i, to in moves if 0 <= to < seq_count])  5.84 us
    ppermute x6, waiting for transfers between devices, move(): lax.ppermute(x, 'seq', [(a * CORES + c, b * CORES + c) for a, b in pairs...  4.93 us
    ppermute x6, starting transfers between devices, swap(): return lax.ppermute(x, 'seq', [(i, i ^ mask) for i in range(seq_count)])  4.74 us
    unnamed x16, local copies, waits for them, and re-layouts  3.54 us
  transfers between devices with their start and end apart: 14, of which 6 were waited for; matrix products, arithmetic and copies ran while one was open for 0% of the time, Pallas kernels for 19%

profile of v1, /device:TPU:0, one launch (start us, length us, event | category | flops | bytes accessed | tf_op | source)
XLA Modules:
  0.0 58.0 jit_solution(6858140057039637146)
XLA Ops:
  0.0 1.8 %select_queries.1 = (bf16[64,1024]{1,0:T(8,128)(2,1)S(1)}, bf16[64,1024]{1,0:T(8,128)(2,1)S(1)}) custom-call(s32[1,64]{1,0:T(1,128)} %bitcast.6, bf16[384,2048]{1,0:T(8,128)(2,1)} %q_own_ref.1), custom_call_target="tpu_custom_call" | custom-call | flops 1 | bytes 1 | tf_op jit(solution)/shard_map/select_queries/pallas_call | solution.py:389
  1.8 0.0 copy-done
  1.9 1.4 %copy-done.1 = bf16[384,2048]{1,0:T(8,128)(2,1)S(1)} copy-done((bf16[384,2048]{1,0:T(8,128)(2,1)S(1)}, bf16[384,2048]{1,0:T(8,128)(2,1)}, u32[]{:S(2)}) %copy-start.1) | copy-done | bytes 1572888
  3.3 1.4 %copy-done.3 = bf16[384,2048]{1,0:T(8,128)(2,1)S(1)} copy-done((bf16[384,2048]{1,0:T(8,128)(2,1)S(1)}, bf16[384,2048]{1,0:T(8,128)(2,1)}, u32[]{:S(2)}) %copy-start.3) | copy-done | bytes 1572888
  4.7 0.7 %copy-done.6 = s32[64]{0:T(128)S(1)} copy-done((s32[64]{0:T(128)S(1)}, s32[64]{0:T(128)}, u32[]{:S(2)}) %copy-start.6) | copy-done | bytes 280
  5.4 0.8 %select_keys_values.1 = (bf16[128,1024]{1,0:T(8,128)(2,1)S(1)}, bf16[128,1024]{1,0:T(8,128)(2,1)S(1)}, bf16[256,1024]{1,0:T(8,128)(2,1)S(1)}, bf16[1152,1024]{1,0:T(8,128)(2,1)S(1)}) custom-call(s32[1,64]{1,0:T(1,128)S(1)} %bitcast.7, bf16[384,2048]{1,0:T(8,128)(2,1)S(1)} %copy-done.1, bf16[384,2048]{1,0:T(8,128)(2,1)S(1)} %copy-done.3, ...), custom_call_target="tpu_custom_call" | custom-call | flops 1 | bytes 1 | tf_op jit(solution)/shard_map/select_keys_values/pallas_call | solution.py:389
  6.2 0.0 copy-start.2
  6.2 0.5 collective-permute-start.3
  6.7 0.1 collective-permute-start
  6.8 1.6 %collective-permute-done.b_ref = bf16[64,1024]{1,0:T(8,128)(2,1)S(1)} collective-permute-done((bf16[64,1024]{1,0:T(8,128)(2,1)S(1)}, bf16[64,1024]{1,0:T(8,128)(2,1)S(1)}, u32[]{:S(2)}, u32[]{:S(2)}) %collective-permute-start) | collective-permute-done | bytes 131104 | tf_op jit(solution)/shard_map/ppermute | solution.py:418
  8.5 0.0 collective-permute-done.3.b_ref
  8.5 0.4 collective-permute-start.4
  9.0 4.6 %collective-permute-start.10 = (bf16[128,1024]{1,0:T(8,128)(2,1)S(1)}, bf16[128,1024]{1,0:T(8,128)(2,1)S(1)}, u32[]{:S(2)}, u32[]{:S(2)}) collective-permute-start(bf16[128,1024]{1,0:T(8,128)(2,1)S(1)} %get-tuple-element.42.a_ref), channel_id=1, source_target_pairs={{0,2},{1,3},{6,4},{7,5},{8,10},{9,11},{14,12},{15,13},{16,18},{17,... | collective-permute-start | bytes 786440 | tf_op jit(solution)/shard_map/ppermute | solution.py:425
  13.6 0.1 collective-permute-start.1
  13.7 8.8 %collective-permute-done.1.b_ref = bf16[64,1024]{1,0:T(8,128)(2,1)S(1)} collective-permute-done((bf16[64,1024]{1,0:T(8,128)(2,1)S(1)}, bf16[64,1024]{1,0:T(8,128)(2,1)S(1)}, u32[]{:S(2)}, u32[]{:S(2)}) %collective-permute-start.1) | collective-permute-done | bytes 131104 | tf_op jit(solution)/shard_map/ppermute | solution.py:418
  22.5 3.6 %collective-permute-start.2 = (bf16[64,1024]{1,0:T(8,128)(2,1)S(1)}, bf16[64,1024]{1,0:T(8,128)(2,1)S(1)}, u32[]{:S(2)}, u32[]{:S(2)}) collective-permute-start(bf16[64,1024]{1,0:T(8,128)(2,1)S(1)} %add_queries.3.q_a_ref), channel_id=1, source_target_pairs={{0,4},{1,5},{2,6},{3,7},{4,0},{5,1},{6,2},{7,3},{8,12},{9,13},{10,... | collective-permute-start | bytes 393224 | tf_op jit(solution)/shard_map/ppermute | solution.py:418
  26.1 1.3 %collective-permute-start.8 = (bf16[128,1024]{1,0:T(8,128)(2,1)S(1)}, bf16[128,1024]{1,0:T(8,128)(2,1)S(1)}, u32[]{:S(2)}, u32[]{:S(2)}) collective-permute-start(bf16[128,1024]{1,0:T(8,128)(2,1)S(1)} %get-tuple-element.38), channel_id=1, source_target_pairs={{1,3},{2,0},{3,5},{4,2},{5,7},{6,4},{9,11},{10,8},{11,13},{12,10},... | collective-permute-start | bytes 786440 | tf_op jit(solution)/shard_map/ppermute | solution.py:422
  27.3 4.6 %collective-permute-start.9 = (bf16[128,1024]{1,0:T(8,128)(2,1)S(1)}, bf16[128,1024]{1,0:T(8,128)(2,1)S(1)}, u32[]{:S(2)}, u32[]{:S(2)}) collective-permute-start(bf16[128,1024]{1,0:T(8,128)(2,1)S(1)} %get-tuple-element.39), channel_id=1, source_target_pairs={{0,2},{2,4},{3,1},{4,6},{5,3},{7,5},{8,10},{10,12},{11,9},{12,14},... | collective-permute-start | bytes 786440 | tf_op jit(solution)/shard_map/ppermute | solution.py:422
  31.9 0.0 collective-permute-done.10.b_ref
  32.0 0.7 %collective-permute-start.11 = (bf16[128,1024]{1,0:T(8,128)(2,1)S(1)}, bf16[128,1024]{1,0:T(8,128)(2,1)S(1)}, u32[]{:S(2)}, u32[]{:S(2)}) collective-permute-start(bf16[128,1024]{1,0:T(8,128)(2,1)S(1)} %add_keys_values.2.a_ref), channel_id=1, source_target_pairs={{2,4},{3,5},{4,2},{5,3},{10,12},{11,13},{12,10},{13,11},{18,20},{1... | collective-permute-start | bytes 786440 | tf_op jit(solution)/shard_map/ppermute | solution.py:425
  32.6 0.0 collective-permute-done.4.sib_ref
  32.7 0.0 copy-done.4
  32.7 0.0 copy-done.2
  32.7 1.6 %prepare.1 = (bf16[896,1024]{1,0:T(8,128)(2,1)S(1)}, bf16[1024,896]{1,0:T(8,128)(2,1)S(1)}, bf16[1024,768]{1,0:T(8,128)(2,1)S(1)}) custom-call(bf16[384,2048]{1,0:T(8,128)(2,1)S(1)} %copy-done, bf16[384,2048]{1,0:T(8,128)(2,1)S(1)} %copy-done.2, bf16[384,2048]{1,0:T(8,128)(2,1)S(1)} %copy-done.4, bf16[1152,1024]{1,0:T(8,128)(2,1)S(1)} %collective-permute-done.4.sib_ref), custom_call_target="tpu_custom_call" | custom-call | flops 1600000000 | bytes 1 | tf_op jit(solution)/shard_map/prepare/pallas_call | solution.py:389
  34.3 0.0 collective-permute-done.2.q_b_ref
  34.3 1.4 %global_partial.1.a_ref = bf16[4,144,128]{2,1,0:T(8,128)(2,1)S(1)} custom-call(bf16[64,1024]{1,0:T(8,128)(2,1)S(1)} %add_queries.3.q_a_ref, bf16[64,1024]{1,0:T(8,128)(2,1)S(1)} %collective-permute-done.2.q_b_ref, bf16[896,1024]{1,0:T(8,128)(2,1)S(1)} %get-tuple-element.33.k_ref, bf16[1024,896]{1,0:T(8,128)(2,1)S(1)} %get-tuple-element.34.v_t_ref), custom_call_target="tpu_custom_call" | custom-call | flops 1 | bytes 1 | tf_op jit(solution)/shard_map/global_partial/pallas_call | solution.py:389
  35.7 3.7 %collective-permute-start.5 = (bf16[4,144,128]{2,1,0:T(8,128)(2,1)S(1)}, bf16[4,144,128]{2,1,0:T(8,128)(2,1)S(1)}, u32[]{:S(2)}, u32[]{:S(2)}) collective-permute-start(bf16[4,144,128]{2,1,0:T(8,128)(2,1)S(1)} %global_partial.1.a_ref), channel_id=1, source_target_pairs={{0,2},{1,3},{6,4},{7,5},{8,10},{9,11},{14,12},{15,13},{16,18},{17,... | collective-permute-start | bytes 442376 | tf_op jit(solution)/shard_map/ppermute | solution.py:425
  39.4 0.0 collective-permute-done.11.b_ref
  39.5 1.3 %collective-permute-start.12 = (bf16[128,1024]{1,0:T(8,128)(2,1)S(1)}, bf16[128,1024]{1,0:T(8,128)(2,1)S(1)}, u32[]{:S(2)}, u32[]{:S(2)}) collective-permute-start(bf16[128,1024]{1,0:T(8,128)(2,1)S(1)} %add_keys_values.3.kv_a_ref), channel_id=1, source_target_pairs={{2,0},{3,1},{4,6},{5,7},{10,8},{11,9},{12,14},{13,15},{18,16},{19,... | collective-permute-start | bytes 786440 | tf_op jit(solution)/shard_map/ppermute | solution.py:425
  40.8 1.3 %collective-permute-done.5.b_ref = bf16[4,144,128]{2,1,0:T(8,128)(2,1)S(1)} collective-permute-done((bf16[4,144,128]{2,1,0:T(8,128)(2,1)S(1)}, bf16[4,144,128]{2,1,0:T(8,128)(2,1)S(1)}, u32[]{:S(2)}, u32[]{:S(2)}) %collective-permute-start.5) | collective-permute-done | bytes 147488 | tf_op jit(solution)/shard_map/ppermute | solution.py:425
  42.1 0.7 %collective-permute-start.6 = (bf16[4,144,128]{2,1,0:T(8,128)(2,1)S(1)}, bf16[4,144,128]{2,1,0:T(8,128)(2,1)S(1)}, u32[]{:S(2)}, u32[]{:S(2)}) collective-permute-start(bf16[4,144,128]{2,1,0:T(8,128)(2,1)S(1)} %merge_partial.1.a_ref), channel_id=1, source_target_pairs={{2,4},{3,5},{4,2},{5,3},{10,12},{11,13},{12,10},{13,11},{18,20},{1... | collective-permute-start | bytes 442376 | tf_op jit(solution)/shard_map/ppermute | solution.py:425
  42.8 0.0 collective-permute-done.8.edge_a_ref
  42.8 0.0 collective-permute-done.9.edge_b_ref
  42.8 0.0 copy-start.5
  42.8 0.0 copy-start.7
  42.8 4.3 %near_attention.1 = (f32[8,6,128,128]{3,2,1,0:T(8,128)S(1)}, f32[8,2,6,128]{3,2,1,0:T(8,128)S(1)}) custom-call(bf16[1024,768]{1,0:T(8,128)(2,1)S(1)} %get-tuple-element.35.q_t_ref, bf16[896,1024]{1,0:T(8,128)(2,1)S(1)} %get-tuple-element.33.k_ref, bf16[1024,896]{1,0:T(8,128)(2,1)S(1)} %get-tuple-element.34.v_t_ref, ...), custom_call_target="tpu_custom_call" | custom-call | flops 4000000000 | bytes 1 | tf_op jit(solution)/shard_map/near_attention/pallas_call | solution.py:389
  47.2 0.0 collective-permute-done.6.b_ref
  47.2 0.0 copy-done.5
  47.2 0.2 global_sums.1.own_sums_ref
  47.4 1.3 %collective-permute-start.7 = (f32[8,128]{1,0:T(8,128)S(1)}, f32[8,128]{1,0:T(8,128)S(1)}, u32[]{:S(2)}, u32[]{:S(2)}) collective-permute-start(f32[8,128]{1,0:T(8,128)S(1)} %global_sums.1.own_sums_ref), channel_id=1, source_target_pairs={{2,0},{3,1},{4,6},{5,7},{10,8},{11,9},{12,14},{13,15},{18,16},{19,... | collective-permute-start | bytes 12296 | tf_op jit(solution)/shard_map/ppermute | solution.py:425
  48.7 2.8 %collective-permute-done.12.kv_b_ref = bf16[128,1024]{1,0:T(8,128)(2,1)S(1)} collective-permute-done((bf16[128,1024]{1,0:T(8,128)(2,1)S(1)}, bf16[128,1024]{1,0:T(8,128)(2,1)S(1)}, u32[]{:S(2)}, u32[]{:S(2)}) %collective-permute-start.12) | collective-permute-done | bytes 262176 | tf_op jit(solution)/shard_map/ppermute | solution.py:425
  51.5 0.0 copy-done.7
  51.5 3.6 %far_attention.1.win_ref = f32[2,6,128]{2,1,0:T(8,128)S(1)} custom-call(bf16[1024,768]{1,0:T(8,128)(2,1)S(1)} %get-tuple-element.35.q_t_ref, f32[8,6,128,128]{3,2,1,0:T(8,128)S(1)} %get-tuple-element.40.acc_ref, f32[8,2,6,128]{3,2,1,0:T(8,128)S(1)} %get-tuple-element.41.stat_ref, bf16[128,1024]{1,0:T(8,128)(2,1)S(1)} %add_keys_values.3.kv_a_ref, ...), custom_call_target="tpu_custom_call" | custom-call | flops 2000000000 | bytes 1 | tf_op jit(solution)/shard_map/far_attention/pallas_call | solution.py:389
  55.1 0.8 %collective-permute-done.7.far_sums_ref = f32[8,128]{1,0:T(8,128)S(1)} collective-permute-done((f32[8,128]{1,0:T(8,128)S(1)}, f32[8,128]{1,0:T(8,128)S(1)}, u32[]{:S(2)}, u32[]{:S(2)}) %collective-permute-start.7) | collective-permute-done | bytes 4128 | tf_op jit(solution)/shard_map/ppermute | solution.py:425
  55.9 0.3 place_global.1
  56.2 0.1 collective-permute-start.13
  56.3 1.2 %collective-permute-done.13 = f32[2,3,128]{2,1,0:T(4,128)S(1)} collective-permute-done((f32[2,3,128]{2,1,0:T(4,128)S(1)}, f32[2,3,128]{2,1,0:T(4,128)S(1)}, u32[]{:S(2)}, u32[]{:S(2)}) %collective-permute-start.13) | collective-permute-done | bytes 3104 | tf_op jit(solution)/shard_map/ppermute | solution.py:418
  57.5 0.6 %fusion.4 = f32[384]{0:T(512)} fusion(f32[2,3,128]{2,1,0:T(4,128)S(1)} %collective-permute-done.13, f32[2,3,128]{2,1,0:T(4,128)S(1)} %get-tuple-element.43), kind=kLoop, calls=%fused_computation.5 | loop fusion | flops 1920 | bytes 7680 | tf_op jit(solution)/shard_map/mul | solution.py:535
  (11 shorter events, 0.2 us)
Async XLA Ops:
  0.0 1.9 %copy-start = (bf16[384,2048]{1,0:T(8,128)(2,1)S(1)}, bf16[384,2048]{1,0:T(8,128)(2,1)}, u32[]{:S(2)}) copy-start(bf16[384,2048]{1,0:T(8,128)(2,1)} %q_own_ref.1) | copy-start | bytes 4718596
  1.9 1.4 %copy-start.1 = (bf16[384,2048]{1,0:T(8,128)(2,1)S(1)}, bf16[384,2048]{1,0:T(8,128)(2,1)}, u32[]{:S(2)}) copy-start(bf16[384,2048]{1,0:T(8,128)(2,1)} %k_own_ref.1) | copy-start | bytes 4718596
  3.3 1.4 %copy-start.3 = (bf16[384,2048]{1,0:T(8,128)(2,1)S(1)}, bf16[384,2048]{1,0:T(8,128)(2,1)}, u32[]{:S(2)}) copy-start(bf16[384,2048]{1,0:T(8,128)(2,1)} %v_own_ref.1) | copy-start | bytes 4718596
  4.7 0.7 %copy-start.6 = (s32[64]{0:T(128)S(1)}, s32[64]{0:T(128)}, u32[]{:S(2)}) copy-start(s32[64]{0:T(128)} %param.8) | copy-start | bytes 772
  5.4 27.3 %copy-start.4 = (bf16[384,2048]{1,0:T(8,128)(2,1)S(1)}, bf16[384,2048]{1,0:T(8,128)(2,1)}, u32[]{:S(2)}) copy-start(bf16[384,2048]{1,0:T(8,128)(2,1)} %v_own_ref.1) | copy-start | bytes 4718596
  6.2 26.5 %copy-start.2 = (bf16[384,2048]{1,0:T(8,128)(2,1)S(1)}, bf16[384,2048]{1,0:T(8,128)(2,1)}, u32[]{:S(2)}) copy-start(bf16[384,2048]{1,0:T(8,128)(2,1)} %k_own_ref.1) | copy-start | bytes 4718596
  6.2 2.3 %collective-permute-start.3 = (bf16[256,1024]{1,0:T(8,128)(2,1)S(1)}, bf16[256,1024]{1,0:T(8,128)(2,1)S(1)}, u32[]{:S(2)}, u32[]{:S(2)}) collective-permute-start(bf16[256,1024]{1,0:T(8,128)(2,1)S(1)} %get-tuple-element.30), channel_id=1, source_target_pairs={{0,1},{1,0},{2,3},{3,2},{4,5},{5,4},{6,7},{7,6},{8,9},{9,8},{10,11... | collective-permute-start | bytes 1572872 | tf_op jit(solution)/shard_map/ppermute | solution.py:418
  6.7 1.7 %collective-permute-start = (bf16[64,1024]{1,0:T(8,128)(2,1)S(1)}, bf16[64,1024]{1,0:T(8,128)(2,1)S(1)}, u32[]{:S(2)}, u32[]{:S(2)}) collective-permute-start(bf16[64,1024]{1,0:T(8,128)(2,1)S(1)} %get-tuple-element.26), channel_id=1, source_target_pairs={{0,1},{1,0},{2,3},{3,2},{4,5},{5,4},{6,7},{7,6},{8,9},{9,8},{10,11... | collective-permute-start | bytes 393224 | tf_op jit(solution)/shard_map/ppermute | solution.py:418
  8.5 24.1 %collective-permute-start.4 = (bf16[1152,1024]{1,0:T(8,128)(2,1)S(1)}, bf16[1152,1024]{1,0:T(8,128)(2,1)S(1)}, u32[]{:S(2)}, u32[]{:S(2)}) collective-permute-start(bf16[1152,1024]{1,0:T(8,128)(2,1)S(1)} %get-tuple-element.32), channel_id=1, source_target_pairs={{0,1},{1,0},{2,3},{3,2},{4,5},{5,4},{6,7},{7,6},{8,9},{9,8},{10,11... | collective-permute-start | bytes 7077896 | tf_op jit(solution)/shard_map/ppermute | solution.py:418
  9.0 22.9 %collective-permute-start.10 = (bf16[128,1024]{1,0:T(8,128)(2,1)S(1)}, bf16[128,1024]{1,0:T(8,128)(2,1)S(1)}, u32[]{:S(2)}, u32[]{:S(2)}) collective-permute-start(bf16[128,1024]{1,0:T(8,128)(2,1)S(1)} %get-tuple-element.42.a_ref), channel_id=1, source_target_pairs={{0,2},{1,3},{6,4},{7,5},{8,10},{9,11},{14,12},{15,13},{16,18},{17,... | collective-permute-start | bytes 786440 | tf_op jit(solution)/shard_map/ppermute | solution.py:425
  13.6 8.9 %collective-permute-start.1 = (bf16[64,1024]{1,0:T(8,128)(2,1)S(1)}, bf16[64,1024]{1,0:T(8,128)(2,1)S(1)}, u32[]{:S(2)}, u32[]{:S(2)}) collective-permute-start(bf16[64,1024]{1,0:T(8,128)(2,1)S(1)} %add_queries.2.a_ref), channel_id=1, source_target_pairs={{0,2},{1,3},{2,0},{3,1},{4,6},{5,7},{6,4},{7,5},{8,10},{9,11},{10,... | collective-permute-start | bytes 393224 | tf_op jit(solution)/shard_map/ppermute | solution.py:418
  22.5 11.8 %collective-permute-start.2 = (bf16[64,1024]{1,0:T(8,128)(2,1)S(1)}, bf16[64,1024]{1,0:T(8,128)(2,1)S(1)}, u32[]{:S(2)}, u32[]{:S(2)}) collective-permute-start(bf16[64,1024]{1,0:T(8,128)(2,1)S(1)} %add_queries.3.q_a_ref), channel_id=1, source_target_pairs={{0,4},{1,5},{2,6},{3,7},{4,0},{5,1},{6,2},{7,3},{8,12},{9,13},{10,... | collective-permute-start | bytes 393224 | tf_op jit(solution)/shard_map/ppermute | solution.py:418
  26.1 16.7 %collective-permute-start.8 = (bf16[128,1024]{1,0:T(8,128)(2,1)S(1)}, bf16[128,1024]{1,0:T(8,128)(2,1)S(1)}, u32[]{:S(2)}, u32[]{:S(2)}) collective-permute-start(bf16[128,1024]{1,0:T(8,128)(2,1)S(1)} %get-tuple-element.38), channel_id=1, source_target_pairs={{1,3},{2,0},{3,5},{4,2},{5,7},{6,4},{9,11},{10,8},{11,13},{12,10},... | collective-permute-start | bytes 786440 | tf_op jit(solution)/shard_map/ppermute | solution.py:422
  27.3 15.5 %collective-permute-start.9 = (bf16[128,1024]{1,0:T(8,128)(2,1)S(1)}, bf16[128,1024]{1,0:T(8,128)(2,1)S(1)}, u32[]{:S(2)}, u32[]{:S(2)}) collective-permute-start(bf16[128,1024]{1,0:T(8,128)(2,1)S(1)} %get-tuple-element.39), channel_id=1, source_target_pairs={{0,2},{2,4},{3,1},{4,6},{5,3},{7,5},{8,10},{10,12},{11,9},{12,14},... | collective-permute-start | bytes 786440 | tf_op jit(solution)/shard_map/ppermute | solution.py:422
  32.0 7.5 %collective-permute-start.11 = (bf16[128,1024]{1,0:T(8,128)(2,1)S(1)}, bf16[128,1024]{1,0:T(8,128)(2,1)S(1)}, u32[]{:S(2)}, u32[]{:S(2)}) collective-permute-start(bf16[128,1024]{1,0:T(8,128)(2,1)S(1)} %add_keys_values.2.a_ref), channel_id=1, source_target_pairs={{2,4},{3,5},{4,2},{5,3},{10,12},{11,13},{12,10},{13,11},{18,20},{1... | collective-permute-start | bytes 786440 | tf_op jit(solution)/shard_map/ppermute | solution.py:425
  35.7 6.4 %collective-permute-start.5 = (bf16[4,144,128]{2,1,0:T(8,128)(2,1)S(1)}, bf16[4,144,128]{2,1,0:T(8,128)(2,1)S(1)}, u32[]{:S(2)}, u32[]{:S(2)}) collective-permute-start(bf16[4,144,128]{2,1,0:T(8,128)(2,1)S(1)} %global_partial.1.a_ref), channel_id=1, source_target_pairs={{0,2},{1,3},{6,4},{7,5},{8,10},{9,11},{14,12},{15,13},{16,18},{17,... | collective-permute-start | bytes 442376 | tf_op jit(solution)/shard_map/ppermute | solution.py:425
  39.5 12.0 %collective-permute-start.12 = (bf16[128,1024]{1,0:T(8,128)(2,1)S(1)}, bf16[128,1024]{1,0:T(8,128)(2,1)S(1)}, u32[]{:S(2)}, u32[]{:S(2)}) collective-permute-start(bf16[128,1024]{1,0:T(8,128)(2,1)S(1)} %add_keys_values.3.kv_a_ref), channel_id=1, source_target_pairs={{2,0},{3,1},{4,6},{5,7},{10,8},{11,9},{12,14},{13,15},{18,16},{19,... | collective-permute-start | bytes 786440 | tf_op jit(solution)/shard_map/ppermute | solution.py:425
  42.1 5.1 %collective-permute-start.6 = (bf16[4,144,128]{2,1,0:T(8,128)(2,1)S(1)}, bf16[4,144,128]{2,1,0:T(8,128)(2,1)S(1)}, u32[]{:S(2)}, u32[]{:S(2)}) collective-permute-start(bf16[4,144,128]{2,1,0:T(8,128)(2,1)S(1)} %merge_partial.1.a_ref), channel_id=1, source_target_pairs={{2,4},{3,5},{4,2},{5,3},{10,12},{11,13},{12,10},{13,11},{18,20},{1... | collective-permute-start | bytes 442376 | tf_op jit(solution)/shard_map/ppermute | solution.py:425
  42.8 4.4 %copy-start.5 = (f32[2048]{0:T(1024)S(1)}, f32[2048]{0:T(1024)}, u32[]{:S(2)}) copy-start(f32[2048]{0:T(1024)} %param.9) | copy-start | bytes 24580
  42.8 8.7 %copy-start.7 = (s32[64]{0:T(128)S(1)}, s32[64]{0:T(128)}, u32[]{:S(2)}) copy-start(s32[64]{0:T(128)} %param.8) | copy-start | bytes 772
  47.4 8.5 %collective-permute-start.7 = (f32[8,128]{1,0:T(8,128)S(1)}, f32[8,128]{1,0:T(8,128)S(1)}, u32[]{:S(2)}, u32[]{:S(2)}) collective-permute-start(f32[8,128]{1,0:T(8,128)S(1)} %global_sums.1.own_sums_ref), channel_id=1, source_target_pairs={{2,0},{3,1},{4,6},{5,7},{10,8},{11,9},{12,14},{13,15},{18,16},{19,... | collective-permute-start | bytes 12296 | tf_op jit(solution)/shard_map/ppermute | solution.py:425
  56.2 1.2 %collective-permute-start.13 = (f32[2,3,128]{2,1,0:T(4,128)S(1)}, f32[2,3,128]{2,1,0:T(4,128)S(1)}, u32[]{:S(2)}, u32[]{:S(2)}) collective-permute-start(f32[2,3,128]{2,1,0:T(4,128)S(1)} %get-tuple-element.44), channel_id=1, source_target_pairs={{0,1},{1,0},{2,3},{3,2},{4,5},{5,4},{6,7},{7,6},{8,9},{9,8},{10,11... | collective-permute-start | bytes 9224 | tf_op jit(solution)/shard_map/ppermute | solution.py:418

commit v2 on v1

--- a/solution.py
+++ b/solution.py
@@ -443,20 +443,20 @@
         [((1, glob), jnp.int32), ((CORES, rows, half), bf16), pltpu.SemaphoreType.DMA((3,))],
         from_hbm=True,
     )
-    later_positions = after((row_positions,), q_sib)[0]
+    q_near = call(add_kernel, "add_queries", small, [q_own, swap(q_sib, 1)])
+    later_positions = after((row_positions,), q_near)[0]
     kv_own, edge_own, kv_sib, bulk_sib = call(
         functools.partial(select_kv_kernel, half),
         "select_keys_values",
         [pair_of, edge, ((2 * glob + 2 * BLK, half), bf16), ((3 * rows, half), bf16)],
         [later_positions, keys, values, queries],
     )
-    q_near = call(add_kernel, "add_queries", small, [q_own, swap(q_sib, 1)])
     kv_near, edge_recv = call(split_kernel, "join_keys_values", [pair_of, edge], [kv_own, swap(kv_sib, 1)])
-    bulk_sib = after((bulk_sib,), q_near, kv_near)[0]
+    bulk_sib = after((bulk_sib,), kv_near)[0]
     bulk_recv = swap(bulk_sib, 1)
-    kv_near = after((kv_near,), q_near)[0]
     for r in range(1, rounds):
         q_near = call(add_kernel, "add_queries", small, [q_near, swap(q_near, 1 << r)])
+    kv_near = after((kv_near,), q_near)[0]
     q_far = swap(q_near, 1 << rounds)
 
     edge_own, edge_recv = after((edge_own, edge_recv), q_near)

time: 58.4 us -> 56.6 us (0.969)
  waiting for transfers between devices: 16.5 us -> 12.9 us
  starting transfers between devices: 22.9 us -> 25.5 us
  local copies, waits for them, and re-layouts: 3.54 us -> 2.83 us
    ppermute x6, waiting for transfers between devices: 11.6 us -> 7.85 us  [swap(): return lax.ppermute(x, 'seq', [(i, i ^ mask) for i in range(seq_count)])]
    ppermute x6, starting transfers between devices: 12.3 us -> 14.4 us  [move(): lax.ppermute(x, 'seq', [(a * CORES + c, b * CORES + c) for a, b in pairs...]
    unnamed x16 -> x14, local copies, waits for them, and re-layouts: 3.54 us -> 2.83 us
    ppermute x2, starting transfers between devices: 5.84 us -> 6.48 us  [shift(): lax.ppermute(x, 'seq', [(i, to) for i, to in moves if 0 <= to < seq_count])]
  transfers between devices with their start and end apart: 14 -> 14, of which waited for: 6 -> 8; matrix products, arithmetic and copies ran while one was open for 0% -> 0% of each run, Pallas kernels for 19% -> 20%
where the time goes in v2:
time: 56.6 us; the launch traced here: 56.3 us
  starting transfers between devices  25.5 us (45%)
  Pallas kernels  14.2 us (25%)
  waiting for transfers between devices  12.9 us (23%)
  local copies, waits for them, and re-layouts  2.83 us (5%)
  other arithmetic  0.59 us (1%)
    ppermute x6, starting transfers between devices, move(): lax.ppermute(x, 'seq', [(a * CORES + c, b * CORES + c) for a, b in pairs...  14.4 us
    pallas_call x14, Pallas kernels, call(): pl.pallas_call(kernel, in_specs=[pl.BlockSpec(memory_space=source)] * len...  14.2 us
    ppermute x6, waiting for transfers between devices, swap(): return lax.ppermute(x, 'seq', [(i, i ^ mask) for i in range(seq_count)])  7.85 us
    ppermute x2, starting transfers between devices, shift(): lax.ppermute(x, 'seq', [(i, to) for i, to in moves if 0 <= to < seq_count])  6.48 us
    ppermute x6, waiting for transfers between devices, move(): lax.ppermute(x, 'seq', [(a * CORES + c, b * CORES + c) for a, b in pairs...  5.03 us
    ppermute x6, starting transfers between devices, swap(): return lax.ppermute(x, 'seq', [(i, i ^ mask) for i in range(seq_count)])  4.63 us
    unnamed x14, local copies, waits for them, and re-layouts  2.83 us
  transfers between devices with their start and end apart: 14, of which 8 were waited for; matrix products, arithmetic and copies ran while one was open for 0% of the time, Pallas kernels for 20%

profile of v2, /device:TPU:0, one launch (start us, length us, event | category | flops | bytes accessed | tf_op | source)
XLA Modules:
  0.0 56.3 jit_solution(13537762767794123354)
XLA Ops:
  0.0 0.0 copy-start
  0.0 1.8 %select_queries.1 = (bf16[64,1024]{1,0:T(8,128)(2,1)S(1)}, bf16[64,1024]{1,0:T(8,128)(2,1)S(1)}) custom-call(s32[1,64]{1,0:T(1,128)} %bitcast.6, bf16[384,2048]{1,0:T(8,128)(2,1)} %q_own_ref.1), custom_call_target="tpu_custom_call" | custom-call | flops 1 | bytes 1 | tf_op jit(solution)/shard_map/select_queries/pallas_call | solution.py:389
  1.8 0.5 collective-permute-start
  2.4 1.0 %collective-permute-done.b_ref = bf16[64,1024]{1,0:T(8,128)(2,1)S(1)} collective-permute-done((bf16[64,1024]{1,0:T(8,128)(2,1)S(1)}, bf16[64,1024]{1,0:T(8,128)(2,1)S(1)}, u32[]{:S(2)}, u32[]{:S(2)}) %collective-permute-start) | collective-permute-done | bytes 131104 | tf_op jit(solution)/shard_map/ppermute | solution.py:418
  3.4 0.0 copy-done.6
  3.4 0.0 copy-done
  3.4 0.0 copy-start.1
  3.4 1.4 %copy-done.1 = bf16[384,2048]{1,0:T(8,128)(2,1)S(1)} copy-done((bf16[384,2048]{1,0:T(8,128)(2,1)S(1)}, bf16[384,2048]{1,0:T(8,128)(2,1)}, u32[]{:S(2)}) %copy-start.1) | copy-done | bytes 1572888
  4.8 1.4 %copy-done.3 = bf16[384,2048]{1,0:T(8,128)(2,1)S(1)} copy-done((bf16[384,2048]{1,0:T(8,128)(2,1)S(1)}, bf16[384,2048]{1,0:T(8,128)(2,1)}, u32[]{:S(2)}) %copy-start.3) | copy-done | bytes 1572888
  6.2 0.8 %select_keys_values.1 = (bf16[128,1024]{1,0:T(8,128)(2,1)S(1)}, bf16[128,1024]{1,0:T(8,128)(2,1)S(1)}, bf16[256,1024]{1,0:T(8,128)(2,1)S(1)}, bf16[1152,1024]{1,0:T(8,128)(2,1)S(1)}) custom-call(s32[1,64]{1,0:T(1,128)S(1)} %bitcast.7, bf16[384,2048]{1,0:T(8,128)(2,1)S(1)} %copy-done.1, bf16[384,2048]{1,0:T(8,128)(2,1)S(1)} %copy-done.3, ...), custom_call_target="tpu_custom_call" | custom-call | flops 1 | bytes 1 | tf_op jit(solution)/shard_map/select_keys_values/pallas_call | solution.py:389
  7.0 0.0 copy-start.2
  7.0 0.4 collective-permute-start.3
  7.5 1.5 %collective-permute-done.3.b_ref = bf16[256,1024]{1,0:T(8,128)(2,1)S(1)} collective-permute-done((bf16[256,1024]{1,0:T(8,128)(2,1)S(1)}, bf16[256,1024]{1,0:T(8,128)(2,1)S(1)}, u32[]{:S(2)}, u32[]{:S(2)}) %collective-permute-start.3) | collective-permute-done | bytes 524320 | tf_op jit(solution)/shard_map/ppermute | solution.py:418
  9.1 0.4 collective-permute-start.4
  9.5 2.7 %collective-permute-start.1 = (bf16[64,1024]{1,0:T(8,128)(2,1)S(1)}, bf16[64,1024]{1,0:T(8,128)(2,1)S(1)}, u32[]{:S(2)}, u32[]{:S(2)}) collective-permute-start(bf16[64,1024]{1,0:T(8,128)(2,1)S(1)} %add_queries.2.a_ref), channel_id=1, source_target_pairs={{0,2},{1,3},{2,0},{3,1},{4,6},{5,7},{6,4},{7,5},{8,10},{9,11},{10,... | collective-permute-start | bytes 393224 | tf_op jit(solution)/shard_map/ppermute | solution.py:418
  12.2 4.0 %collective-permute-done.1.b_ref = bf16[64,1024]{1,0:T(8,128)(2,1)S(1)} collective-permute-done((bf16[64,1024]{1,0:T(8,128)(2,1)S(1)}, bf16[64,1024]{1,0:T(8,128)(2,1)S(1)}, u32[]{:S(2)}, u32[]{:S(2)}) %collective-permute-start.1) | collective-permute-done | bytes 131104 | tf_op jit(solution)/shard_map/ppermute | solution.py:418
  16.2 3.7 %collective-permute-start.10 = (bf16[128,1024]{1,0:T(8,128)(2,1)S(1)}, bf16[128,1024]{1,0:T(8,128)(2,1)S(1)}, u32[]{:S(2)}, u32[]{:S(2)}) collective-permute-start(bf16[128,1024]{1,0:T(8,128)(2,1)S(1)} %get-tuple-element.42.a_ref), channel_id=1, source_target_pairs={{0,2},{1,3},{6,4},{7,5},{8,10},{9,11},{14,12},{15,13},{16,18},{17,... | collective-permute-start | bytes 786440 | tf_op jit(solution)/shard_map/ppermute | solution.py:425
  19.9 0.5 collective-permute-start.2
  20.4 1.3 %collective-permute-start.8 = (bf16[128,1024]{1,0:T(8,128)(2,1)S(1)}, bf16[128,1024]{1,0:T(8,128)(2,1)S(1)}, u32[]{:S(2)}, u32[]{:S(2)}) collective-permute-start(bf16[128,1024]{1,0:T(8,128)(2,1)S(1)} %get-tuple-element.38), channel_id=1, source_target_pairs={{1,3},{2,0},{3,5},{4,2},{5,7},{6,4},{9,11},{10,8},{11,13},{12,10},... | collective-permute-start | bytes 786440 | tf_op jit(solution)/shard_map/ppermute | solution.py:422
  21.7 5.2 %collective-permute-start.9 = (bf16[128,1024]{1,0:T(8,128)(2,1)S(1)}, bf16[128,1024]{1,0:T(8,128)(2,1)S(1)}, u32[]{:S(2)}, u32[]{:S(2)}) collective-permute-start(bf16[128,1024]{1,0:T(8,128)(2,1)S(1)} %get-tuple-element.39), channel_id=1, source_target_pairs={{0,2},{2,4},{3,1},{4,6},{5,3},{7,5},{8,10},{10,12},{11,9},{12,14},... | collective-permute-start | bytes 786440 | tf_op jit(solution)/shard_map/ppermute | solution.py:422
  26.9 0.0 collective-permute-done.10.b_ref
  26.9 0.7 %collective-permute-start.11 = (bf16[128,1024]{1,0:T(8,128)(2,1)S(1)}, bf16[128,1024]{1,0:T(8,128)(2,1)S(1)}, u32[]{:S(2)}, u32[]{:S(2)}) collective-permute-start(bf16[128,1024]{1,0:T(8,128)(2,1)S(1)} %add_keys_values.2.a_ref), channel_id=1, source_target_pairs={{2,4},{3,5},{4,2},{5,3},{10,12},{11,13},{12,10},{13,11},{18,20},{1... | collective-permute-start | bytes 786440 | tf_op jit(solution)/shard_map/ppermute | solution.py:425
  27.6 0.0 collective-permute-done.4.sib_ref
  27.6 0.0 copy-done.4
  27.6 0.0 copy-done.2
  27.6 1.6 %prepare.1 = (bf16[896,1024]{1,0:T(8,128)(2,1)S(1)}, bf16[1024,896]{1,0:T(8,128)(2,1)S(1)}, bf16[1024,768]{1,0:T(8,128)(2,1)S(1)}) custom-call(bf16[384,2048]{1,0:T(8,128)(2,1)S(1)} %copy-done, bf16[384,2048]{1,0:T(8,128)(2,1)S(1)} %copy-done.2, bf16[384,2048]{1,0:T(8,128)(2,1)S(1)} %copy-done.4, bf16[1152,1024]{1,0:T(8,128)(2,1)S(1)} %collective-permute-done.4.sib_ref), custom_call_target="tpu_custom_call" | custom-call | flops 1600000000 | bytes 1 | tf_op jit(solution)/shard_map/prepare/pallas_call | solution.py:389
  29.3 0.1 collective-permute-done.2.q_b_ref
  29.4 1.3 %global_partial.1.a_ref = bf16[4,144,128]{2,1,0:T(8,128)(2,1)S(1)} custom-call(bf16[64,1024]{1,0:T(8,128)(2,1)S(1)} %add_queries.3.q_a_ref, bf16[64,1024]{1,0:T(8,128)(2,1)S(1)} %collective-permute-done.2.q_b_ref, bf16[896,1024]{1,0:T(8,128)(2,1)S(1)} %get-tuple-element.33.k_ref, bf16[1024,896]{1,0:T(8,128)(2,1)S(1)} %get-tuple-element.34.v_t_ref), custom_call_target="tpu_custom_call" | custom-call | flops 1 | bytes 1 | tf_op jit(solution)/shard_map/global_partial/pallas_call | solution.py:389
  30.8 6.8 %collective-permute-start.5 = (bf16[4,144,128]{2,1,0:T(8,128)(2,1)S(1)}, bf16[4,144,128]{2,1,0:T(8,128)(2,1)S(1)}, u32[]{:S(2)}, u32[]{:S(2)}) collective-permute-start(bf16[4,144,128]{2,1,0:T(8,128)(2,1)S(1)} %global_partial.1.a_ref), channel_id=1, source_target_pairs={{0,2},{1,3},{6,4},{7,5},{8,10},{9,11},{14,12},{15,13},{16,18},{17,... | collective-permute-start | bytes 442376 | tf_op jit(solution)/shard_map/ppermute | solution.py:425
  37.6 0.0 collective-permute-done.11.b_ref
  37.7 1.3 %collective-permute-start.12 = (bf16[128,1024]{1,0:T(8,128)(2,1)S(1)}, bf16[128,1024]{1,0:T(8,128)(2,1)S(1)}, u32[]{:S(2)}, u32[]{:S(2)}) collective-permute-start(bf16[128,1024]{1,0:T(8,128)(2,1)S(1)} %add_keys_values.3.kv_a_ref), channel_id=1, source_target_pairs={{2,0},{3,1},{4,6},{5,7},{10,8},{11,9},{12,14},{13,15},{18,16},{19,... | collective-permute-start | bytes 786440 | tf_op jit(solution)/shard_map/ppermute | solution.py:425
  39.0 1.3 %collective-permute-done.5.b_ref = bf16[4,144,128]{2,1,0:T(8,128)(2,1)S(1)} collective-permute-done((bf16[4,144,128]{2,1,0:T(8,128)(2,1)S(1)}, bf16[4,144,128]{2,1,0:T(8,128)(2,1)S(1)}, u32[]{:S(2)}, u32[]{:S(2)}) %collective-permute-start.5) | collective-permute-done | bytes 147488 | tf_op jit(solution)/shard_map/ppermute | solution.py:425
  40.3 0.7 %collective-permute-start.6 = (bf16[4,144,128]{2,1,0:T(8,128)(2,1)S(1)}, bf16[4,144,128]{2,1,0:T(8,128)(2,1)S(1)}, u32[]{:S(2)}, u32[]{:S(2)}) collective-permute-start(bf16[4,144,128]{2,1,0:T(8,128)(2,1)S(1)} %merge_partial.1.a_ref), channel_id=1, source_target_pairs={{2,4},{3,5},{4,2},{5,3},{10,12},{11,13},{12,10},{13,11},{18,20},{1... | collective-permute-start | bytes 442376 | tf_op jit(solution)/shard_map/ppermute | solution.py:425
  41.0 0.0 collective-permute-done.8.edge_a_ref
  41.0 0.0 collective-permute-done.9.edge_b_ref
  41.0 0.0 copy-start.5
  41.0 4.3 %near_attention.1 = (f32[8,6,128,128]{3,2,1,0:T(8,128)S(1)}, f32[8,2,6,128]{3,2,1,0:T(8,128)S(1)}) custom-call(bf16[1024,768]{1,0:T(8,128)(2,1)S(1)} %get-tuple-element.35.q_t_ref, bf16[896,1024]{1,0:T(8,128)(2,1)S(1)} %get-tuple-element.33.k_ref, bf16[1024,896]{1,0:T(8,128)(2,1)S(1)} %get-tuple-element.34.v_t_ref, ...), custom_call_target="tpu_custom_call" | custom-call | flops 4000000000 | bytes 1 | tf_op jit(solution)/shard_map/near_attention/pallas_call | solution.py:389
  45.3 0.0 collective-permute-done.6.b_ref
  45.4 0.0 copy-done.5
  45.4 0.2 global_sums.1.own_sums_ref
  45.6 1.3 %collective-permute-start.7 = (f32[8,128]{1,0:T(8,128)S(1)}, f32[8,128]{1,0:T(8,128)S(1)}, u32[]{:S(2)}, u32[]{:S(2)}) collective-permute-start(f32[8,128]{1,0:T(8,128)S(1)} %global_sums.1.own_sums_ref), channel_id=1, source_target_pairs={{2,0},{3,1},{4,6},{5,7},{10,8},{11,9},{12,14},{13,15},{18,16},{19,... | collective-permute-start | bytes 12296 | tf_op jit(solution)/shard_map/ppermute | solution.py:425
  46.9 2.9 %collective-permute-done.12.kv_b_ref = bf16[128,1024]{1,0:T(8,128)(2,1)S(1)} collective-permute-done((bf16[128,1024]{1,0:T(8,128)(2,1)S(1)}, bf16[128,1024]{1,0:T(8,128)(2,1)S(1)}, u32[]{:S(2)}, u32[]{:S(2)}) %collective-permute-start.12) | collective-permute-done | bytes 262176 | tf_op jit(solution)/shard_map/ppermute | solution.py:425
  49.8 3.6 %far_attention.1.win_ref = f32[2,6,128]{2,1,0:T(8,128)S(1)} custom-call(bf16[1024,768]{1,0:T(8,128)(2,1)S(1)} %get-tuple-element.35.q_t_ref, f32[8,6,128,128]{3,2,1,0:T(8,128)S(1)} %get-tuple-element.40.acc_ref, f32[8,2,6,128]{3,2,1,0:T(8,128)S(1)} %get-tuple-element.41.stat_ref, bf16[128,1024]{1,0:T(8,128)(2,1)S(1)} %add_keys_values.3.kv_a_ref, ...), custom_call_target="tpu_custom_call" | custom-call | flops 2000000000 | bytes 1 | tf_op jit(solution)/shard_map/far_attention/pallas_call | solution.py:389
  53.3 0.8 %collective-permute-done.7.far_sums_ref = f32[8,128]{1,0:T(8,128)S(1)} collective-permute-done((f32[8,128]{1,0:T(8,128)S(1)}, f32[8,128]{1,0:T(8,128)S(1)}, u32[]{:S(2)}, u32[]{:S(2)}) %collective-permute-start.7) | collective-permute-done | bytes 4128 | tf_op jit(solution)/shard_map/ppermute | solution.py:425
  54.2 0.3 place_global.1
  54.5 0.1 collective-permute-start.13
  54.6 1.2 %collective-permute-done.13 = f32[2,3,128]{2,1,0:T(4,128)S(1)} collective-permute-done((f32[2,3,128]{2,1,0:T(4,128)S(1)}, f32[2,3,128]{2,1,0:T(4,128)S(1)}, u32[]{:S(2)}, u32[]{:S(2)}) %collective-permute-start.13) | collective-permute-done | bytes 3104 | tf_op jit(solution)/shard_map/ppermute | solution.py:418
  55.7 0.6 %fusion.4 = f32[384]{0:T(512)} fusion(f32[2,3,128]{2,1,0:T(4,128)S(1)} %collective-permute-done.13, f32[2,3,128]{2,1,0:T(4,128)S(1)} %get-tuple-element.43), kind=kLoop, calls=%fused_computation.5 | loop fusion | flops 1920 | bytes 7680 | tf_op jit(solution)/shard_map/mul | solution.py:535
  (9 shorter events, 0.2 us)
Async XLA Ops:
  0.0 3.4 %copy-start.6 = (s32[64]{0:T(128)S(1)}, s32[64]{0:T(128)}, u32[]{:S(2)}) copy-start(s32[64]{0:T(128)} %param.8) | copy-start | bytes 772
  0.0 3.4 %copy-start = (bf16[384,2048]{1,0:T(8,128)(2,1)S(1)}, bf16[384,2048]{1,0:T(8,128)(2,1)}, u32[]{:S(2)}) copy-start(bf16[384,2048]{1,0:T(8,128)(2,1)} %q_own_ref.1) | copy-start | bytes 4718596
  1.8 1.5 %collective-permute-start = (bf16[64,1024]{1,0:T(8,128)(2,1)S(1)}, bf16[64,1024]{1,0:T(8,128)(2,1)S(1)}, u32[]{:S(2)}, u32[]{:S(2)}) collective-permute-start(bf16[64,1024]{1,0:T(8,128)(2,1)S(1)} %get-tuple-element.26), channel_id=1, source_target_pairs={{0,1},{1,0},{2,3},{3,2},{4,5},{5,4},{6,7},{7,6},{8,9},{9,8},{10,11... | collective-permute-start | bytes 393224 | tf_op jit(solution)/shard_map/ppermute | solution.py:418
  3.4 1.4 %copy-start.1 = (bf16[384,2048]{1,0:T(8,128)(2,1)S(1)}, bf16[384,2048]{1,0:T(8,128)(2,1)}, u32[]{:S(2)}) copy-start(bf16[384,2048]{1,0:T(8,128)(2,1)} %k_own_ref.1) | copy-start | bytes 4718596
  4.8 1.4 %copy-start.3 = (bf16[384,2048]{1,0:T(8,128)(2,1)S(1)}, bf16[384,2048]{1,0:T(8,128)(2,1)}, u32[]{:S(2)}) copy-start(bf16[384,2048]{1,0:T(8,128)(2,1)} %v_own_ref.1) | copy-start | bytes 4718596
  6.2 21.4 %copy-start.4 = (bf16[384,2048]{1,0:T(8,128)(2,1)S(1)}, bf16[384,2048]{1,0:T(8,128)(2,1)}, u32[]{:S(2)}) copy-start(bf16[384,2048]{1,0:T(8,128)(2,1)} %v_own_ref.1) | copy-start | bytes 4718596
  7.0 20.6 %copy-start.2 = (bf16[384,2048]{1,0:T(8,128)(2,1)S(1)}, bf16[384,2048]{1,0:T(8,128)(2,1)}, u32[]{:S(2)}) copy-start(bf16[384,2048]{1,0:T(8,128)(2,1)} %k_own_ref.1) | copy-start | bytes 4718596
  7.0 2.0 %collective-permute-start.3 = (bf16[256,1024]{1,0:T(8,128)(2,1)S(1)}, bf16[256,1024]{1,0:T(8,128)(2,1)S(1)}, u32[]{:S(2)}, u32[]{:S(2)}) collective-permute-start(bf16[256,1024]{1,0:T(8,128)(2,1)S(1)} %get-tuple-element.30), channel_id=1, source_target_pairs={{0,1},{1,0},{2,3},{3,2},{4,5},{5,4},{6,7},{7,6},{8,9},{9,8},{10,11... | collective-permute-start | bytes 1572872 | tf_op jit(solution)/shard_map/ppermute | solution.py:418
  9.1 18.5 %collective-permute-start.4 = (bf16[1152,1024]{1,0:T(8,128)(2,1)S(1)}, bf16[1152,1024]{1,0:T(8,128)(2,1)S(1)}, u32[]{:S(2)}, u32[]{:S(2)}) collective-permute-start(bf16[1152,1024]{1,0:T(8,128)(2,1)S(1)} %get-tuple-element.32), channel_id=1, source_target_pairs={{0,1},{1,0},{2,3},{3,2},{4,5},{5,4},{6,7},{7,6},{8,9},{9,8},{10,11... | collective-permute-start | bytes 7077896 | tf_op jit(solution)/shard_map/ppermute | solution.py:418
  9.5 6.7 %collective-permute-start.1 = (bf16[64,1024]{1,0:T(8,128)(2,1)S(1)}, bf16[64,1024]{1,0:T(8,128)(2,1)S(1)}, u32[]{:S(2)}, u32[]{:S(2)}) collective-permute-start(bf16[64,1024]{1,0:T(8,128)(2,1)S(1)} %add_queries.2.a_ref), channel_id=1, source_target_pairs={{0,2},{1,3},{2,0},{3,1},{4,6},{5,7},{6,4},{7,5},{8,10},{9,11},{10,... | collective-permute-start | bytes 393224 | tf_op jit(solution)/shard_map/ppermute | solution.py:418
  16.2 10.6 %collective-permute-start.10 = (bf16[128,1024]{1,0:T(8,128)(2,1)S(1)}, bf16[128,1024]{1,0:T(8,128)(2,1)S(1)}, u32[]{:S(2)}, u32[]{:S(2)}) collective-permute-start(bf16[128,1024]{1,0:T(8,128)(2,1)S(1)} %get-tuple-element.42.a_ref), channel_id=1, source_target_pairs={{0,2},{1,3},{6,4},{7,5},{8,10},{9,11},{14,12},{15,13},{16,18},{17,... | collective-permute-start | bytes 786440 | tf_op jit(solution)/shard_map/ppermute | solution.py:425
  19.9 9.5 %collective-permute-start.2 = (bf16[64,1024]{1,0:T(8,128)(2,1)S(1)}, bf16[64,1024]{1,0:T(8,128)(2,1)S(1)}, u32[]{:S(2)}, u32[]{:S(2)}) collective-permute-start(bf16[64,1024]{1,0:T(8,128)(2,1)S(1)} %add_queries.3.q_a_ref), channel_id=1, source_target_pairs={{0,4},{1,5},{2,6},{3,7},{4,0},{5,1},{6,2},{7,3},{8,12},{9,13},{10,... | collective-permute-start | bytes 393224 | tf_op jit(solution)/shard_map/ppermute | solution.py:418
  20.4 20.6 %collective-permute-start.8 = (bf16[128,1024]{1,0:T(8,128)(2,1)S(1)}, bf16[128,1024]{1,0:T(8,128)(2,1)S(1)}, u32[]{:S(2)}, u32[]{:S(2)}) collective-permute-start(bf16[128,1024]{1,0:T(8,128)(2,1)S(1)} %get-tuple-element.38), channel_id=1, source_target_pairs={{1,3},{2,0},{3,5},{4,2},{5,7},{6,4},{9,11},{10,8},{11,13},{12,10},... | collective-permute-start | bytes 786440 | tf_op jit(solution)/shard_map/ppermute | solution.py:422
  21.7 19.3 %collective-permute-start.9 = (bf16[128,1024]{1,0:T(8,128)(2,1)S(1)}, bf16[128,1024]{1,0:T(8,128)(2,1)S(1)}, u32[]{:S(2)}, u32[]{:S(2)}) collective-permute-start(bf16[128,1024]{1,0:T(8,128)(2,1)S(1)} %get-tuple-element.39), channel_id=1, source_target_pairs={{0,2},{2,4},{3,1},{4,6},{5,3},{7,5},{8,10},{10,12},{11,9},{12,14},... | collective-permute-start | bytes 786440 | tf_op jit(solution)/shard_map/ppermute | solution.py:422
  26.9 10.7 %collective-permute-start.11 = (bf16[128,1024]{1,0:T(8,128)(2,1)S(1)}, bf16[128,1024]{1,0:T(8,128)(2,1)S(1)}, u32[]{:S(2)}, u32[]{:S(2)}) collective-permute-start(bf16[128,1024]{1,0:T(8,128)(2,1)S(1)} %add_keys_values.2.a_ref), channel_id=1, source_target_pairs={{2,4},{3,5},{4,2},{5,3},{10,12},{11,13},{12,10},{13,11},{18,20},{1... | collective-permute-start | bytes 786440 | tf_op jit(solution)/shard_map/ppermute | solution.py:425
  30.8 9.5 %collective-permute-start.5 = (bf16[4,144,128]{2,1,0:T(8,128)(2,1)S(1)}, bf16[4,144,128]{2,1,0:T(8,128)(2,1)S(1)}, u32[]{:S(2)}, u32[]{:S(2)}) collective-permute-start(bf16[4,144,128]{2,1,0:T(8,128)(2,1)S(1)} %global_partial.1.a_ref), channel_id=1, source_target_pairs={{0,2},{1,3},{6,4},{7,5},{8,10},{9,11},{14,12},{15,13},{16,18},{17,... | collective-permute-start | bytes 442376 | tf_op jit(solution)/shard_map/ppermute | solution.py:425
  37.7 12.1 %collective-permute-start.12 = (bf16[128,1024]{1,0:T(8,128)(2,1)S(1)}, bf16[128,1024]{1,0:T(8,128)(2,1)S(1)}, u32[]{:S(2)}, u32[]{:S(2)}) collective-permute-start(bf16[128,1024]{1,0:T(8,128)(2,1)S(1)} %add_keys_values.3.kv_a_ref), channel_id=1, source_target_pairs={{2,0},{3,1},{4,6},{5,7},{10,8},{11,9},{12,14},{13,15},{18,16},{19,... | collective-permute-start | bytes 786440 | tf_op jit(solution)/shard_map/ppermute | solution.py:425
  40.3 5.1 %collective-permute-start.6 = (bf16[4,144,128]{2,1,0:T(8,128)(2,1)S(1)}, bf16[4,144,128]{2,1,0:T(8,128)(2,1)S(1)}, u32[]{:S(2)}, u32[]{:S(2)}) collective-permute-start(bf16[4,144,128]{2,1,0:T(8,128)(2,1)S(1)} %merge_partial.1.a_ref), channel_id=1, source_target_pairs={{2,4},{3,5},{4,2},{5,3},{10,12},{11,13},{12,10},{13,11},{18,20},{1... | collective-permute-start | bytes 442376 | tf_op jit(solution)/shard_map/ppermute | solution.py:425
  41.0 4.4 %copy-start.5 = (f32[2048]{0:T(1024)S(1)}, f32[2048]{0:T(1024)}, u32[]{:S(2)}) copy-start(f32[2048]{0:T(1024)} %param.9) | copy-start | bytes 24580
  45.6 8.6 %collective-permute-start.7 = (f32[8,128]{1,0:T(8,128)S(1)}, f32[8,128]{1,0:T(8,128)S(1)}, u32[]{:S(2)}, u32[]{:S(2)}) collective-permute-start(f32[8,128]{1,0:T(8,128)S(1)} %global_sums.1.own_sums_ref), channel_id=1, source_target_pairs={{2,0},{3,1},{4,6},{5,7},{10,8},{11,9},{12,14},{13,15},{18,16},{19,... | collective-permute-start | bytes 12296 | tf_op jit(solution)/shard_map/ppermute | solution.py:425
  54.5 1.2 %collective-permute-start.13 = (f32[2,3,128]{2,1,0:T(4,128)S(1)}, f32[2,3,128]{2,1,0:T(4,128)S(1)}, u32[]{:S(2)}, u32[]{:S(2)}) collective-permute-start(f32[2,3,128]{2,1,0:T(4,128)S(1)} %get-tuple-element.44), channel_id=1, source_target_pairs={{0,1},{1,0},{2,3},{3,2},{4,5},{5,4},{6,7},{7,6},{8,9},{9,8},{10,11... | collective-permute-start | bytes 9224 | tf_op jit(solution)/shard_map/ppermute | solution.py:418

commit v3 on v2

--- a/solution.py
+++ b/solution.py
@@ -73,54 +73,53 @@
     return jnp.transpose(jnp.broadcast_to(wide, (LANES, LANES)))[: row.shape[1]]
 
 
-def pick(x_ref, hit, out_ref, at, cols):
-    contract = (((0,), (0,)), ((), ()))
-    picked = lax.dot_general(hit, x_ref[:, cols], contract, preferred_element_type=jnp.float32)
-    out_ref[at : at + hit.shape[1], :] = picked.astype(jnp.bfloat16)
-
-
 def own_positions(pos_ref, rows):
     core, chip = device_place()
     row = (chip * CORES + core) * rows + lax.broadcasted_iota(jnp.int32, (rows, pos_ref.shape[1]), 0)
     return jnp.where(row == pos_ref[...], 1.0, 0.0).astype(jnp.bfloat16)
 
 
-def select_q_kernel(half, pos_hbm, q_hbm, own_ref, sib_ref, pos_ref, q_ref, sems):
-    core, _ = device_place()
-    copies = [pltpu.make_async_copy(pos_hbm, pos_ref, sems.at[2])]
-    for slot, which in ((0, 1 - core), (1, core)):
-        cols = pl.ds(pl.multiple_of(which * half, half), half)
-        copies.append(pltpu.make_async_copy(q_hbm.at[:, cols], q_ref.at[slot], sems.at[slot]))
-    for copy in copies:
-        copy.start()
-    copies[0].wait()
-    hit = own_positions(pos_ref, q_ref.shape[1])
-    for slot, out_ref in ((0, sib_ref), (1, own_ref)):
-        copies[1 + slot].wait()
-        pick(q_ref.at[slot], hit, out_ref, 0, slice(None))
-
-
-def select_kv_kernel(half, pos_ref, k_ref, v_ref, q_ref, own_ref, edge_ref, sib_ref, bulk_ref):
-    rows = k_ref.shape[0]
-    glob = pos_ref.shape[1]
-    hit = own_positions(pos_ref, rows)
+def select_kernel(half, pos_hbm, q_hbm, k_hbm, v_hbm, sel_ref, sib_ref, edge_ref, mine_ref, bulk_ref, pos_ref, sems):
+    rows = q_hbm.shape[0]
     core, _ = device_place()
     block = pl.ds(pl.multiple_of(core * (rows - BLK), BLK), BLK)
-    mine = pl.ds(pl.multiple_of(core * half, half), half)
-    theirs = pl.ds(pl.multiple_of((1 - core) * half, half), half)
-    for i, x_ref in enumerate((k_ref, v_ref)):
-        pick(x_ref, hit, sib_ref, i * glob, theirs)
-        sib_ref[2 * glob + i * BLK : 2 * glob + (i + 1) * BLK, :] = x_ref[block, theirs]
-        bulk_ref[i * rows : (i + 1) * rows, :] = x_ref[:, theirs]
-        pick(x_ref, hit, own_ref, i * glob, mine)
-        edge_ref[i * BLK : (i + 1) * BLK, :] = x_ref[block, mine]
-    bulk_ref[2 * rows :, :] = q_ref[:, theirs]
-
-
-def split_kernel(a_ref, b_ref, sum_ref, rest_ref):
-    count = sum_ref.shape[0]
-    sum_ref[...] = a_ref[...] + b_ref[:count, :]
-    rest_ref[...] = b_ref[count:, :]
+    pos_copy = pltpu.make_async_copy(pos_hbm, pos_ref, sems.at[0])
+    copies = []
+    for i, x_hbm in enumerate((q_hbm, k_hbm, v_hbm)):
+        for to_ref, which in ((bulk_ref, 1 - core), (mine_ref, core)):
+            cols = pl.ds(pl.multiple_of(which * half, half), half)
+            to = to_ref.at[i * rows : (i + 1) * rows, :]
+            copies.append(pltpu.make_async_copy(x_hbm.at[:, cols], to, sems.at[1 + len(copies)]))
+    edges = [
+        pltpu.make_async_copy(x_hbm.at[block, :], edge_ref.at[i * BLK : (i + 1) * BLK, :], sems.at[7 + i])
+        for i, x_hbm in enumerate((k_hbm, v_hbm))
+    ]
+    for copy in (pos_copy, *copies, *edges):
+        copy.start()
+    pos_copy.wait()
+    hit = own_positions(pos_ref, rows)
+    glob = hit.shape[1]
+    contract = (((0,), (0,)), ((), ()))
+    for i in range(3):
+        for copy, x_ref, out_ref in ((copies[2 * i], bulk_ref, sib_ref), (copies[2 * i + 1], mine_ref, sel_ref)):
+            copy.wait()
+            x = x_ref[i * rows : (i + 1) * rows, :]
+            picked = lax.dot_general(hit, x, contract, preferred_element_type=jnp.float32)
+            out_ref[i * glob : (i + 1) * glob, :] = picked.astype(jnp.bfloat16)
+    for copy in edges:
+        copy.wait()
+
+
+def join_kernel(own_ref, recv_ref, q_ref, kv_ref):
+    count = q_ref.shape[0]
+    q_ref[...] = own_ref[:count, :] + recv_ref[:count, :]
+    kv_ref[...] = own_ref[count:, :] + recv_ref[count:, :]
+
+
+def edge_kernel(full_ref, out_ref):
+    half = out_ref.shape[1]
+    core, _ = device_place()
+    out_ref[...] = full_ref[:, pl.ds(pl.multiple_of((1 - core) * half, half), half)]
 
 
 def add_kernel(a_ref, b_ref, out_ref):
@@ -135,26 +134,24 @@
     return (chip == 1) | (chip == 2)
 
 
-def prepare_kernel(q_own_ref, k_own_ref, v_own_ref, sib_ref, k_ref, v_t_ref, q_t_ref, v_all):
-    rows = k_own_ref.shape[0]
+def prepare_kernel(own_ref, sib_ref, k_ref, v_t_ref, q_t_ref, v_all):
+    rows = own_ref.shape[0] // 3
     half = k_ref.shape[1]
     core, _ = device_place()
-    cols = pl.ds(pl.multiple_of(core * half, half), half)
-    own = pl.multiple_of(core * rows, BLK)
-    sib = pl.multiple_of((1 - core) * rows, BLK)
     zero = jnp.zeros((BLK, half), jnp.bfloat16)
-    for i, (ref, own_ref) in enumerate(((k_ref, k_own_ref), (v_all, v_own_ref))):
+    for ref in (k_ref, v_all):
         ref[:BLK, :] = zero
         ref[BLK + CORES * rows :, :] = zero
-        ref[pl.ds(pl.multiple_of(own + BLK, BLK), rows), :] = own_ref[:, cols]
-        ref[pl.ds(pl.multiple_of(sib + BLK, BLK), rows), :] = sib_ref[i * rows : (i + 1) * rows, :]
+    for part_ref, which in ((own_ref, core), (sib_ref, 1 - core)):
+        at = pl.ds(pl.multiple_of(which * rows + BLK, BLK), rows)
+        k_ref[at, :] = part_ref[rows : 2 * rows, :]
+        v_all[at, :] = part_ref[2 * rows :, :]
 
     def turn(head, carry):
         lanes = pl.ds(pl.multiple_of(head * LANES, LANES), LANES)
         v_t_ref[lanes, :] = jnp.transpose(v_all[:, lanes])
-        source = pl.ds(pl.multiple_of(core * half + head * LANES, LANES), LANES)
-        q_t_ref[lanes, pl.ds(pl.multiple_of(own, LANES), rows)] = jnp.transpose(q_own_ref[:, source])
-        q_t_ref[lanes, pl.ds(pl.multiple_of(sib, LANES), rows)] = jnp.transpose(sib_ref[2 * rows :, lanes])
+        for part_ref, which in ((own_ref, core), (sib_ref, 1 - core)):
+            q_t_ref[lanes, pl.ds(pl.multiple_of(which * rows, LANES), rows)] = jnp.transpose(part_ref[:rows, lanes])
         return carry
 
     lax.fori_loop(0, half // LANES, turn, 0)
@@ -274,15 +271,17 @@
     first_bias = jnp.where(left & (chip == 0), NEG, 0.0)
     last_bias = jnp.where((~left) & (chip == chips - 1), NEG, 0.0)
 
+    mine = pl.ds(pl.multiple_of(core * half, half), half)
+
     @pl.when(core == 1)
     def _():
-        edges[0] = edge_a_ref[...]
+        edges[0] = edge_a_ref[:, mine]
         edges[1] = edge_b_ref[...]
 
     @pl.when(core == 0)
     def _():
         edges[0] = edge_b_ref[...]
-        edges[1] = edge_a_ref[...]
+        edges[1] = edge_a_ref[:, mine]
 
     def one_head(head, carry):
         cols = pl.ds(pl.multiple_of(head * LANES, LANES), LANES)
@@ -417,8 +416,8 @@
     def swap(x, mask):
         return lax.ppermute(x, "seq", [(i, i ^ mask) for i in range(seq_count)])
 
-    def shift(x, even, odd):
-        moves = [(i, i + (odd if i % CORES else even) * CORES) for i in range(seq_count)]
+    def move_cores(x):
+        moves = [(i, i + (CORES if i % CORES else -CORES)) for i in range(seq_count)]
         return lax.ppermute(x, "seq", [(i, to) for i, to in moves if 0 <= to < seq_count])
 
     def move(x, pairs):
@@ -434,34 +433,35 @@
     row_positions = global_positions.reshape(1, glob)
     small = ((glob, half), bf16)
     pair_of = ((2 * glob, half), bf16)
+    three = ((3 * glob, half), bf16)
+    bulk = ((3 * rows, half), bf16)
     edge = ((2 * BLK, half), bf16)
-    q_own, q_sib = call(
-        functools.partial(select_q_kernel, half),
-        "select_queries",
-        [small, small],
-        [row_positions, queries],
-        [((1, glob), jnp.int32), ((CORES, rows, half), bf16), pltpu.SemaphoreType.DMA((3,))],
+    own, sib, edge_own, mine, bulk_sib = call(
+        functools.partial(select_kernel, half),
+        "select_rows",
+        [three, three, ((2 * BLK, model_width), bf16), bulk, bulk],
+        [row_positions, queries, keys, values],
+        [((1, glob), jnp.int32), pltpu.SemaphoreType.DMA((9,))],
         from_hbm=True,
     )
-    q_near = call(add_kernel, "add_queries", small, [q_own, swap(q_sib, 1)])
-    later_positions = after((row_positions,), q_near)[0]
-    kv_own, edge_own, kv_sib, bulk_sib = call(
-        functools.partial(select_kv_kernel, half),
-        "select_keys_values",
-        [pair_of, edge, ((2 * glob + 2 * BLK, half), bf16), ((3 * rows, half), bf16)],
-        [later_positions, keys, values, queries],
-    )
-    kv_near, edge_recv = call(split_kernel, "join_keys_values", [pair_of, edge], [kv_own, swap(kv_sib, 1)])
-    bulk_sib = after((bulk_sib,), kv_near)[0]
+    q_near, kv_near = call(join_kernel, "join_cores", [small, pair_of], [own, swap(sib, 1)])
+    edge_a = move_cores(edge_own)
+    bulk_sib = after((bulk_sib,), q_near)[0]
     bulk_recv = swap(bulk_sib, 1)
     for r in range(1, rounds):
         q_near = call(add_kernel, "add_queries", small, [q_near, swap(q_near, 1 << r)])
-    kv_near = after((kv_near,), q_near)[0]
+    edge_a = after((edge_a,), q_near)[0]
     q_far = swap(q_near, 1 << rounds)
-
-    edge_own, edge_recv = after((edge_own, edge_recv), q_near)
-    edge_a = shift(edge_own, -1, 1)
-    edge_b = shift(edge_recv, 1, -1)
+    edge_b = swap(call(edge_kernel, "split_edges", edge, [edge_a]), 1)
+    k_all, v_t, q_t = call(
+        prepare_kernel,
+        "prepare",
+        [((tokens + 2 * BLK, half), bf16), ((half, tokens + 2 * BLK), bf16), ((half, tokens), bf16)],
+        [mine, bulk_recv],
+        [((tokens + 2 * BLK, half), bf16)],
+        micros=1.6,
+    )
+    kv_near = after((kv_near,), k_all)[0]
     if chips == 4:
         kv_near = call(add_kernel, "add_keys_values", pair_of, [kv_near, move(kv_near, inward)])
         kv_near = call(add_kernel, "add_keys_values", pair_of, [kv_near, move(kv_near, across)])
@@ -471,14 +471,6 @@
             kv_near = call(add_kernel, "add_keys_values", pair_of, [kv_near, swap(kv_near, 1 << r)])
         kv_far = swap(kv_near, 1 << rounds)
 
-    k_all, v_t, q_t = call(
-        prepare_kernel,
-        "prepare",
-        [((tokens + 2 * BLK, half), bf16), ((half, tokens + 2 * BLK), bf16), ((half, tokens), bf16)],
-        [queries, keys, values, bulk_recv],
-        [((tokens + 2 * BLK, half), bf16)],
-        micros=1.6,
-    )
     part = ((half_heads // 2, head_size + STAT_ROWS, LANES), bf16)
     message = call(
         functools.partial(global_kernel, scale2),

time: 56.6 us -> 57.5 us (1.016)
  waiting for transfers between devices: 12.9 us -> 25.6 us
  starting transfers between devices: 25.5 us -> 16.5 us
  local copies, waits for them, and re-layouts: 2.83 us -> 0.01 us
    ppermute x6, waiting for transfers between devices: 7.85 us -> 19.6 us  [swap(): return lax.ppermute(x, 'seq', [(i, i ^ mask) for i in range(seq_count)])]
    ppermute x2 -> x1, starting transfers between devices: 6.48 us -> 1.28 us  [move_cores(): lax.ppermute(x, 'seq', [(i, to) for i, to in moves if 0 <= to < seq_count])]
    ppermute x6, starting transfers between devices: 14.4 us -> 10.1 us  [move(): lax.ppermute(x, 'seq', [(a * CORES + c, b * CORES + c) for a, b in pairs...]
    unnamed x14 -> x4, local copies, waits for them, and re-layouts: 2.83 us -> 0.01 us
    ppermute x6, waiting for transfers between devices: 5.03 us -> 5.92 us  [move(): lax.ppermute(x, 'seq', [(a * CORES + c, b * CORES + c) for a, b in pairs...]
    pallas_call x14 -> x13, Pallas kernels: 14.2 us -> 14.5 us  [call(): pl.pallas_call(kernel, in_specs=[pl.BlockSpec(memory_space=source)] * len...]
  transfers between devices with their start and end apart: 14 -> 13, of which waited for: 8 -> 7; matrix products, arithmetic and copies ran while one was open for 0% -> 0% of each run, Pallas kernels for 20% -> 20%
where the time goes in v3:
time: 57.5 us; the launch traced here: 57.3 us
  waiting for transfers between devices  25.6 us (45%)
  starting transfers between devices  16.5 us (29%)
  Pallas kernels  14.5 us (25%)
  other arithmetic  0.59 us (1%)
    ppermute x6, waiting for transfers between devices, swap(): return lax.ppermute(x, 'seq', [(i, i ^ mask) for i in range(seq_count)])  19.6 us
    pallas_call x13, Pallas kernels, call(): pl.pallas_call(kernel, in_specs=[pl.BlockSpec(memory_space=source)] * len...  14.5 us
    ppermute x6, starting transfers between devices, move(): lax.ppermute(x, 'seq', [(a * CORES + c, b * CORES + c) for a, b in pairs...  10.1 us
    ppermute x6, waiting for transfers between devices, move(): lax.ppermute(x, 'seq', [(a * CORES + c, b * CORES + c) for a, b in pairs...  5.92 us
    ppermute x6, starting transfers between devices, swap(): return lax.ppermute(x, 'seq', [(i, i ^ mask) for i in range(seq_count)])  5.12 us
    ppermute x1, starting transfers between devices, move_cores(): lax.ppermute(x, 'seq', [(i, to) for i, to in moves if 0 <= to < seq_count])  1.28 us
  transfers between devices with their start and end apart: 13, of which 7 were waited for; matrix products, arithmetic and copies ran while one was open for 0% of the time, Pallas kernels for 20%

profile of v3, /device:TPU:0, one launch (start us, length us, event | category | flops | bytes accessed | tf_op | source)
XLA Modules:
  0.0 57.3 jit_solution(18252335359805309198)
XLA Ops:
  0.0 2.8 %select_rows.1 = (bf16[192,1024]{1,0:T(8,128)(2,1)S(1)}, bf16[192,1024]{1,0:T(8,128)(2,1)S(1)}, bf16[128,2048]{1,0:T(8,128)(2,1)S(1)}, bf16[1152,1024]{1,0:T(8,128)(2,1)S(1)}, bf16[1152,1024]{1,0:T(8,128)(2,1)S(1)}) custom-call(s32[1,64]{1,0:T(1,128)} %bitcast.6, bf16[384,2048]{1,0:T(8,128)(2,1)} %q_hbm.1, bf16[384,2048]{1,0:T(8,128)(2,1)} %k_hbm.1, ...), custom_call_target="tpu_custom_call" | custom-call | flops 1 | bytes 1 | tf_op jit(solution)/shard_map/select_rows/pallas_call | solution.py:388
  2.8 0.5 collective-permute-start
  3.4 1.3 %collective-permute-done.recv_ref = bf16[192,1024]{1,0:T(8,128)(2,1)S(1)} collective-permute-done((bf16[192,1024]{1,0:T(8,128)(2,1)S(1)}, bf16[192,1024]{1,0:T(8,128)(2,1)S(1)}, u32[]{:S(2)}, u32[]{:S(2)}) %collective-permute-start) | collective-permute-done | bytes 393248 | tf_op jit(solution)/shard_map/ppermute | solution.py:417
  4.8 0.4 collective-permute-start.3
  5.2 1.3 %collective-permute-start.7 = (bf16[128,2048]{1,0:T(8,128)(2,1)S(1)}, bf16[128,2048]{1,0:T(8,128)(2,1)S(1)}, u32[]{:S(2)}, u32[]{:S(2)}) collective-permute-start(bf16[128,2048]{1,0:T(8,128)(2,1)S(1)} %get-tuple-element.31), channel_id=1, source_target_pairs={{1,3},{2,0},{3,5},{4,2},{5,7},{6,4},{9,11},{10,8},{11,13},{12,10},... | collective-permute-start | bytes 1572872 | tf_op jit(solution)/shard_map/ppermute | solution.py:421
  6.5 2.9 %collective-permute-done.3.sib_ref = bf16[1152,1024]{1,0:T(8,128)(2,1)S(1)} collective-permute-done((bf16[1152,1024]{1,0:T(8,128)(2,1)S(1)}, bf16[1152,1024]{1,0:T(8,128)(2,1)S(1)}, u32[]{:S(2)}, u32[]{:S(2)}) %collective-permute-start.3) | collective-permute-done | bytes 2359328 | tf_op jit(solution)/shard_map/ppermute | solution.py:417
  9.4 1.6 %prepare.1 = (bf16[896,1024]{1,0:T(8,128)(2,1)S(1)}, bf16[1024,896]{1,0:T(8,128)(2,1)S(1)}, bf16[1024,768]{1,0:T(8,128)(2,1)S(1)}) custom-call(bf16[1152,1024]{1,0:T(8,128)(2,1)S(1)} %get-tuple-element.25.own_ref, bf16[1152,1024]{1,0:T(8,128)(2,1)S(1)} %collective-permute-done.3.sib_ref), custom_call_target="tpu_custom_call" | custom-call | flops 1600000000 | bytes 1 | tf_op jit(solution)/shard_map/prepare/pallas_call | solution.py:388
  11.0 4.9 %collective-permute-start.9 = (bf16[128,1024]{1,0:T(8,128)(2,1)S(1)}, bf16[128,1024]{1,0:T(8,128)(2,1)S(1)}, u32[]{:S(2)}, u32[]{:S(2)}) collective-permute-start(bf16[128,1024]{1,0:T(8,128)(2,1)S(1)} %get-tuple-element.36.a_ref), channel_id=1, source_target_pairs={{0,2},{1,3},{6,4},{7,5},{8,10},{9,11},{14,12},{15,13},{16,18},{17,... | collective-permute-start | bytes 786440 | tf_op jit(solution)/shard_map/ppermute | solution.py:424
  15.9 0.1 collective-permute-start.1
  16.0 8.6 %collective-permute-done.1.b_ref = bf16[64,1024]{1,0:T(8,128)(2,1)S(1)} collective-permute-done((bf16[64,1024]{1,0:T(8,128)(2,1)S(1)}, bf16[64,1024]{1,0:T(8,128)(2,1)S(1)}, u32[]{:S(2)}, u32[]{:S(2)}) %collective-permute-start.1) | collective-permute-done | bytes 131104 | tf_op jit(solution)/shard_map/ppermute | solution.py:417
  24.5 3.9 %collective-permute-start.2 = (bf16[64,1024]{1,0:T(8,128)(2,1)S(1)}, bf16[64,1024]{1,0:T(8,128)(2,1)S(1)}, u32[]{:S(2)}, u32[]{:S(2)}) collective-permute-start(bf16[64,1024]{1,0:T(8,128)(2,1)S(1)} %add_queries.1.q_a_ref), channel_id=1, source_target_pairs={{0,4},{1,5},{2,6},{3,7},{4,0},{5,1},{6,2},{7,3},{8,12},{9,13},{10,... | collective-permute-start | bytes 393224 | tf_op jit(solution)/shard_map/ppermute | solution.py:417
  28.5 0.0 collective-permute-done.7.full_ref.edge_a_ref
  28.5 0.0 collective-permute-done.9.b_ref
  28.5 0.7 %collective-permute-start.10 = (bf16[128,1024]{1,0:T(8,128)(2,1)S(1)}, bf16[128,1024]{1,0:T(8,128)(2,1)S(1)}, u32[]{:S(2)}, u32[]{:S(2)}) collective-permute-start(bf16[128,1024]{1,0:T(8,128)(2,1)S(1)} %add_keys_values.2.a_ref), channel_id=1, source_target_pairs={{2,4},{3,5},{4,2},{5,3},{10,12},{11,13},{12,10},{13,11},{18,20},{1... | collective-permute-start | bytes 786440 | tf_op jit(solution)/shard_map/ppermute | solution.py:424
  29.3 0.1 collective-permute-start.8
  29.3 5.7 %collective-permute-done.2.q_b_ref = bf16[64,1024]{1,0:T(8,128)(2,1)S(1)} collective-permute-done((bf16[64,1024]{1,0:T(8,128)(2,1)S(1)}, bf16[64,1024]{1,0:T(8,128)(2,1)S(1)}, u32[]{:S(2)}, u32[]{:S(2)}) %collective-permute-start.2) | collective-permute-done | bytes 131104 | tf_op jit(solution)/shard_map/ppermute | solution.py:417
  35.0 1.4 %global_partial.1.a_ref = bf16[4,144,128]{2,1,0:T(8,128)(2,1)S(1)} custom-call(bf16[64,1024]{1,0:T(8,128)(2,1)S(1)} %add_queries.1.q_a_ref, bf16[64,1024]{1,0:T(8,128)(2,1)S(1)} %collective-permute-done.2.q_b_ref, bf16[896,1024]{1,0:T(8,128)(2,1)S(1)} %get-tuple-element.28.k_ref, bf16[1024,896]{1,0:T(8,128)(2,1)S(1)} %get-tuple-element.29.v_t_ref), custom_call_target="tpu_custom_call" | custom-call | flops 1 | bytes 1 | tf_op jit(solution)/shard_map/global_partial/pallas_call | solution.py:388
  36.4 1.3 %collective-permute-start.4 = (bf16[4,144,128]{2,1,0:T(8,128)(2,1)S(1)}, bf16[4,144,128]{2,1,0:T(8,128)(2,1)S(1)}, u32[]{:S(2)}, u32[]{:S(2)}) collective-permute-start(bf16[4,144,128]{2,1,0:T(8,128)(2,1)S(1)} %global_partial.1.a_ref), channel_id=1, source_target_pairs={{0,2},{1,3},{6,4},{7,5},{8,10},{9,11},{14,12},{15,13},{16,18},{17,... | collective-permute-start | bytes 442376 | tf_op jit(solution)/shard_map/ppermute | solution.py:424
  37.7 2.9 %collective-permute-done.4.b_ref = bf16[4,144,128]{2,1,0:T(8,128)(2,1)S(1)} collective-permute-done((bf16[4,144,128]{2,1,0:T(8,128)(2,1)S(1)}, bf16[4,144,128]{2,1,0:T(8,128)(2,1)S(1)}, u32[]{:S(2)}, u32[]{:S(2)}) %collective-permute-start.4) | collective-permute-done | bytes 147488 | tf_op jit(solution)/shard_map/ppermute | solution.py:424
  40.6 0.7 %collective-permute-start.5 = (bf16[4,144,128]{2,1,0:T(8,128)(2,1)S(1)}, bf16[4,144,128]{2,1,0:T(8,128)(2,1)S(1)}, u32[]{:S(2)}, u32[]{:S(2)}) collective-permute-start(bf16[4,144,128]{2,1,0:T(8,128)(2,1)S(1)} %merge_partial.1.a_ref), channel_id=1, source_target_pairs={{2,4},{3,5},{4,2},{5,3},{10,12},{11,13},{12,10},{13,11},{18,20},{1... | collective-permute-start | bytes 442376 | tf_op jit(solution)/shard_map/ppermute | solution.py:424
  41.3 0.0 collective-permute-done.10.b_ref
  41.3 1.3 %collective-permute-start.11 = (bf16[128,1024]{1,0:T(8,128)(2,1)S(1)}, bf16[128,1024]{1,0:T(8,128)(2,1)S(1)}, u32[]{:S(2)}, u32[]{:S(2)}) collective-permute-start(bf16[128,1024]{1,0:T(8,128)(2,1)S(1)} %add_keys_values.3.kv_a_ref), channel_id=1, source_target_pairs={{2,0},{3,1},{4,6},{5,7},{10,8},{11,9},{12,14},{13,15},{18,16},{19,... | collective-permute-start | bytes 786440 | tf_op jit(solution)/shard_map/ppermute | solution.py:424
  42.6 0.0 collective-permute-done.8.edge_b_ref
  42.6 0.0 copy-start
  42.6 0.0 copy-start.1
  42.6 4.3 %near_attention.1 = (f32[8,6,128,128]{3,2,1,0:T(8,128)S(1)}, f32[8,2,6,128]{3,2,1,0:T(8,128)S(1)}) custom-call(bf16[1024,768]{1,0:T(8,128)(2,1)S(1)} %get-tuple-element.30.q_t_ref, bf16[896,1024]{1,0:T(8,128)(2,1)S(1)} %get-tuple-element.28.k_ref, bf16[1024,896]{1,0:T(8,128)(2,1)S(1)} %get-tuple-element.29.v_t_ref, ...), custom_call_target="tpu_custom_call" | custom-call | flops 4000000000 | bytes 1 | tf_op jit(solution)/shard_map/near_attention/pallas_call | solution.py:388
  47.0 0.0 collective-permute-done.5.b_ref
  47.0 0.0 copy-done
  47.0 0.2 global_sums.1.own_sums_ref
  47.2 1.3 %collective-permute-start.6 = (f32[8,128]{1,0:T(8,128)S(1)}, f32[8,128]{1,0:T(8,128)S(1)}, u32[]{:S(2)}, u32[]{:S(2)}) collective-permute-start(f32[8,128]{1,0:T(8,128)S(1)} %global_sums.1.own_sums_ref), channel_id=1, source_target_pairs={{2,0},{3,1},{4,6},{5,7},{10,8},{11,9},{12,14},{13,15},{18,16},{19,... | collective-permute-start | bytes 12296 | tf_op jit(solution)/shard_map/ppermute | solution.py:424
  48.5 3.0 %collective-permute-done.11.kv_b_ref = bf16[128,1024]{1,0:T(8,128)(2,1)S(1)} collective-permute-done((bf16[128,1024]{1,0:T(8,128)(2,1)S(1)}, bf16[128,1024]{1,0:T(8,128)(2,1)S(1)}, u32[]{:S(2)}, u32[]{:S(2)}) %collective-permute-start.11) | collective-permute-done | bytes 262176 | tf_op jit(solution)/shard_map/ppermute | solution.py:424
  51.6 0.0 copy-done.1
  51.6 3.6 %far_attention.1.win_ref = f32[2,6,128]{2,1,0:T(8,128)S(1)} custom-call(bf16[1024,768]{1,0:T(8,128)(2,1)S(1)} %get-tuple-element.30.q_t_ref, f32[8,6,128,128]{3,2,1,0:T(8,128)S(1)} %get-tuple-element.33.acc_ref, f32[8,2,6,128]{3,2,1,0:T(8,128)S(1)} %get-tuple-element.34.stat_ref, bf16[128,1024]{1,0:T(8,128)(2,1)S(1)} %add_keys_values.3.kv_a_ref, ...), custom_call_target="tpu_custom_call" | custom-call | flops 2000000000 | bytes 1 | tf_op jit(solution)/shard_map/far_attention/pallas_call | solution.py:388
  55.2 0.0 collective-permute-done.6.far_sums_ref
  55.2 0.3 place_global.1
  55.5 0.1 collective-permute-start.12
  55.6 1.2 %collective-permute-done.12 = f32[2,3,128]{2,1,0:T(4,128)S(1)} collective-permute-done((f32[2,3,128]{2,1,0:T(4,128)S(1)}, f32[2,3,128]{2,1,0:T(4,128)S(1)}, u32[]{:S(2)}, u32[]{:S(2)}) %collective-permute-start.12) | collective-permute-done | bytes 3104 | tf_op jit(solution)/shard_map/ppermute | solution.py:417
  56.7 0.6 %fusion.4 = f32[384]{0:T(512)} fusion(f32[2,3,128]{2,1,0:T(4,128)S(1)} %collective-permute-done.12, f32[2,3,128]{2,1,0:T(4,128)S(1)} %get-tuple-element.37), kind=kLoop, calls=%fused_computation.5 | loop fusion | flops 1920 | bytes 7680 | tf_op jit(solution)/shard_map/mul | solution.py:527
  (6 shorter events, 0.2 us)
Async XLA Ops:
  2.8 1.9 %collective-permute-start = (bf16[192,1024]{1,0:T(8,128)(2,1)S(1)}, bf16[192,1024]{1,0:T(8,128)(2,1)S(1)}, u32[]{:S(2)}, u32[]{:S(2)}) collective-permute-start(bf16[192,1024]{1,0:T(8,128)(2,1)S(1)} %get-tuple-element.23), channel_id=1, source_target_pairs={{0,1},{1,0},{2,3},{3,2},{4,5},{5,4},{6,7},{7,6},{8,9},{9,8},{10,11... | collective-permute-start | bytes 1179656 | tf_op jit(solution)/shard_map/ppermute | solution.py:417
  4.8 4.6 %collective-permute-start.3 = (bf16[1152,1024]{1,0:T(8,128)(2,1)S(1)}, bf16[1152,1024]{1,0:T(8,128)(2,1)S(1)}, u32[]{:S(2)}, u32[]{:S(2)}) collective-permute-start(bf16[1152,1024]{1,0:T(8,128)(2,1)S(1)} %get-tuple-element.27), channel_id=1, source_target_pairs={{0,1},{1,0},{2,3},{3,2},{4,5},{5,4},{6,7},{7,6},{8,9},{9,8},{10,11... | collective-permute-start | bytes 7077896 | tf_op jit(solution)/shard_map/ppermute | solution.py:417
  5.2 23.3 %collective-permute-start.7 = (bf16[128,2048]{1,0:T(8,128)(2,1)S(1)}, bf16[128,2048]{1,0:T(8,128)(2,1)S(1)}, u32[]{:S(2)}, u32[]{:S(2)}) collective-permute-start(bf16[128,2048]{1,0:T(8,128)(2,1)S(1)} %get-tuple-element.31), channel_id=1, source_target_pairs={{1,3},{2,0},{3,5},{4,2},{5,7},{6,4},{9,11},{10,8},{11,13},{12,10},... | collective-permute-start | bytes 1572872 | tf_op jit(solution)/shard_map/ppermute | solution.py:421
  11.0 17.5 %collective-permute-start.9 = (bf16[128,1024]{1,0:T(8,128)(2,1)S(1)}, bf16[128,1024]{1,0:T(8,128)(2,1)S(1)}, u32[]{:S(2)}, u32[]{:S(2)}) collective-permute-start(bf16[128,1024]{1,0:T(8,128)(2,1)S(1)} %get-tuple-element.36.a_ref), channel_id=1, source_target_pairs={{0,2},{1,3},{6,4},{7,5},{8,10},{9,11},{14,12},{15,13},{16,18},{17,... | collective-permute-start | bytes 786440 | tf_op jit(solution)/shard_map/ppermute | solution.py:424
  15.9 8.6 %collective-permute-start.1 = (bf16[64,1024]{1,0:T(8,128)(2,1)S(1)}, bf16[64,1024]{1,0:T(8,128)(2,1)S(1)}, u32[]{:S(2)}, u32[]{:S(2)}) collective-permute-start(bf16[64,1024]{1,0:T(8,128)(2,1)S(1)} %get-tuple-element.24.a_ref), channel_id=1, source_target_pairs={{0,2},{1,3},{2,0},{3,1},{4,6},{5,7},{6,4},{7,5},{8,10},{9,11},{10,... | collective-permute-start | bytes 393224 | tf_op jit(solution)/shard_map/ppermute | solution.py:417
  24.5 10.5 %collective-permute-start.2 = (bf16[64,1024]{1,0:T(8,128)(2,1)S(1)}, bf16[64,1024]{1,0:T(8,128)(2,1)S(1)}, u32[]{:S(2)}, u32[]{:S(2)}) collective-permute-start(bf16[64,1024]{1,0:T(8,128)(2,1)S(1)} %add_queries.1.q_a_ref), channel_id=1, source_target_pairs={{0,4},{1,5},{2,6},{3,7},{4,0},{5,1},{6,2},{7,3},{8,12},{9,13},{10,... | collective-permute-start | bytes 393224 | tf_op jit(solution)/shard_map/ppermute | solution.py:417
  28.5 12.7 %collective-permute-start.10 = (bf16[128,1024]{1,0:T(8,128)(2,1)S(1)}, bf16[128,1024]{1,0:T(8,128)(2,1)S(1)}, u32[]{:S(2)}, u32[]{:S(2)}) collective-permute-start(bf16[128,1024]{1,0:T(8,128)(2,1)S(1)} %add_keys_values.2.a_ref), channel_id=1, source_target_pairs={{2,4},{3,5},{4,2},{5,3},{10,12},{11,13},{12,10},{13,11},{18,20},{1... | collective-permute-start | bytes 786440 | tf_op jit(solution)/shard_map/ppermute | solution.py:424
  29.3 13.4 %collective-permute-start.8 = (bf16[128,1024]{1,0:T(8,128)(2,1)S(1)}, bf16[128,1024]{1,0:T(8,128)(2,1)S(1)}, u32[]{:S(2)}, u32[]{:S(2)}) collective-permute-start(bf16[128,1024]{1,0:T(8,128)(2,1)S(1)} %split_edges.1), channel_id=1, source_target_pairs={{0,1},{1,0},{2,3},{3,2},{4,5},{5,4},{6,7},{7,6},{8,9},{9,8},{10,11... | collective-permute-start | bytes 786440 | tf_op jit(solution)/shard_map/ppermute | solution.py:417
  36.4 4.2 %collective-permute-start.4 = (bf16[4,144,128]{2,1,0:T(8,128)(2,1)S(1)}, bf16[4,144,128]{2,1,0:T(8,128)(2,1)S(1)}, u32[]{:S(2)}, u32[]{:S(2)}) collective-permute-start(bf16[4,144,128]{2,1,0:T(8,128)(2,1)S(1)} %global_partial.1.a_ref), channel_id=1, source_target_pairs={{0,2},{1,3},{6,4},{7,5},{8,10},{9,11},{14,12},{15,13},{16,18},{17,... | collective-permute-start | bytes 442376 | tf_op jit(solution)/shard_map/ppermute | solution.py:424
  40.6 6.4 %collective-permute-start.5 = (bf16[4,144,128]{2,1,0:T(8,128)(2,1)S(1)}, bf16[4,144,128]{2,1,0:T(8,128)(2,1)S(1)}, u32[]{:S(2)}, u32[]{:S(2)}) collective-permute-start(bf16[4,144,128]{2,1,0:T(8,128)(2,1)S(1)} %merge_partial.1.a_ref), channel_id=1, source_target_pairs={{2,4},{3,5},{4,2},{5,3},{10,12},{11,13},{12,10},{13,11},{18,20},{1... | collective-permute-start | bytes 442376 | tf_op jit(solution)/shard_map/ppermute | solution.py:424
  41.3 10.3 %collective-permute-start.11 = (bf16[128,1024]{1,0:T(8,128)(2,1)S(1)}, bf16[128,1024]{1,0:T(8,128)(2,1)S(1)}, u32[]{:S(2)}, u32[]{:S(2)}) collective-permute-start(bf16[128,1024]{1,0:T(8,128)(2,1)S(1)} %add_keys_values.3.kv_a_ref), channel_id=1, source_target_pairs={{2,0},{3,1},{4,6},{5,7},{10,8},{11,9},{12,14},{13,15},{18,16},{19,... | collective-permute-start | bytes 786440 | tf_op jit(solution)/shard_map/ppermute | solution.py:424
  42.6 4.4 %copy-start = (f32[2048]{0:T(1024)S(1)}, f32[2048]{0:T(1024)}, u32[]{:S(2)}) copy-start(f32[2048]{0:T(1024)} %param.9) | copy-start | bytes 24580
  42.6 9.0 %copy-start.1 = (s32[64]{0:T(128)S(1)}, s32[64]{0:T(128)}, u32[]{:S(2)}) copy-start(s32[64]{0:T(128)} %param.8) | copy-start | bytes 772
  47.2 7.9 %collective-permute-start.6 = (f32[8,128]{1,0:T(8,128)S(1)}, f32[8,128]{1,0:T(8,128)S(1)}, u32[]{:S(2)}, u32[]{:S(2)}) collective-permute-start(f32[8,128]{1,0:T(8,128)S(1)} %global_sums.1.own_sums_ref), channel_id=1, source_target_pairs={{2,0},{3,1},{4,6},{5,7},{10,8},{11,9},{12,14},{13,15},{18,16},{19,... | collective-permute-start | bytes 12296 | tf_op jit(solution)/shard_map/ppermute | solution.py:424
  55.5 1.2 %collective-permute-start.12 = (f32[2,3,128]{2,1,0:T(4,128)S(1)}, f32[2,3,128]{2,1,0:T(4,128)S(1)}, u32[]{:S(2)}, u32[]{:S(2)}) collective-permute-start(f32[2,3,128]{2,1,0:T(4,128)S(1)} %get-tuple-element.38), channel_id=1, source_target_pairs={{0,1},{1,0},{2,3},{3,2},{4,5},{5,4},{6,7},{7,6},{8,9},{9,8},{10,11... | collective-permute-start | bytes 9224 | tf_op jit(solution)/shard_map/ppermute | solution.py:417

commit v4 on v3

--- a/solution.py
+++ b/solution.py
@@ -453,6 +453,7 @@
     edge_a = after((edge_a,), q_near)[0]
     q_far = swap(q_near, 1 << rounds)
     edge_b = swap(call(edge_kernel, "split_edges", edge, [edge_a]), 1)
+    bulk_recv = after((bulk_recv,), q_near)[0]
     k_all, v_t, q_t = call(
         prepare_kernel,
         "prepare",
@@ -460,6 +461,14 @@
         [mine, bulk_recv],
         [((tokens + 2 * BLK, half), bf16)],
         micros=1.6,
+    )
+    near_acc, near_stat = call(
+        functools.partial(near_kernel, scale2),
+        "near_attention",
+        [((half_heads, n_pairs, head_size, LANES), f32), ((half_heads, 2, n_pairs, LANES), f32)],
+        [q_t, k_all, v_t, edge_a, edge_b],
+        [((n_pairs, 4 * BLK, LANES), f32), ((n_pairs, 4 * BLK, LANES), bf16), ((2, 2 * BLK, half), bf16)],
+        micros=4.0,
     )
     kv_near = after((kv_near,), k_all)[0]
     if chips == 4:
@@ -478,11 +487,12 @@
         part,
         [q_near, q_far, k_all, v_t],
         [((half_heads // 2, tokens, LANES), f32), ((half_heads // 2, tokens + 2 * BLK, LANES), bf16)],
+        micros=20.0,
     )
     weights = score_weight.reshape(HEADS, head_size)
     if chips == 4:
         message = call(
-            functools.partial(inward_kernel, scale2), "merge_partial", part, [message, move(message, inward)]
+            functools.partial(inward_kernel, scale2), "merge_partial", part, [message, after((move(message, inward),), kv_near)[0]]
         )
         message_far = move(message, across)
     else:
@@ -496,14 +506,6 @@
     )
     sums_far = move(sums, outward) if chips == 4 else sums
 
-    near_acc, near_stat = call(
-        functools.partial(near_kernel, scale2),
-        "near_attention",
-        [((half_heads, n_pairs, head_size, LANES), f32), ((half_heads, 2, n_pairs, LANES), f32)],
-        [q_t, k_all, v_t, edge_a, edge_b],
-        [((n_pairs, 4 * BLK, LANES), f32), ((n_pairs, 4 * BLK, LANES), bf16), ((2, 2 * BLK, half), bf16)],
-        micros=4.0,
-    )
     window = call(
         functools.partial(far_kernel, scale2),
         "far_attention",

time: 57.5 us -> 51.7 us (0.90)
  waiting for transfers between devices: 25.6 us -> 15.6 us
  starting transfers between devices: 16.5 us -> 20.7 us
    ppermute x6, waiting for transfers between devices: 19.6 us -> 5.92 us  [swap(): return lax.ppermute(x, 'seq', [(i, i ^ mask) for i in range(seq_count)])]
    ppermute x6, starting transfers between devices: 10.1 us -> 15.5 us  [move(): lax.ppermute(x, 'seq', [(a * CORES + c, b * CORES + c) for a, b in pairs...]
    ppermute x6, waiting for transfers between devices: 5.92 us -> 8.63 us  [move(): lax.ppermute(x, 'seq', [(a * CORES + c, b * CORES + c) for a, b in pairs...]
    ppermute x6, starting transfers between devices: 5.12 us -> 3.89 us  [swap(): return lax.ppermute(x, 'seq', [(i, i ^ mask) for i in range(seq_count)])]
    ppermute x1, waiting for transfers between devices: 0.01 us -> 1.05 us  [move_cores(): lax.ppermute(x, 'seq', [(i, to) for i, to in moves if 0 <= to < seq_count])]
  transfers between devices with their start and end apart: 13 -> 13, of which waited for: 7 -> 8; matrix products, arithmetic and copies ran while one was open for 0% -> 0% of each run, Pallas kernels for 20% -> 22%
where the time goes in v4:
time: 51.7 us; the launch traced here: 51.5 us
  starting transfers between devices  20.7 us (40%)
  waiting for transfers between devices  15.6 us (30%)
  Pallas kernels  14.4 us (28%)
  other arithmetic  0.59 us (1%)
    ppermute x6, starting transfers between devices, move(): lax.ppermute(x, 'seq', [(a * CORES + c, b * CORES + c) for a, b in pairs...  15.5 us
    pallas_call x13, Pallas kernels, call(): pl.pallas_call(kernel, in_specs=[pl.BlockSpec(memory_space=source)] * len...  14.4 us
    ppermute x6, waiting for transfers between devices, move(): lax.ppermute(x, 'seq', [(a * CORES + c, b * CORES + c) for a, b in pairs...  8.63 us
    ppermute x6, waiting for transfers between devices, swap(): return lax.ppermute(x, 'seq', [(i, i ^ mask) for i in range(seq_count)])  5.92 us
    ppermute x6, starting transfers between devices, swap(): return lax.ppermute(x, 'seq', [(i, i ^ mask) for i in range(seq_count)])  3.89 us
    ppermute x1, starting transfers between devices, move_cores(): lax.ppermute(x, 'seq', [(i, to) for i, to in moves if 0 <= to < seq_count])  1.28 us
    ppermute x1, waiting for transfers between devices, move_cores(): lax.ppermute(x, 'seq', [(i, to) for i, to in moves if 0 <= to < seq_count])  1.05 us
  transfers between devices with their start and end apart: 13, of which 8 were waited for; matrix products, arithmetic and copies ran while one was open for 0% of the time, Pallas kernels for 22%

profile of v4, /device:TPU:0, one launch (start us, length us, event | category | flops | bytes accessed | tf_op | source)
XLA Modules:
  0.0 51.5 jit_solution(9433140612332555971)
XLA Ops:
  0.0 2.8 %select_rows.1 = (bf16[192,1024]{1,0:T(8,128)(2,1)S(1)}, bf16[192,1024]{1,0:T(8,128)(2,1)S(1)}, bf16[128,2048]{1,0:T(8,128)(2,1)S(1)}, bf16[1152,1024]{1,0:T(8,128)(2,1)S(1)}, bf16[1152,1024]{1,0:T(8,128)(2,1)S(1)}) custom-call(s32[1,64]{1,0:T(1,128)} %bitcast.6, bf16[384,2048]{1,0:T(8,128)(2,1)} %q_hbm.1, bf16[384,2048]{1,0:T(8,128)(2,1)} %k_hbm.1, ...), custom_call_target="tpu_custom_call" | custom-call | flops 1 | bytes 1 | tf_op jit(solution)/shard_map/select_rows/pallas_call | solution.py:388
  2.8 0.5 %collective-permute-start = (bf16[192,1024]{1,0:T(8,128)(2,1)S(1)}, bf16[192,1024]{1,0:T(8,128)(2,1)S(1)}, u32[]{:S(2)}, u32[]{:S(2)}) collective-permute-start(bf16[192,1024]{1,0:T(8,128)(2,1)S(1)} %get-tuple-element.25), channel_id=1, source_target_pairs={{0,1},{1,0},{2,3},{3,2},{4,5},{5,4},{6,7},{7,6},{8,9},{9,8},{10,11... | collective-permute-start | bytes 1179656 | tf_op jit(solution)/shard_map/ppermute | solution.py:417
  3.4 1.3 %collective-permute-done.recv_ref = bf16[192,1024]{1,0:T(8,128)(2,1)S(1)} collective-permute-done((bf16[192,1024]{1,0:T(8,128)(2,1)S(1)}, bf16[192,1024]{1,0:T(8,128)(2,1)S(1)}, u32[]{:S(2)}, u32[]{:S(2)}) %collective-permute-start) | collective-permute-done | bytes 393248 | tf_op jit(solution)/shard_map/ppermute | solution.py:417
  4.8 0.4 collective-permute-start.3
  5.2 2.7 %collective-permute-start.1 = (bf16[64,1024]{1,0:T(8,128)(2,1)S(1)}, bf16[64,1024]{1,0:T(8,128)(2,1)S(1)}, u32[]{:S(2)}, u32[]{:S(2)}) collective-permute-start(bf16[64,1024]{1,0:T(8,128)(2,1)S(1)} %get-tuple-element.26.a_ref), channel_id=1, source_target_pairs={{0,2},{1,3},{2,0},{3,1},{4,6},{5,7},{6,4},{7,5},{8,10},{9,11},{10,... | collective-permute-start | bytes 393224 | tf_op jit(solution)/shard_map/ppermute | solution.py:417
  7.9 1.3 %collective-permute-start.9 = (bf16[128,2048]{1,0:T(8,128)(2,1)S(1)}, bf16[128,2048]{1,0:T(8,128)(2,1)S(1)}, u32[]{:S(2)}, u32[]{:S(2)}) collective-permute-start(bf16[128,2048]{1,0:T(8,128)(2,1)S(1)} %get-tuple-element.37), channel_id=1, source_target_pairs={{1,3},{2,0},{3,5},{4,2},{5,7},{6,4},{9,11},{10,8},{11,13},{12,10},... | collective-permute-start | bytes 1572872 | tf_op jit(solution)/shard_map/ppermute | solution.py:421
  9.2 2.7 %collective-permute-done.1.b_ref = bf16[64,1024]{1,0:T(8,128)(2,1)S(1)} collective-permute-done((bf16[64,1024]{1,0:T(8,128)(2,1)S(1)}, bf16[64,1024]{1,0:T(8,128)(2,1)S(1)}, u32[]{:S(2)}, u32[]{:S(2)}) %collective-permute-start.1) | collective-permute-done | bytes 131104 | tf_op jit(solution)/shard_map/ppermute | solution.py:417
  12.0 0.0 collective-permute-done.3.sib_ref
  12.0 1.6 %prepare.1 = (bf16[896,1024]{1,0:T(8,128)(2,1)S(1)}, bf16[1024,896]{1,0:T(8,128)(2,1)S(1)}, bf16[1024,768]{1,0:T(8,128)(2,1)S(1)}) custom-call(bf16[1152,1024]{1,0:T(8,128)(2,1)S(1)} %get-tuple-element.27.own_ref, bf16[1152,1024]{1,0:T(8,128)(2,1)S(1)} %collective-permute-done.3.sib_ref), custom_call_target="tpu_custom_call" | custom-call | flops 1600000000 | bytes 1 | tf_op jit(solution)/shard_map/prepare/pallas_call | solution.py:388
  13.6 4.2 %collective-permute-start.5 = (bf16[128,1024]{1,0:T(8,128)(2,1)S(1)}, bf16[128,1024]{1,0:T(8,128)(2,1)S(1)}, u32[]{:S(2)}, u32[]{:S(2)}) collective-permute-start(bf16[128,1024]{1,0:T(8,128)(2,1)S(1)} %get-tuple-element.34.a_ref), channel_id=1, source_target_pairs={{0,2},{1,3},{6,4},{7,5},{8,10},{9,11},{14,12},{15,13},{16,18},{17,... | collective-permute-start | bytes 786440 | tf_op jit(solution)/shard_map/ppermute | solution.py:424
  17.8 0.1 collective-permute-start.2
  17.9 1.1 %collective-permute-done.9.full_ref.edge_a_ref = bf16[128,2048]{1,0:T(8,128)(2,1)S(1)} collective-permute-done((bf16[128,2048]{1,0:T(8,128)(2,1)S(1)}, bf16[128,2048]{1,0:T(8,128)(2,1)S(1)}, u32[]{:S(2)}, u32[]{:S(2)}) %collective-permute-start.9) | collective-permute-done | bytes 524320 | tf_op jit(solution)/shard_map/ppermute | solution.py:421
  19.0 0.1 collective-permute-start.10
  19.1 4.9 %collective-permute-done.5.b_ref = bf16[128,1024]{1,0:T(8,128)(2,1)S(1)} collective-permute-done((bf16[128,1024]{1,0:T(8,128)(2,1)S(1)}, bf16[128,1024]{1,0:T(8,128)(2,1)S(1)}, u32[]{:S(2)}, u32[]{:S(2)}) %collective-permute-start.5) | collective-permute-done | bytes 262176 | tf_op jit(solution)/shard_map/ppermute | solution.py:424
  24.0 0.7 %collective-permute-start.6 = (bf16[128,1024]{1,0:T(8,128)(2,1)S(1)}, bf16[128,1024]{1,0:T(8,128)(2,1)S(1)}, u32[]{:S(2)}, u32[]{:S(2)}) collective-permute-start(bf16[128,1024]{1,0:T(8,128)(2,1)S(1)} %add_keys_values.2.a_ref), channel_id=1, source_target_pairs={{2,4},{3,5},{4,2},{5,3},{10,12},{11,13},{12,10},{13,11},{18,20},{1... | collective-permute-start | bytes 786440 | tf_op jit(solution)/shard_map/ppermute | solution.py:424
  24.7 0.7 %collective-permute-done.2.q_b_ref = bf16[64,1024]{1,0:T(8,128)(2,1)S(1)} collective-permute-done((bf16[64,1024]{1,0:T(8,128)(2,1)S(1)}, bf16[64,1024]{1,0:T(8,128)(2,1)S(1)}, u32[]{:S(2)}, u32[]{:S(2)}) %collective-permute-start.2) | collective-permute-done | bytes 131104 | tf_op jit(solution)/shard_map/ppermute | solution.py:417
  25.4 1.3 %global_partial.1.a_ref = bf16[4,144,128]{2,1,0:T(8,128)(2,1)S(1)} custom-call(bf16[64,1024]{1,0:T(8,128)(2,1)S(1)} %add_queries.1.q_a_ref, bf16[64,1024]{1,0:T(8,128)(2,1)S(1)} %collective-permute-done.2.q_b_ref, bf16[896,1024]{1,0:T(8,128)(2,1)S(1)} %get-tuple-element.31.k_ref, bf16[1024,896]{1,0:T(8,128)(2,1)S(1)} %get-tuple-element.32.v_t_ref), custom_call_target="tpu_custom_call" | custom-call | flops 20000000000 | bytes 1 | tf_op jit(solution)/shard_map/global_partial/pallas_call | solution.py:388
  26.7 7.4 %collective-permute-start.4 = (bf16[4,144,128]{2,1,0:T(8,128)(2,1)S(1)}, bf16[4,144,128]{2,1,0:T(8,128)(2,1)S(1)}, u32[]{:S(2)}, u32[]{:S(2)}) collective-permute-start(bf16[4,144,128]{2,1,0:T(8,128)(2,1)S(1)} %global_partial.1.a_ref), channel_id=1, source_target_pairs={{0,2},{1,3},{6,4},{7,5},{8,10},{9,11},{14,12},{15,13},{16,18},{17,... | collective-permute-start | bytes 442376 | tf_op jit(solution)/shard_map/ppermute | solution.py:424
  34.1 0.0 collective-permute-done.6.b_ref
  34.1 1.3 %collective-permute-start.11 = (bf16[128,1024]{1,0:T(8,128)(2,1)S(1)}, bf16[128,1024]{1,0:T(8,128)(2,1)S(1)}, u32[]{:S(2)}, u32[]{:S(2)}) collective-permute-start(bf16[128,1024]{1,0:T(8,128)(2,1)S(1)} %add_keys_values.3.kv_a_ref), channel_id=1, source_target_pairs={{2,0},{3,1},{4,6},{5,7},{10,8},{11,9},{12,14},{13,15},{18,16},{19,... | collective-permute-start | bytes 786440 | tf_op jit(solution)/shard_map/ppermute | solution.py:424
  35.4 1.3 %collective-permute-done.4.b_ref = bf16[4,144,128]{2,1,0:T(8,128)(2,1)S(1)} collective-permute-done((bf16[4,144,128]{2,1,0:T(8,128)(2,1)S(1)}, bf16[4,144,128]{2,1,0:T(8,128)(2,1)S(1)}, u32[]{:S(2)}, u32[]{:S(2)}) %collective-permute-start.4) | collective-permute-done | bytes 147488 | tf_op jit(solution)/shard_map/ppermute | solution.py:424
  36.7 0.7 %collective-permute-start.7 = (bf16[4,144,128]{2,1,0:T(8,128)(2,1)S(1)}, bf16[4,144,128]{2,1,0:T(8,128)(2,1)S(1)}, u32[]{:S(2)}, u32[]{:S(2)}) collective-permute-start(bf16[4,144,128]{2,1,0:T(8,128)(2,1)S(1)} %merge_partial.1.a_ref), channel_id=1, source_target_pairs={{2,4},{3,5},{4,2},{5,3},{10,12},{11,13},{12,10},{13,11},{18,20},{1... | collective-permute-start | bytes 442376 | tf_op jit(solution)/shard_map/ppermute | solution.py:424
  37.4 0.0 collective-permute-done.10.edge_b_ref
  37.4 0.0 copy-start
  37.4 0.0 copy-start.1
  37.4 4.3 %near_attention.1 = (f32[8,6,128,128]{3,2,1,0:T(8,128)S(1)}, f32[8,2,6,128]{3,2,1,0:T(8,128)S(1)}) custom-call(bf16[1024,768]{1,0:T(8,128)(2,1)S(1)} %get-tuple-element.36.q_t_ref, bf16[896,1024]{1,0:T(8,128)(2,1)S(1)} %get-tuple-element.31.k_ref, bf16[1024,896]{1,0:T(8,128)(2,1)S(1)} %get-tuple-element.32.v_t_ref, ...), custom_call_target="tpu_custom_call" | custom-call | flops 4000000000 | bytes 1 | tf_op jit(solution)/shard_map/near_attention/pallas_call | solution.py:388
  41.8 0.0 collective-permute-done.7.b_ref
  41.8 0.0 copy-done
  41.8 0.2 global_sums.1.own_sums_ref
  42.1 1.3 %collective-permute-start.8 = (f32[8,128]{1,0:T(8,128)S(1)}, f32[8,128]{1,0:T(8,128)S(1)}, u32[]{:S(2)}, u32[]{:S(2)}) collective-permute-start(f32[8,128]{1,0:T(8,128)S(1)} %global_sums.1.own_sums_ref), channel_id=1, source_target_pairs={{2,0},{3,1},{4,6},{5,7},{10,8},{11,9},{12,14},{13,15},{18,16},{19,... | collective-permute-start | bytes 12296 | tf_op jit(solution)/shard_map/ppermute | solution.py:424
  43.3 0.0 collective-permute-done.11.kv_b_ref
  43.4 0.0 copy-done.1
  43.4 3.6 %far_attention.1.win_ref = f32[2,6,128]{2,1,0:T(8,128)S(1)} custom-call(bf16[1024,768]{1,0:T(8,128)(2,1)S(1)} %get-tuple-element.36.q_t_ref, f32[8,6,128,128]{3,2,1,0:T(8,128)S(1)} %get-tuple-element.39.acc_ref, f32[8,2,6,128]{3,2,1,0:T(8,128)S(1)} %get-tuple-element.40.stat_ref, bf16[128,1024]{1,0:T(8,128)(2,1)S(1)} %add_keys_values.3.kv_a_ref, ...), custom_call_target="tpu_custom_call" | custom-call | flops 2000000000 | bytes 1 | tf_op jit(solution)/shard_map/far_attention/pallas_call | solution.py:388
  47.0 2.5 %collective-permute-done.8.far_sums_ref = f32[8,128]{1,0:T(8,128)S(1)} collective-permute-done((f32[8,128]{1,0:T(8,128)S(1)}, f32[8,128]{1,0:T(8,128)S(1)}, u32[]{:S(2)}, u32[]{:S(2)}) %collective-permute-start.8) | collective-permute-done | bytes 4128 | tf_op jit(solution)/shard_map/ppermute | solution.py:424
  49.4 0.3 place_global.1
  49.7 0.1 collective-permute-start.12
  49.8 1.2 %collective-permute-done.12 = f32[2,3,128]{2,1,0:T(4,128)S(1)} collective-permute-done((f32[2,3,128]{2,1,0:T(4,128)S(1)}, f32[2,3,128]{2,1,0:T(4,128)S(1)}, u32[]{:S(2)}, u32[]{:S(2)}) %collective-permute-start.12) | collective-permute-done | bytes 3104 | tf_op jit(solution)/shard_map/ppermute | solution.py:417
  50.9 0.6 %fusion.4 = f32[384]{0:T(512)} fusion(f32[2,3,128]{2,1,0:T(4,128)S(1)} %collective-permute-done.12, f32[2,3,128]{2,1,0:T(4,128)S(1)} %get-tuple-element.41), kind=kLoop, calls=%fused_computation.5 | loop fusion | flops 1920 | bytes 7680 | tf_op jit(solution)/shard_map/mul | solution.py:529
  (6 shorter events, 0.1 us)
Async XLA Ops:
  2.8 1.9 %collective-permute-start = (bf16[192,1024]{1,0:T(8,128)(2,1)S(1)}, bf16[192,1024]{1,0:T(8,128)(2,1)S(1)}, u32[]{:S(2)}, u32[]{:S(2)}) collective-permute-start(bf16[192,1024]{1,0:T(8,128)(2,1)S(1)} %get-tuple-element.25), channel_id=1, source_target_pairs={{0,1},{1,0},{2,3},{3,2},{4,5},{5,4},{6,7},{7,6},{8,9},{9,8},{10,11... | collective-permute-start | bytes 1179656 | tf_op jit(solution)/shard_map/ppermute | solution.py:417
  4.8 7.2 %collective-permute-start.3 = (bf16[1152,1024]{1,0:T(8,128)(2,1)S(1)}, bf16[1152,1024]{1,0:T(8,128)(2,1)S(1)}, u32[]{:S(2)}, u32[]{:S(2)}) collective-permute-start(bf16[1152,1024]{1,0:T(8,128)(2,1)S(1)} %get-tuple-element.29), channel_id=1, source_target_pairs={{0,1},{1,0},{2,3},{3,2},{4,5},{5,4},{6,7},{7,6},{8,9},{9,8},{10,11... | collective-permute-start | bytes 7077896 | tf_op jit(solution)/shard_map/ppermute | solution.py:417
  5.2 6.7 %collective-permute-start.1 = (bf16[64,1024]{1,0:T(8,128)(2,1)S(1)}, bf16[64,1024]{1,0:T(8,128)(2,1)S(1)}, u32[]{:S(2)}, u32[]{:S(2)}) collective-permute-start(bf16[64,1024]{1,0:T(8,128)(2,1)S(1)} %get-tuple-element.26.a_ref), channel_id=1, source_target_pairs={{0,2},{1,3},{2,0},{3,1},{4,6},{5,7},{6,4},{7,5},{8,10},{9,11},{10,... | collective-permute-start | bytes 393224 | tf_op jit(solution)/shard_map/ppermute | solution.py:417
  7.9 11.1 %collective-permute-start.9 = (bf16[128,2048]{1,0:T(8,128)(2,1)S(1)}, bf16[128,2048]{1,0:T(8,128)(2,1)S(1)}, u32[]{:S(2)}, u32[]{:S(2)}) collective-permute-start(bf16[128,2048]{1,0:T(8,128)(2,1)S(1)} %get-tuple-element.37), channel_id=1, source_target_pairs={{1,3},{2,0},{3,5},{4,2},{5,7},{6,4},{9,11},{10,8},{11,13},{12,10},... | collective-permute-start | bytes 1572872 | tf_op jit(solution)/shard_map/ppermute | solution.py:421
  13.6 10.3 %collective-permute-start.5 = (bf16[128,1024]{1,0:T(8,128)(2,1)S(1)}, bf16[128,1024]{1,0:T(8,128)(2,1)S(1)}, u32[]{:S(2)}, u32[]{:S(2)}) collective-permute-start(bf16[128,1024]{1,0:T(8,128)(2,1)S(1)} %get-tuple-element.34.a_ref), channel_id=1, source_target_pairs={{0,2},{1,3},{6,4},{7,5},{8,10},{9,11},{14,12},{15,13},{16,18},{17,... | collective-permute-start | bytes 786440 | tf_op jit(solution)/shard_map/ppermute | solution.py:424
  17.8 7.5 %collective-permute-start.2 = (bf16[64,1024]{1,0:T(8,128)(2,1)S(1)}, bf16[64,1024]{1,0:T(8,128)(2,1)S(1)}, u32[]{:S(2)}, u32[]{:S(2)}) collective-permute-start(bf16[64,1024]{1,0:T(8,128)(2,1)S(1)} %add_queries.1.q_a_ref), channel_id=1, source_target_pairs={{0,4},{1,5},{2,6},{3,7},{4,0},{5,1},{6,2},{7,3},{8,12},{9,13},{10,... | collective-permute-start | bytes 393224 | tf_op jit(solution)/shard_map/ppermute | solution.py:417
  19.0 18.4 %collective-permute-start.10 = (bf16[128,1024]{1,0:T(8,128)(2,1)S(1)}, bf16[128,1024]{1,0:T(8,128)(2,1)S(1)}, u32[]{:S(2)}, u32[]{:S(2)}) collective-permute-start(bf16[128,1024]{1,0:T(8,128)(2,1)S(1)} %split_edges.1), channel_id=1, source_target_pairs={{0,1},{1,0},{2,3},{3,2},{4,5},{5,4},{6,7},{7,6},{8,9},{9,8},{10,11... | collective-permute-start | bytes 786440 | tf_op jit(solution)/shard_map/ppermute | solution.py:417
  24.0 10.1 %collective-permute-start.6 = (bf16[128,1024]{1,0:T(8,128)(2,1)S(1)}, bf16[128,1024]{1,0:T(8,128)(2,1)S(1)}, u32[]{:S(2)}, u32[]{:S(2)}) collective-permute-start(bf16[128,1024]{1,0:T(8,128)(2,1)S(1)} %add_keys_values.2.a_ref), channel_id=1, source_target_pairs={{2,4},{3,5},{4,2},{5,3},{10,12},{11,13},{12,10},{13,11},{18,20},{1... | collective-permute-start | bytes 786440 | tf_op jit(solution)/shard_map/ppermute | solution.py:424
  26.7 10.0 %collective-permute-start.4 = (bf16[4,144,128]{2,1,0:T(8,128)(2,1)S(1)}, bf16[4,144,128]{2,1,0:T(8,128)(2,1)S(1)}, u32[]{:S(2)}, u32[]{:S(2)}) collective-permute-start(bf16[4,144,128]{2,1,0:T(8,128)(2,1)S(1)} %global_partial.1.a_ref), channel_id=1, source_target_pairs={{0,2},{1,3},{6,4},{7,5},{8,10},{9,11},{14,12},{15,13},{16,18},{17,... | collective-permute-start | bytes 442376 | tf_op jit(solution)/shard_map/ppermute | solution.py:424
  34.1 9.2 %collective-permute-start.11 = (bf16[128,1024]{1,0:T(8,128)(2,1)S(1)}, bf16[128,1024]{1,0:T(8,128)(2,1)S(1)}, u32[]{:S(2)}, u32[]{:S(2)}) collective-permute-start(bf16[128,1024]{1,0:T(8,128)(2,1)S(1)} %add_keys_values.3.kv_a_ref), channel_id=1, source_target_pairs={{2,0},{3,1},{4,6},{5,7},{10,8},{11,9},{12,14},{13,15},{18,16},{19,... | collective-permute-start | bytes 786440 | tf_op jit(solution)/shard_map/ppermute | solution.py:424
  36.7 5.1 %collective-permute-start.7 = (bf16[4,144,128]{2,1,0:T(8,128)(2,1)S(1)}, bf16[4,144,128]{2,1,0:T(8,128)(2,1)S(1)}, u32[]{:S(2)}, u32[]{:S(2)}) collective-permute-start(bf16[4,144,128]{2,1,0:T(8,128)(2,1)S(1)} %merge_partial.1.a_ref), channel_id=1, source_target_pairs={{2,4},{3,5},{4,2},{5,3},{10,12},{11,13},{12,10},{13,11},{18,20},{1... | collective-permute-start | bytes 442376 | tf_op jit(solution)/shard_map/ppermute | solution.py:424
  37.4 4.4 %copy-start = (f32[2048]{0:T(1024)S(1)}, f32[2048]{0:T(1024)}, u32[]{:S(2)}) copy-start(f32[2048]{0:T(1024)} %param.9) | copy-start | bytes 24580
  37.4 5.9 %copy-start.1 = (s32[64]{0:T(128)S(1)}, s32[64]{0:T(128)}, u32[]{:S(2)}) copy-start(s32[64]{0:T(128)} %param.8) | copy-start | bytes 772
  42.1 7.4 %collective-permute-start.8 = (f32[8,128]{1,0:T(8,128)S(1)}, f32[8,128]{1,0:T(8,128)S(1)}, u32[]{:S(2)}, u32[]{:S(2)}) collective-permute-start(f32[8,128]{1,0:T(8,128)S(1)} %global_sums.1.own_sums_ref), channel_id=1, source_target_pairs={{2,0},{3,1},{4,6},{5,7},{10,8},{11,9},{12,14},{13,15},{18,16},{19,... | collective-permute-start | bytes 12296 | tf_op jit(solution)/shard_map/ppermute | solution.py:424
  49.7 1.2 %collective-permute-start.12 = (f32[2,3,128]{2,1,0:T(4,128)S(1)}, f32[2,3,128]{2,1,0:T(4,128)S(1)}, u32[]{:S(2)}, u32[]{:S(2)}) collective-permute-start(f32[2,3,128]{2,1,0:T(4,128)S(1)} %get-tuple-element.42), channel_id=1, source_target_pairs={{0,1},{1,0},{2,3},{3,2},{4,5},{5,4},{6,7},{7,6},{8,9},{9,8},{10,11... | collective-permute-start | bytes 9224 | tf_op jit(solution)/shard_map/ppermute | solution.py:417

commit v5 on v4

--- a/solution.py
+++ b/solution.py
@@ -221,7 +221,7 @@
     for pair in range(pairs):
         a = get_message(a_ref, pair, head_size)
         b = get_message(b_ref, pair, head_size)
-        if on_line():
+        if False:
             b = tuple(jnp.where(is_inner(chip), y, x) for x, y in zip(a, b))
         out, _, _ = merged(a, b, scale2)
         w_a = w_ref[pl.ds(core * 2 * pairs + 2 * pair, 1), :]
@@ -238,7 +238,7 @@
     glob = pos_ref.shape[1]
     core, chip = device_place()
     sums = own_sums_ref[...]
-    if on_line():
+    if False:
         sums = jnp.where(is_inner(chip), sums, far_sums_ref[...])
     parts = [p.astype(jnp.float32) for p in (*pieces(sums[0:1]), *pieces(sums[1:2]))] + [jnp.ones((1, LANES), jnp.float32)]
     row = lax.broadcasted_iota(jnp.int32, (16, LANES), 0)
@@ -490,7 +490,7 @@
         micros=20.0,
     )
     weights = score_weight.reshape(HEADS, head_size)
-    if chips == 4:
+    if chips == 3:
         message = call(
             functools.partial(inward_kernel, scale2), "merge_partial", part, [message, after((move(message, inward),), kv_near)[0]]
         )
@@ -498,13 +498,13 @@
     else:
         for r in range(1, rounds):
             message = call(
-                functools.partial(merge_kernel, scale2), "merge_partial", part, [message, swap(message, 1 << r)]
+                functools.partial(merge_kernel, scale2), "merge_partial", part, [message, after((swap(message, 1 << r),), kv_near)[0]]
             )
         message_far = swap(message, 1 << rounds)
     sums = call(
         functools.partial(sums_kernel, scale2), "global_sums", ((8, LANES), f32), [message, message_far, weights]
     )
-    sums_far = move(sums, outward) if chips == 4 else sums
+    sums_far = sums
 
     window = call(
         functools.partial(far_kernel, scale2),

time: 51.7 us -> 50.2 us (0.971)
  starting transfers between devices: 20.7 us -> 19.5 us
    ppermute x6 -> x3, starting transfers between devices: 15.5 us -> 6.2 us  [move(): lax.ppermute(x, 'seq', [(a * CORES + c, b * CORES + c) for a, b in pairs...]
    ppermute x6 -> x8, starting transfers between devices: 3.89 us -> 12 us  [swap(): return lax.ppermute(x, 'seq', [(i, i ^ mask) for i in range(seq_count)])]
    ppermute x6 -> x3, waiting for transfers between devices: 8.63 us -> 5.7 us  [move(): lax.ppermute(x, 'seq', [(a * CORES + c, b * CORES + c) for a, b in pairs...]
    ppermute x6 -> x8, waiting for transfers between devices: 5.92 us -> 8.49 us  [swap(): return lax.ppermute(x, 'seq', [(i, i ^ mask) for i in range(seq_count)])]
  transfers between devices with their start and end apart: 13 -> 12, of which waited for: 8 -> 9; matrix products, arithmetic and copies ran while one was open for 0% -> 0% of each run, Pallas kernels for 22% -> 15%
where the time goes in v5:
time: 50.2 us; the launch traced here: 50 us
  starting transfers between devices  19.5 us (39%)
  waiting for transfers between devices  15.2 us (30%)
  Pallas kernels  14.5 us (29%)
  other arithmetic  0.59 us (1%)
    pallas_call x13, Pallas kernels, call(): pl.pallas_call(kernel, in_specs=[pl.BlockSpec(memory_space=source)] * len...  14.5 us
    ppermute x8, starting transfers between devices, swap(): return lax.ppermute(x, 'seq', [(i, i ^ mask) for i in range(seq_count)])  12 us
    ppermute x8, waiting for transfers between devices, swap(): return lax.ppermute(x, 'seq', [(i, i ^ mask) for i in range(seq_count)])  8.49 us
    ppermute x3, starting transfers between devices, move(): lax.ppermute(x, 'seq', [(a * CORES + c, b * CORES + c) for a, b in pairs...  6.2 us
    ppermute x3, waiting for transfers between devices, move(): lax.ppermute(x, 'seq', [(a * CORES + c, b * CORES + c) for a, b in pairs...  5.7 us
    ppermute x1, starting transfers between devices, move_cores(): lax.ppermute(x, 'seq', [(i, to) for i, to in moves if 0 <= to < seq_count])  1.28 us
    ppermute x1, waiting for transfers between devices, move_cores(): lax.ppermute(x, 'seq', [(i, to) for i, to in moves if 0 <= to < seq_count])  1.05 us
  transfers between devices with their start and end apart: 12, of which 9 were waited for; matrix products, arithmetic and copies ran while one was open for 0% of the time, Pallas kernels for 15%

profile of v5, /device:TPU:0, one launch (start us, length us, event | category | flops | bytes accessed | tf_op | source)
XLA Modules:
  0.0 50.0 jit_solution(3335125908950764009)
XLA Ops:
  0.0 2.8 %select_rows.1 = (bf16[192,1024]{1,0:T(8,128)(2,1)S(1)}, bf16[192,1024]{1,0:T(8,128)(2,1)S(1)}, bf16[128,2048]{1,0:T(8,128)(2,1)S(1)}, bf16[1152,1024]{1,0:T(8,128)(2,1)S(1)}, bf16[1152,1024]{1,0:T(8,128)(2,1)S(1)}) custom-call(s32[1,64]{1,0:T(1,128)} %bitcast.6, bf16[384,2048]{1,0:T(8,128)(2,1)} %q_hbm.1, bf16[384,2048]{1,0:T(8,128)(2,1)} %k_hbm.1, ...), custom_call_target="tpu_custom_call" | custom-call | flops 1 | bytes 1 | tf_op jit(solution)/shard_map/select_rows/pallas_call | solution.py:388
  2.8 0.5 %collective-permute-start = (bf16[192,1024]{1,0:T(8,128)(2,1)S(1)}, bf16[192,1024]{1,0:T(8,128)(2,1)S(1)}, u32[]{:S(2)}, u32[]{:S(2)}) collective-permute-start(bf16[192,1024]{1,0:T(8,128)(2,1)S(1)} %get-tuple-element.25), channel_id=1, source_target_pairs={{0,1},{1,0},{2,3},{3,2},{4,5},{5,4},{6,7},{7,6},{8,9},{9,8},{10,11... | collective-permute-start | bytes 1179656 | tf_op jit(solution)/shard_map/ppermute | solution.py:417
  3.4 1.3 %collective-permute-done.recv_ref = bf16[192,1024]{1,0:T(8,128)(2,1)S(1)} collective-permute-done((bf16[192,1024]{1,0:T(8,128)(2,1)S(1)}, bf16[192,1024]{1,0:T(8,128)(2,1)S(1)}, u32[]{:S(2)}, u32[]{:S(2)}) %collective-permute-start) | collective-permute-done | bytes 393248 | tf_op jit(solution)/shard_map/ppermute | solution.py:417
  4.8 0.4 collective-permute-start.3
  5.2 2.7 %collective-permute-start.1 = (bf16[64,1024]{1,0:T(8,128)(2,1)S(1)}, bf16[64,1024]{1,0:T(8,128)(2,1)S(1)}, u32[]{:S(2)}, u32[]{:S(2)}) collective-permute-start(bf16[64,1024]{1,0:T(8,128)(2,1)S(1)} %get-tuple-element.26.a_ref), channel_id=1, source_target_pairs={{0,2},{1,3},{2,0},{3,1},{4,6},{5,7},{6,4},{7,5},{8,10},{9,11},{10,... | collective-permute-start | bytes 393224 | tf_op jit(solution)/shard_map/ppermute | solution.py:417
  7.9 1.3 %collective-permute-start.8 = (bf16[128,2048]{1,0:T(8,128)(2,1)S(1)}, bf16[128,2048]{1,0:T(8,128)(2,1)S(1)}, u32[]{:S(2)}, u32[]{:S(2)}) collective-permute-start(bf16[128,2048]{1,0:T(8,128)(2,1)S(1)} %get-tuple-element.37), channel_id=1, source_target_pairs={{1,3},{2,0},{3,5},{4,2},{5,7},{6,4},{9,11},{10,8},{11,13},{12,10},... | collective-permute-start | bytes 1572872 | tf_op jit(solution)/shard_map/ppermute | solution.py:421
  9.2 2.7 %collective-permute-done.1.b_ref = bf16[64,1024]{1,0:T(8,128)(2,1)S(1)} collective-permute-done((bf16[64,1024]{1,0:T(8,128)(2,1)S(1)}, bf16[64,1024]{1,0:T(8,128)(2,1)S(1)}, u32[]{:S(2)}, u32[]{:S(2)}) %collective-permute-start.1) | collective-permute-done | bytes 131104 | tf_op jit(solution)/shard_map/ppermute | solution.py:417
  12.0 0.0 collective-permute-done.3.sib_ref
  12.0 1.6 %prepare.1 = (bf16[896,1024]{1,0:T(8,128)(2,1)S(1)}, bf16[1024,896]{1,0:T(8,128)(2,1)S(1)}, bf16[1024,768]{1,0:T(8,128)(2,1)S(1)}) custom-call(bf16[1152,1024]{1,0:T(8,128)(2,1)S(1)} %get-tuple-element.27.own_ref, bf16[1152,1024]{1,0:T(8,128)(2,1)S(1)} %collective-permute-done.3.sib_ref), custom_call_target="tpu_custom_call" | custom-call | flops 1600000000 | bytes 1 | tf_op jit(solution)/shard_map/prepare/pallas_call | solution.py:388
  13.6 4.2 %collective-permute-start.5 = (bf16[128,1024]{1,0:T(8,128)(2,1)S(1)}, bf16[128,1024]{1,0:T(8,128)(2,1)S(1)}, u32[]{:S(2)}, u32[]{:S(2)}) collective-permute-start(bf16[128,1024]{1,0:T(8,128)(2,1)S(1)} %get-tuple-element.34.a_ref), channel_id=1, source_target_pairs={{0,2},{1,3},{6,4},{7,5},{8,10},{9,11},{14,12},{15,13},{16,18},{17,... | collective-permute-start | bytes 786440 | tf_op jit(solution)/shard_map/ppermute | solution.py:424
  17.8 0.1 collective-permute-start.2
  17.9 1.1 %collective-permute-done.8.full_ref.edge_a_ref = bf16[128,2048]{1,0:T(8,128)(2,1)S(1)} collective-permute-done((bf16[128,2048]{1,0:T(8,128)(2,1)S(1)}, bf16[128,2048]{1,0:T(8,128)(2,1)S(1)}, u32[]{:S(2)}, u32[]{:S(2)}) %collective-permute-start.8) | collective-permute-done | bytes 524320 | tf_op jit(solution)/shard_map/ppermute | solution.py:421
  19.0 0.1 collective-permute-start.9
  19.1 4.9 %collective-permute-done.5.b_ref = bf16[128,1024]{1,0:T(8,128)(2,1)S(1)} collective-permute-done((bf16[128,1024]{1,0:T(8,128)(2,1)S(1)}, bf16[128,1024]{1,0:T(8,128)(2,1)S(1)}, u32[]{:S(2)}, u32[]{:S(2)}) %collective-permute-start.5) | collective-permute-done | bytes 262176 | tf_op jit(solution)/shard_map/ppermute | solution.py:424
  24.0 0.7 %collective-permute-start.6 = (bf16[128,1024]{1,0:T(8,128)(2,1)S(1)}, bf16[128,1024]{1,0:T(8,128)(2,1)S(1)}, u32[]{:S(2)}, u32[]{:S(2)}) collective-permute-start(bf16[128,1024]{1,0:T(8,128)(2,1)S(1)} %add_keys_values.2.a_ref), channel_id=1, source_target_pairs={{2,4},{3,5},{4,2},{5,3},{10,12},{11,13},{12,10},{13,11},{18,20},{1... | collective-permute-start | bytes 786440 | tf_op jit(solution)/shard_map/ppermute | solution.py:424
  24.7 0.7 %collective-permute-done.2.q_b_ref = bf16[64,1024]{1,0:T(8,128)(2,1)S(1)} collective-permute-done((bf16[64,1024]{1,0:T(8,128)(2,1)S(1)}, bf16[64,1024]{1,0:T(8,128)(2,1)S(1)}, u32[]{:S(2)}, u32[]{:S(2)}) %collective-permute-start.2) | collective-permute-done | bytes 131104 | tf_op jit(solution)/shard_map/ppermute | solution.py:417
  25.4 1.3 %global_partial.1.a_ref = bf16[4,144,128]{2,1,0:T(8,128)(2,1)S(1)} custom-call(bf16[64,1024]{1,0:T(8,128)(2,1)S(1)} %add_queries.1.q_a_ref, bf16[64,1024]{1,0:T(8,128)(2,1)S(1)} %collective-permute-done.2.q_b_ref, bf16[896,1024]{1,0:T(8,128)(2,1)S(1)} %get-tuple-element.31.k_ref, bf16[1024,896]{1,0:T(8,128)(2,1)S(1)} %get-tuple-element.32.v_t_ref), custom_call_target="tpu_custom_call" | custom-call | flops 20000000000 | bytes 1 | tf_op jit(solution)/shard_map/global_partial/pallas_call | solution.py:388
  26.7 5.5 %collective-permute-start.4 = (bf16[4,144,128]{2,1,0:T(8,128)(2,1)S(1)}, bf16[4,144,128]{2,1,0:T(8,128)(2,1)S(1)}, u32[]{:S(2)}, u32[]{:S(2)}) collective-permute-start(bf16[4,144,128]{2,1,0:T(8,128)(2,1)S(1)} %global_partial.1.a_ref), channel_id=1, source_target_pairs={{0,2},{1,3},{2,0},{3,1},{4,6},{5,7},{6,4},{7,5},{8,10},{9,11},{10,... | collective-permute-start | bytes 442376 | tf_op jit(solution)/shard_map/ppermute | solution.py:417
  32.2 0.0 collective-permute-done.6.b_ref
  32.3 1.3 %collective-permute-start.10 = (bf16[128,1024]{1,0:T(8,128)(2,1)S(1)}, bf16[128,1024]{1,0:T(8,128)(2,1)S(1)}, u32[]{:S(2)}, u32[]{:S(2)}) collective-permute-start(bf16[128,1024]{1,0:T(8,128)(2,1)S(1)} %add_keys_values.3.kv_a_ref), channel_id=1, source_target_pairs={{2,0},{3,1},{4,6},{5,7},{10,8},{11,9},{12,14},{13,15},{18,16},{19,... | collective-permute-start | bytes 786440 | tf_op jit(solution)/shard_map/ppermute | solution.py:424
  33.6 1.8 %collective-permute-done.4.b_ref = bf16[4,144,128]{2,1,0:T(8,128)(2,1)S(1)} collective-permute-done((bf16[4,144,128]{2,1,0:T(8,128)(2,1)S(1)}, bf16[4,144,128]{2,1,0:T(8,128)(2,1)S(1)}, u32[]{:S(2)}, u32[]{:S(2)}) %collective-permute-start.4) | collective-permute-done | bytes 147488 | tf_op jit(solution)/shard_map/ppermute | solution.py:417
  35.3 0.1 merge_partial.1.a_ref
  35.4 2.6 %collective-permute-start.7 = (bf16[4,144,128]{2,1,0:T(8,128)(2,1)S(1)}, bf16[4,144,128]{2,1,0:T(8,128)(2,1)S(1)}, u32[]{:S(2)}, u32[]{:S(2)}) collective-permute-start(bf16[4,144,128]{2,1,0:T(8,128)(2,1)S(1)} %merge_partial.1.a_ref), channel_id=1, source_target_pairs={{0,4},{1,5},{2,6},{3,7},{4,0},{5,1},{6,2},{7,3},{8,12},{9,13},{10,... | collective-permute-start | bytes 442376 | tf_op jit(solution)/shard_map/ppermute | solution.py:417
  38.1 0.0 collective-permute-done.9.edge_b_ref
  38.1 0.0 copy-start
  38.1 0.0 copy-start.1
  38.1 4.3 %near_attention.1 = (f32[8,6,128,128]{3,2,1,0:T(8,128)S(1)}, f32[8,2,6,128]{3,2,1,0:T(8,128)S(1)}) custom-call(bf16[1024,768]{1,0:T(8,128)(2,1)S(1)} %get-tuple-element.36.q_t_ref, bf16[896,1024]{1,0:T(8,128)(2,1)S(1)} %get-tuple-element.31.k_ref, bf16[1024,896]{1,0:T(8,128)(2,1)S(1)} %get-tuple-element.32.v_t_ref, ...), custom_call_target="tpu_custom_call" | custom-call | flops 4000000000 | bytes 1 | tf_op jit(solution)/shard_map/near_attention/pallas_call | solution.py:388
  42.4 0.8 %collective-permute-done.7.b_ref = bf16[4,144,128]{2,1,0:T(8,128)(2,1)S(1)} collective-permute-done((bf16[4,144,128]{2,1,0:T(8,128)(2,1)S(1)}, bf16[4,144,128]{2,1,0:T(8,128)(2,1)S(1)}, u32[]{:S(2)}, u32[]{:S(2)}) %collective-permute-start.7) | collective-permute-done | bytes 147488 | tf_op jit(solution)/shard_map/ppermute | solution.py:417
  43.2 0.0 copy-done
  43.2 0.2 global_sums.1.own_sums_ref.far_sums_ref
  43.5 0.8 %collective-permute-done.10.kv_b_ref = bf16[128,1024]{1,0:T(8,128)(2,1)S(1)} collective-permute-done((bf16[128,1024]{1,0:T(8,128)(2,1)S(1)}, bf16[128,1024]{1,0:T(8,128)(2,1)S(1)}, u32[]{:S(2)}, u32[]{:S(2)}) %collective-permute-start.10) | collective-permute-done | bytes 262176 | tf_op jit(solution)/shard_map/ppermute | solution.py:424
  44.3 0.0 copy-done.1
  44.3 3.6 %far_attention.1.win_ref = f32[2,6,128]{2,1,0:T(8,128)S(1)} custom-call(bf16[1024,768]{1,0:T(8,128)(2,1)S(1)} %get-tuple-element.36.q_t_ref, f32[8,6,128,128]{3,2,1,0:T(8,128)S(1)} %get-tuple-element.39.acc_ref, f32[8,2,6,128]{3,2,1,0:T(8,128)S(1)} %get-tuple-element.40.stat_ref, bf16[128,1024]{1,0:T(8,128)(2,1)S(1)} %add_keys_values.3.kv_a_ref, ...), custom_call_target="tpu_custom_call" | custom-call | flops 2000000000 | bytes 1 | tf_op jit(solution)/shard_map/far_attention/pallas_call | solution.py:388
  47.9 0.3 place_global.1
  48.2 0.1 collective-permute-start.11
  48.3 1.2 %collective-permute-done.11 = f32[2,3,128]{2,1,0:T(4,128)S(1)} collective-permute-done((f32[2,3,128]{2,1,0:T(4,128)S(1)}, f32[2,3,128]{2,1,0:T(4,128)S(1)}, u32[]{:S(2)}, u32[]{:S(2)}) %collective-permute-start.11) | collective-permute-done | bytes 3104 | tf_op jit(solution)/shard_map/ppermute | solution.py:417
  49.4 0.6 %fusion.4 = f32[384]{0:T(512)} fusion(f32[2,3,128]{2,1,0:T(4,128)S(1)} %collective-permute-done.11, f32[2,3,128]{2,1,0:T(4,128)S(1)} %get-tuple-element.41), kind=kLoop, calls=%fused_computation.5 | loop fusion | flops 1920 | bytes 7680 | tf_op jit(solution)/shard_map/mul | solution.py:529
  (5 shorter events, 0.1 us)
Async XLA Ops:
  2.8 1.9 %collective-permute-start = (bf16[192,1024]{1,0:T(8,128)(2,1)S(1)}, bf16[192,1024]{1,0:T(8,128)(2,1)S(1)}, u32[]{:S(2)}, u32[]{:S(2)}) collective-permute-start(bf16[192,1024]{1,0:T(8,128)(2,1)S(1)} %get-tuple-element.25), channel_id=1, source_target_pairs={{0,1},{1,0},{2,3},{3,2},{4,5},{5,4},{6,7},{7,6},{8,9},{9,8},{10,11... | collective-permute-start | bytes 1179656 | tf_op jit(solution)/shard_map/ppermute | solution.py:417
  4.8 7.2 %collective-permute-start.3 = (bf16[1152,1024]{1,0:T(8,128)(2,1)S(1)}, bf16[1152,1024]{1,0:T(8,128)(2,1)S(1)}, u32[]{:S(2)}, u32[]{:S(2)}) collective-permute-start(bf16[1152,1024]{1,0:T(8,128)(2,1)S(1)} %get-tuple-element.29), channel_id=1, source_target_pairs={{0,1},{1,0},{2,3},{3,2},{4,5},{5,4},{6,7},{7,6},{8,9},{9,8},{10,11... | collective-permute-start | bytes 7077896 | tf_op jit(solution)/shard_map/ppermute | solution.py:417
  5.2 6.7 %collective-permute-start.1 = (bf16[64,1024]{1,0:T(8,128)(2,1)S(1)}, bf16[64,1024]{1,0:T(8,128)(2,1)S(1)}, u32[]{:S(2)}, u32[]{:S(2)}) collective-permute-start(bf16[64,1024]{1,0:T(8,128)(2,1)S(1)} %get-tuple-element.26.a_ref), channel_id=1, source_target_pairs={{0,2},{1,3},{2,0},{3,1},{4,6},{5,7},{6,4},{7,5},{8,10},{9,11},{10,... | collective-permute-start | bytes 393224 | tf_op jit(solution)/shard_map/ppermute | solution.py:417
  7.9 11.1 %collective-permute-start.8 = (bf16[128,2048]{1,0:T(8,128)(2,1)S(1)}, bf16[128,2048]{1,0:T(8,128)(2,1)S(1)}, u32[]{:S(2)}, u32[]{:S(2)}) collective-permute-start(bf16[128,2048]{1,0:T(8,128)(2,1)S(1)} %get-tuple-element.37), channel_id=1, source_target_pairs={{1,3},{2,0},{3,5},{4,2},{5,7},{6,4},{9,11},{10,8},{11,13},{12,10},... | collective-permute-start | bytes 1572872 | tf_op jit(solution)/shard_map/ppermute | solution.py:421
  13.6 10.3 %collective-permute-start.5 = (bf16[128,1024]{1,0:T(8,128)(2,1)S(1)}, bf16[128,1024]{1,0:T(8,128)(2,1)S(1)}, u32[]{:S(2)}, u32[]{:S(2)}) collective-permute-start(bf16[128,1024]{1,0:T(8,128)(2,1)S(1)} %get-tuple-element.34.a_ref), channel_id=1, source_target_pairs={{0,2},{1,3},{6,4},{7,5},{8,10},{9,11},{14,12},{15,13},{16,18},{17,... | collective-permute-start | bytes 786440 | tf_op jit(solution)/shard_map/ppermute | solution.py:424
  17.8 7.5 %collective-permute-start.2 = (bf16[64,1024]{1,0:T(8,128)(2,1)S(1)}, bf16[64,1024]{1,0:T(8,128)(2,1)S(1)}, u32[]{:S(2)}, u32[]{:S(2)}) collective-permute-start(bf16[64,1024]{1,0:T(8,128)(2,1)S(1)} %add_queries.1.q_a_ref), channel_id=1, source_target_pairs={{0,4},{1,5},{2,6},{3,7},{4,0},{5,1},{6,2},{7,3},{8,12},{9,13},{10,... | collective-permute-start | bytes 393224 | tf_op jit(solution)/shard_map/ppermute | solution.py:417
  19.0 19.1 %collective-permute-start.9 = (bf16[128,1024]{1,0:T(8,128)(2,1)S(1)}, bf16[128,1024]{1,0:T(8,128)(2,1)S(1)}, u32[]{:S(2)}, u32[]{:S(2)}) collective-permute-start(bf16[128,1024]{1,0:T(8,128)(2,1)S(1)} %split_edges.1), channel_id=1, source_target_pairs={{0,1},{1,0},{2,3},{3,2},{4,5},{5,4},{6,7},{7,6},{8,9},{9,8},{10,11... | collective-permute-start | bytes 786440 | tf_op jit(solution)/shard_map/ppermute | solution.py:417
  24.0 8.2 %collective-permute-start.6 = (bf16[128,1024]{1,0:T(8,128)(2,1)S(1)}, bf16[128,1024]{1,0:T(8,128)(2,1)S(1)}, u32[]{:S(2)}, u32[]{:S(2)}) collective-permute-start(bf16[128,1024]{1,0:T(8,128)(2,1)S(1)} %add_keys_values.2.a_ref), channel_id=1, source_target_pairs={{2,4},{3,5},{4,2},{5,3},{10,12},{11,13},{12,10},{13,11},{18,20},{1... | collective-permute-start | bytes 786440 | tf_op jit(solution)/shard_map/ppermute | solution.py:424
  26.7 8.6 %collective-permute-start.4 = (bf16[4,144,128]{2,1,0:T(8,128)(2,1)S(1)}, bf16[4,144,128]{2,1,0:T(8,128)(2,1)S(1)}, u32[]{:S(2)}, u32[]{:S(2)}) collective-permute-start(bf16[4,144,128]{2,1,0:T(8,128)(2,1)S(1)} %global_partial.1.a_ref), channel_id=1, source_target_pairs={{0,2},{1,3},{2,0},{3,1},{4,6},{5,7},{6,4},{7,5},{8,10},{9,11},{10,... | collective-permute-start | bytes 442376 | tf_op jit(solution)/shard_map/ppermute | solution.py:417
  32.3 12.0 %collective-permute-start.10 = (bf16[128,1024]{1,0:T(8,128)(2,1)S(1)}, bf16[128,1024]{1,0:T(8,128)(2,1)S(1)}, u32[]{:S(2)}, u32[]{:S(2)}) collective-permute-start(bf16[128,1024]{1,0:T(8,128)(2,1)S(1)} %add_keys_values.3.kv_a_ref), channel_id=1, source_target_pairs={{2,0},{3,1},{4,6},{5,7},{10,8},{11,9},{12,14},{13,15},{18,16},{19,... | collective-permute-start | bytes 786440 | tf_op jit(solution)/shard_map/ppermute | solution.py:424
  35.4 7.8 %collective-permute-start.7 = (bf16[4,144,128]{2,1,0:T(8,128)(2,1)S(1)}, bf16[4,144,128]{2,1,0:T(8,128)(2,1)S(1)}, u32[]{:S(2)}, u32[]{:S(2)}) collective-permute-start(bf16[4,144,128]{2,1,0:T(8,128)(2,1)S(1)} %merge_partial.1.a_ref), channel_id=1, source_target_pairs={{0,4},{1,5},{2,6},{3,7},{4,0},{5,1},{6,2},{7,3},{8,12},{9,13},{10,... | collective-permute-start | bytes 442376 | tf_op jit(solution)/shard_map/ppermute | solution.py:417
  38.1 5.1 %copy-start = (f32[2048]{0:T(1024)S(1)}, f32[2048]{0:T(1024)}, u32[]{:S(2)}) copy-start(f32[2048]{0:T(1024)} %param.9) | copy-start | bytes 24580
  38.1 6.2 %copy-start.1 = (s32[64]{0:T(128)S(1)}, s32[64]{0:T(128)}, u32[]{:S(2)}) copy-start(s32[64]{0:T(128)} %param.8) | copy-start | bytes 772
  48.2 1.2 %collective-permute-start.11 = (f32[2,3,128]{2,1,0:T(4,128)S(1)}, f32[2,3,128]{2,1,0:T(4,128)S(1)}, u32[]{:S(2)}, u32[]{:S(2)}) collective-permute-start(f32[2,3,128]{2,1,0:T(4,128)S(1)} %get-tuple-element.42), channel_id=1, source_target_pairs={{0,1},{1,0},{2,3},{3,2},{4,5},{5,4},{6,7},{7,6},{8,9},{9,8},{10,11... | collective-permute-start | bytes 9224 | tf_op jit(solution)/shard_map/ppermute | solution.py:417

commit v6 on v5

--- a/solution.py
+++ b/solution.py
@@ -261,7 +261,23 @@
                 out_ref[i, j : j + 1, :] = jnp.where(is_glob, value, win_ref[i, pl.ds(pair, 1), :])
 
 
-def near_kernel(scale2, q_t_ref, k_ref, v_t_ref, edge_a_ref, edge_b_ref, acc_ref, stat_ref, s_buf, e_buf, edges):
+def near_kernel(
+    scale2,
+    q_t_ref,
+    k_ref,
+    v_t_ref,
+    edge_a_ref,
+    edge_b_ref,
+    w_ref,
+    pos_ref,
+    acc_ref,
+    stat_ref,
+    bias,
+    w_cols,
+    s_buf,
+    e_buf,
+    edges,
+):
     half, tokens = q_t_ref.shape
     n_pairs = tokens // LANES
     core, chip = device_place()
@@ -282,6 +298,16 @@
     def _():
         edges[0] = edge_b_ref[...]
         edges[1] = edge_a_ref[:, mine]
+
+    glob = pos_ref.shape[1]
+    heads = half // LANES
+    glob_block = column_of(pos_ref[...] // BLK)
+    for j in range(n_pairs):
+        block = (chip * n_pairs + j) * (LANES // BLK) + lax.broadcasted_iota(jnp.int32, (glob, LANES), 1) // BLK
+        bias[j] = jnp.where(jnp.abs(glob_block - block.astype(jnp.float32)) > 1.5, 0.0, NEG)
+    for head in range(heads):
+        row = w_ref[pl.ds(core * heads + head, 1), :]
+        w_cols[head] = jnp.transpose(jnp.broadcast_to(row, (LANES, LANES)))
 
     def one_head(head, carry):
         cols = pl.ds(pl.multiple_of(head * LANES, LANES), LANES)
@@ -323,25 +349,17 @@
             acc_ref[head, j] = dot_n(jnp.concatenate([v_0, v_1], axis=1), e_buf[j])
         return carry
 
-    lax.fori_loop(0, half // LANES, one_head, 0)
+    lax.fori_loop(0, half // LANES, one_head, 0, unroll=1)
 
 
 def far_kernel(
-    scale2, q_t_ref, acc_ref, stat_ref, kv_a_ref, kv_b_ref, w_ref, pos_ref, out_ref, s_buf, e_buf, bias, w_cols
+    scale2, q_t_ref, acc_ref, stat_ref, kv_a_ref, kv_b_ref, bias, w_cols, out_ref, s_buf, e_buf
 ):
     half, tokens = q_t_ref.shape
-    glob = pos_ref.shape[1]
+    glob = bias.shape[1]
     heads = half // LANES
     n_pairs = tokens // LANES
     core, chip = device_place()
-    glob_block = column_of(pos_ref[...] // BLK)
-    for j in range(n_pairs):
-        block = (chip * n_pairs + j) * (LANES // BLK) + lax.broadcasted_iota(jnp.int32, (glob, LANES), 1) // BLK
-        bias[j] = jnp.where(jnp.abs(glob_block - block.astype(jnp.float32)) > 1.5, 0.0, NEG)
-    for head in range(heads):
-        row = w_ref[pl.ds(core * heads + head, 1), :]
-        w_cols[head] = jnp.transpose(jnp.broadcast_to(row, (LANES, LANES)))
-
     def one_head(head, carry):
         cols = pl.ds(pl.multiple_of(head * LANES, LANES), LANES)
         kv_a = kv_a_ref[:, cols]
@@ -350,16 +368,16 @@
         kv = kv_a + kv_b_ref[:, cols]
         kg = kv[:glob]
         for j in range(n_pairs):
-            s_buf[j] = dot_n(kg, q_t_ref[cols, j * LANES : (j + 1) * LANES])
+            s_buf[head, j] = dot_n(kg, q_t_ref[cols, j * LANES : (j + 1) * LANES])
         near_peaks = stat_ref[head, 0]
         near_totals = stat_ref[head, 1]
         near_weights, inverses = [], []
         for j in range(n_pairs):
-            far = s_buf[j] + bias[j]
+            far = s_buf[head, j] + bias[j]
             near_peak = near_peaks[j : j + 1]
             peak = jnp.maximum(jnp.max(far, axis=0, keepdims=True), near_peak)
             e_far = jnp.exp2((far - peak) * scale2)
-            e_buf[j] = e_far.astype(jnp.bfloat16)
+            e_buf[head, j] = e_far.astype(jnp.bfloat16)
             near_weight = jnp.exp2((near_peak - peak) * scale2)
             total = near_totals[j : j + 1] * near_weight + jnp.sum(e_far, axis=0, keepdims=True)
             near_weights.append(near_weight)
@@ -368,14 +386,14 @@
         w = w_cols[head]
         lins, sqs = [], []
         for j in range(n_pairs):
-            acc = acc_ref[head, j] * near_weights[j] + dot_n(vg_t, e_buf[j])
+            acc = acc_ref[head, j] * near_weights[j] + dot_n(vg_t, e_buf[head, j])
             lins.append(jnp.sum(acc * w, axis=0, keepdims=True) * inverses[j])
             sqs.append(jnp.sum(acc * acc, axis=0, keepdims=True) * (inverses[j] * inverses[j]))
         lin, sq = carry
         return lin + jnp.concatenate(lins, axis=0), sq + jnp.concatenate(sqs, axis=0)
 
     none = jnp.zeros((n_pairs, LANES), jnp.float32)
-    lin, sq = lax.fori_loop(0, heads, one_head, (none, none))
+    lin, sq = lax.fori_loop(0, heads, one_head, (none, none), unroll=8)
     out_ref[0] = lin
     out_ref[1] = sq
 
@@ -431,6 +449,7 @@
         return lax.optimization_barrier((*arrays, *others))[: len(arrays)]
 
     row_positions = global_positions.reshape(1, glob)
+    weights = score_weight.reshape(HEADS, head_size)
     small = ((glob, half), bf16)
     pair_of = ((2 * glob, half), bf16)
     three = ((3 * glob, half), bf16)
@@ -462,11 +481,16 @@
         [((tokens + 2 * BLK, half), bf16)],
         micros=1.6,
     )
-    near_acc, near_stat = call(
+    near_acc, near_stat, bias, weight_cols = call(
         functools.partial(near_kernel, scale2),
         "near_attention",
-        [((half_heads, n_pairs, head_size, LANES), f32), ((half_heads, 2, n_pairs, LANES), f32)],
-        [q_t, k_all, v_t, edge_a, edge_b],
+        [
+            ((half_heads, n_pairs, head_size, LANES), f32),
+            ((half_heads, 2, n_pairs, LANES), f32),
+            ((n_pairs, glob, LANES), f32),
+            ((half_heads, LANES, LANES), f32),
+        ],
+        [q_t, k_all, v_t, edge_a, edge_b, weights, row_positions],
         [((n_pairs, 4 * BLK, LANES), f32), ((n_pairs, 4 * BLK, LANES), bf16), ((2, 2 * BLK, half), bf16)],
         micros=4.0,
     )
@@ -489,7 +513,6 @@
         [((half_heads // 2, tokens, LANES), f32), ((half_heads // 2, tokens + 2 * BLK, LANES), bf16)],
         micros=20.0,
     )
-    weights = score_weight.reshape(HEADS, head_size)
     if chips == 3:
         message = call(
             functools.partial(inward_kernel, scale2), "merge_partial", part, [message, after((move(message, inward),), kv_near)[0]]
@@ -510,12 +533,10 @@
         functools.partial(far_kernel, scale2),
         "far_attention",
         ((2, n_pairs, LANES), f32),
-        [q_t, near_acc, near_stat, kv_near, kv_far, weights, row_positions],
+        [q_t, near_acc, near_stat, kv_near, kv_far, bias, weight_cols],
         [
-            ((n_pairs, glob, LANES), f32),
-            ((n_pairs, glob, LANES), bf16),
-            ((n_pairs, glob, LANES), f32),
-            ((half_heads, LANES, LANES), f32),
+            ((half_heads, n_pairs, glob, LANES), f32),
+            ((half_heads, n_pairs, glob, LANES), bf16),
         ],
         micros=2.0,
     )

time: 50.2 us -> 48.8 us (0.972)
  Pallas kernels: 14.5 us -> 13.5 us
    pallas_call x13, Pallas kernels: 14.5 us -> 13.5 us  [call(): pl.pallas_call(kernel, in_specs=[pl.BlockSpec(memory_space=source)] * len...]
  transfers between devices with their start and end apart: 12 -> 12, of which waited for: 9 -> 9; matrix products, arithmetic and copies ran while one was open for 0% -> 0% of each run, Pallas kernels for 15% -> 17%
where the time goes in v6:
time: 48.8 us; the launch traced here: 48.6 us
  starting transfers between devices  19.5 us (40%)
  waiting for transfers between devices  14.9 us (31%)
  Pallas kernels  13.5 us (28%)
  other arithmetic  0.59 us (1%)
    pallas_call x13, Pallas kernels, call(): pl.pallas_call(kernel, in_specs=[pl.BlockSpec(memory_space=source)] * len...  13.5 us
    ppermute x8, starting transfers between devices, swap(): return lax.ppermute(x, 'seq', [(i, i ^ mask) for i in range(seq_count)])  12 us
    ppermute x8, waiting for transfers between devices, swap(): return lax.ppermute(x, 'seq', [(i, i ^ mask) for i in range(seq_count)])  8.23 us
    ppermute x3, starting transfers between devices, move(): lax.ppermute(x, 'seq', [(a * CORES + c, b * CORES + c) for a, b in pairs...  6.19 us
    ppermute x3, waiting for transfers between devices, move(): lax.ppermute(x, 'seq', [(a * CORES + c, b * CORES + c) for a, b in pairs...  5.62 us
    ppermute x1, starting transfers between devices, move_cores(): lax.ppermute(x, 'seq', [(i, to) for i, to in moves if 0 <= to < seq_count])  1.28 us
    ppermute x1, waiting for transfers between devices, move_cores(): lax.ppermute(x, 'seq', [(i, to) for i, to in moves if 0 <= to < seq_count])  1.06 us
  transfers between devices with their start and end apart: 12, of which 9 were waited for; matrix products, arithmetic and copies ran while one was open for 0% of the time, Pallas kernels for 17%

profile of v6, /device:TPU:0, one launch (start us, length us, event | category | flops | bytes accessed | tf_op | source)
XLA Modules:
  0.0 48.6 jit_solution(2703988488800422295)
XLA Ops:
  0.0 2.8 %select_rows.1 = (bf16[192,1024]{1,0:T(8,128)(2,1)S(1)}, bf16[192,1024]{1,0:T(8,128)(2,1)S(1)}, bf16[128,2048]{1,0:T(8,128)(2,1)S(1)}, bf16[1152,1024]{1,0:T(8,128)(2,1)S(1)}, bf16[1152,1024]{1,0:T(8,128)(2,1)S(1)}) custom-call(s32[1,64]{1,0:T(1,128)} %bitcast.6, bf16[384,2048]{1,0:T(8,128)(2,1)} %q_hbm.1, bf16[384,2048]{1,0:T(8,128)(2,1)} %k_hbm.1, ...), custom_call_target="tpu_custom_call" | custom-call | flops 1 | bytes 1 | tf_op jit(solution)/shard_map/select_rows/pallas_call | solution.py:406
  2.8 0.5 %collective-permute-start = (bf16[192,1024]{1,0:T(8,128)(2,1)S(1)}, bf16[192,1024]{1,0:T(8,128)(2,1)S(1)}, u32[]{:S(2)}, u32[]{:S(2)}) collective-permute-start(bf16[192,1024]{1,0:T(8,128)(2,1)S(1)} %get-tuple-element.27), channel_id=1, source_target_pairs={{0,1},{1,0},{2,3},{3,2},{4,5},{5,4},{6,7},{7,6},{8,9},{9,8},{10,11... | collective-permute-start | bytes 1179656 | tf_op jit(solution)/shard_map/ppermute | solution.py:435
  3.4 1.3 %collective-permute-done.recv_ref = bf16[192,1024]{1,0:T(8,128)(2,1)S(1)} collective-permute-done((bf16[192,1024]{1,0:T(8,128)(2,1)S(1)}, bf16[192,1024]{1,0:T(8,128)(2,1)S(1)}, u32[]{:S(2)}, u32[]{:S(2)}) %collective-permute-start) | collective-permute-done | bytes 393248 | tf_op jit(solution)/shard_map/ppermute | solution.py:435
  4.8 0.4 collective-permute-start.3
  5.2 2.7 %collective-permute-start.1 = (bf16[64,1024]{1,0:T(8,128)(2,1)S(1)}, bf16[64,1024]{1,0:T(8,128)(2,1)S(1)}, u32[]{:S(2)}, u32[]{:S(2)}) collective-permute-start(bf16[64,1024]{1,0:T(8,128)(2,1)S(1)} %get-tuple-element.28.a_ref), channel_id=1, source_target_pairs={{0,2},{1,3},{2,0},{3,1},{4,6},{5,7},{6,4},{7,5},{8,10},{9,11},{10,... | collective-permute-start | bytes 393224 | tf_op jit(solution)/shard_map/ppermute | solution.py:435
  7.9 1.3 %collective-permute-start.8 = (bf16[128,2048]{1,0:T(8,128)(2,1)S(1)}, bf16[128,2048]{1,0:T(8,128)(2,1)S(1)}, u32[]{:S(2)}, u32[]{:S(2)}) collective-permute-start(bf16[128,2048]{1,0:T(8,128)(2,1)S(1)} %get-tuple-element.39), channel_id=1, source_target_pairs={{1,3},{2,0},{3,5},{4,2},{5,7},{6,4},{9,11},{10,8},{11,13},{12,10},... | collective-permute-start | bytes 1572872 | tf_op jit(solution)/shard_map/ppermute | solution.py:439
  9.2 2.7 %collective-permute-done.1.b_ref = bf16[64,1024]{1,0:T(8,128)(2,1)S(1)} collective-permute-done((bf16[64,1024]{1,0:T(8,128)(2,1)S(1)}, bf16[64,1024]{1,0:T(8,128)(2,1)S(1)}, u32[]{:S(2)}, u32[]{:S(2)}) %collective-permute-start.1) | collective-permute-done | bytes 131104 | tf_op jit(solution)/shard_map/ppermute | solution.py:435
  12.0 0.0 collective-permute-done.3.sib_ref
  12.0 1.6 %prepare.1 = (bf16[896,1024]{1,0:T(8,128)(2,1)S(1)}, bf16[1024,896]{1,0:T(8,128)(2,1)S(1)}, bf16[1024,768]{1,0:T(8,128)(2,1)S(1)}) custom-call(bf16[1152,1024]{1,0:T(8,128)(2,1)S(1)} %get-tuple-element.29.own_ref, bf16[1152,1024]{1,0:T(8,128)(2,1)S(1)} %collective-permute-done.3.sib_ref), custom_call_target="tpu_custom_call" | custom-call | flops 1600000000 | bytes 1 | tf_op jit(solution)/shard_map/prepare/pallas_call | solution.py:406
  13.6 4.2 %collective-permute-start.5 = (bf16[128,1024]{1,0:T(8,128)(2,1)S(1)}, bf16[128,1024]{1,0:T(8,128)(2,1)S(1)}, u32[]{:S(2)}, u32[]{:S(2)}) collective-permute-start(bf16[128,1024]{1,0:T(8,128)(2,1)S(1)} %get-tuple-element.36.a_ref), channel_id=1, source_target_pairs={{0,2},{1,3},{6,4},{7,5},{8,10},{9,11},{14,12},{15,13},{16,18},{17,... | collective-permute-start | bytes 786440 | tf_op jit(solution)/shard_map/ppermute | solution.py:442
  17.8 0.1 collective-permute-start.2
  17.9 1.1 %collective-permute-done.8.full_ref.edge_a_ref = bf16[128,2048]{1,0:T(8,128)(2,1)S(1)} collective-permute-done((bf16[128,2048]{1,0:T(8,128)(2,1)S(1)}, bf16[128,2048]{1,0:T(8,128)(2,1)S(1)}, u32[]{:S(2)}, u32[]{:S(2)}) %collective-permute-start.8) | collective-permute-done | bytes 524320 | tf_op jit(solution)/shard_map/ppermute | solution.py:439
  19.0 0.1 collective-permute-start.9
  19.1 4.9 %collective-permute-done.5.b_ref = bf16[128,1024]{1,0:T(8,128)(2,1)S(1)} collective-permute-done((bf16[128,1024]{1,0:T(8,128)(2,1)S(1)}, bf16[128,1024]{1,0:T(8,128)(2,1)S(1)}, u32[]{:S(2)}, u32[]{:S(2)}) %collective-permute-start.5) | collective-permute-done | bytes 262176 | tf_op jit(solution)/shard_map/ppermute | solution.py:442
  24.0 0.7 %collective-permute-start.6 = (bf16[128,1024]{1,0:T(8,128)(2,1)S(1)}, bf16[128,1024]{1,0:T(8,128)(2,1)S(1)}, u32[]{:S(2)}, u32[]{:S(2)}) collective-permute-start(bf16[128,1024]{1,0:T(8,128)(2,1)S(1)} %add_keys_values.2.a_ref), channel_id=1, source_target_pairs={{2,4},{3,5},{4,2},{5,3},{10,12},{11,13},{12,10},{13,11},{18,20},{1... | collective-permute-start | bytes 786440 | tf_op jit(solution)/shard_map/ppermute | solution.py:442
  24.7 0.7 %collective-permute-done.2.q_b_ref = bf16[64,1024]{1,0:T(8,128)(2,1)S(1)} collective-permute-done((bf16[64,1024]{1,0:T(8,128)(2,1)S(1)}, bf16[64,1024]{1,0:T(8,128)(2,1)S(1)}, u32[]{:S(2)}, u32[]{:S(2)}) %collective-permute-start.2) | collective-permute-done | bytes 131104 | tf_op jit(solution)/shard_map/ppermute | solution.py:435
  25.3 0.0 copy-start
  25.3 0.0 copy-start.1
  25.4 1.4 %global_partial.1.a_ref = bf16[4,144,128]{2,1,0:T(8,128)(2,1)S(1)} custom-call(bf16[64,1024]{1,0:T(8,128)(2,1)S(1)} %add_queries.1.q_a_ref, bf16[64,1024]{1,0:T(8,128)(2,1)S(1)} %collective-permute-done.2.q_b_ref, bf16[896,1024]{1,0:T(8,128)(2,1)S(1)} %get-tuple-element.33.k_ref, bf16[1024,896]{1,0:T(8,128)(2,1)S(1)} %get-tuple-element.34.v_t_ref), custom_call_target="tpu_custom_call" | custom-call | flops 20000000000 | bytes 1 | tf_op jit(solution)/shard_map/global_partial/pallas_call | solution.py:406
  26.7 5.5 %collective-permute-start.4 = (bf16[4,144,128]{2,1,0:T(8,128)(2,1)S(1)}, bf16[4,144,128]{2,1,0:T(8,128)(2,1)S(1)}, u32[]{:S(2)}, u32[]{:S(2)}) collective-permute-start(bf16[4,144,128]{2,1,0:T(8,128)(2,1)S(1)} %global_partial.1.a_ref), channel_id=1, source_target_pairs={{0,2},{1,3},{2,0},{3,1},{4,6},{5,7},{6,4},{7,5},{8,10},{9,11},{10,... | collective-permute-start | bytes 442376 | tf_op jit(solution)/shard_map/ppermute | solution.py:435
  32.3 0.0 collective-permute-done.6.b_ref
  32.3 1.3 %collective-permute-start.10 = (bf16[128,1024]{1,0:T(8,128)(2,1)S(1)}, bf16[128,1024]{1,0:T(8,128)(2,1)S(1)}, u32[]{:S(2)}, u32[]{:S(2)}) collective-permute-start(bf16[128,1024]{1,0:T(8,128)(2,1)S(1)} %add_keys_values.3.kv_a_ref), channel_id=1, source_target_pairs={{2,0},{3,1},{4,6},{5,7},{10,8},{11,9},{12,14},{13,15},{18,16},{19,... | collective-permute-start | bytes 786440 | tf_op jit(solution)/shard_map/ppermute | solution.py:442
  33.6 1.8 %collective-permute-done.4.b_ref = bf16[4,144,128]{2,1,0:T(8,128)(2,1)S(1)} collective-permute-done((bf16[4,144,128]{2,1,0:T(8,128)(2,1)S(1)}, bf16[4,144,128]{2,1,0:T(8,128)(2,1)S(1)}, u32[]{:S(2)}, u32[]{:S(2)}) %collective-permute-start.4) | collective-permute-done | bytes 147488 | tf_op jit(solution)/shard_map/ppermute | solution.py:435
  35.4 0.1 merge_partial.1.a_ref
  35.5 2.6 %collective-permute-start.7 = (bf16[4,144,128]{2,1,0:T(8,128)(2,1)S(1)}, bf16[4,144,128]{2,1,0:T(8,128)(2,1)S(1)}, u32[]{:S(2)}, u32[]{:S(2)}) collective-permute-start(bf16[4,144,128]{2,1,0:T(8,128)(2,1)S(1)} %merge_partial.1.a_ref), channel_id=1, source_target_pairs={{0,4},{1,5},{2,6},{3,7},{4,0},{5,1},{6,2},{7,3},{8,12},{9,13},{10,... | collective-permute-start | bytes 442376 | tf_op jit(solution)/shard_map/ppermute | solution.py:435
  38.1 0.0 collective-permute-done.9.edge_b_ref
  38.1 0.0 copy-done
  38.1 0.0 copy-done.1
  38.1 4.6 %near_attention.1 = (f32[8,6,128,128]{3,2,1,0:T(8,128)S(1)}, f32[8,2,6,128]{3,2,1,0:T(8,128)S(1)}, f32[6,64,128]{2,1,0:T(8,128)S(1)}, f32[8,128,128]{2,1,0:T(8,128)S(1)}) custom-call(bf16[1024,768]{1,0:T(8,128)(2,1)S(1)} %get-tuple-element.38.q_t_ref, bf16[896,1024]{1,0:T(8,128)(2,1)S(1)} %get-tuple-element.33.k_ref, ...), custom_call_target="tpu_custom_call" | custom-call | flops 4000000000 | bytes 1 | tf_op jit(solution)/shard_map/near_attention/pallas_call | solution.py:406
  42.8 0.5 %collective-permute-done.7.b_ref = bf16[4,144,128]{2,1,0:T(8,128)(2,1)S(1)} collective-permute-done((bf16[4,144,128]{2,1,0:T(8,128)(2,1)S(1)}, bf16[4,144,128]{2,1,0:T(8,128)(2,1)S(1)}, u32[]{:S(2)}, u32[]{:S(2)}) %collective-permute-start.7) | collective-permute-done | bytes 147488 | tf_op jit(solution)/shard_map/ppermute | solution.py:435
  43.3 0.2 global_sums.1.own_sums_ref.far_sums_ref
  43.5 0.8 %collective-permute-done.10.kv_b_ref = bf16[128,1024]{1,0:T(8,128)(2,1)S(1)} collective-permute-done((bf16[128,1024]{1,0:T(8,128)(2,1)S(1)}, bf16[128,1024]{1,0:T(8,128)(2,1)S(1)}, u32[]{:S(2)}, u32[]{:S(2)}) %collective-permute-start.10) | collective-permute-done | bytes 262176 | tf_op jit(solution)/shard_map/ppermute | solution.py:442
  44.3 2.2 %far_attention.1.win_ref = f32[2,6,128]{2,1,0:T(8,128)S(1)} custom-call(bf16[1024,768]{1,0:T(8,128)(2,1)S(1)} %get-tuple-element.38.q_t_ref, f32[8,6,128,128]{3,2,1,0:T(8,128)S(1)} %get-tuple-element.41.acc_ref, f32[8,2,6,128]{3,2,1,0:T(8,128)S(1)} %get-tuple-element.42.stat_ref, bf16[128,1024]{1,0:T(8,128)(2,1)S(1)} %add_keys_values.3.kv_a_ref, ...), custom_call_target="tpu_custom_call" | custom-call | flops 2000000000 | bytes 1 | tf_op jit(solution)/shard_map/far_attention/pallas_call | solution.py:406
  46.5 0.3 place_global.1
  46.8 0.1 collective-permute-start.11
  46.9 1.2 %collective-permute-done.11 = f32[2,3,128]{2,1,0:T(4,128)S(1)} collective-permute-done((f32[2,3,128]{2,1,0:T(4,128)S(1)}, f32[2,3,128]{2,1,0:T(4,128)S(1)}, u32[]{:S(2)}, u32[]{:S(2)}) %collective-permute-start.11) | collective-permute-done | bytes 3104 | tf_op jit(solution)/shard_map/ppermute | solution.py:435
  48.0 0.6 %fusion.4 = f32[384]{0:T(512)} fusion(f32[2,3,128]{2,1,0:T(4,128)S(1)} %collective-permute-done.11, f32[2,3,128]{2,1,0:T(4,128)S(1)} %get-tuple-element.45), kind=kLoop, calls=%fused_computation.5 | loop fusion | flops 1920 | bytes 7680 | tf_op jit(solution)/shard_map/mul | solution.py:550
  (5 shorter events, 0.1 us)
Async XLA Ops:
  2.8 1.9 %collective-permute-start = (bf16[192,1024]{1,0:T(8,128)(2,1)S(1)}, bf16[192,1024]{1,0:T(8,128)(2,1)S(1)}, u32[]{:S(2)}, u32[]{:S(2)}) collective-permute-start(bf16[192,1024]{1,0:T(8,128)(2,1)S(1)} %get-tuple-element.27), channel_id=1, source_target_pairs={{0,1},{1,0},{2,3},{3,2},{4,5},{5,4},{6,7},{7,6},{8,9},{9,8},{10,11... | collective-permute-start | bytes 1179656 | tf_op jit(solution)/shard_map/ppermute | solution.py:435
  4.8 7.2 %collective-permute-start.3 = (bf16[1152,1024]{1,0:T(8,128)(2,1)S(1)}, bf16[1152,1024]{1,0:T(8,128)(2,1)S(1)}, u32[]{:S(2)}, u32[]{:S(2)}) collective-permute-start(bf16[1152,1024]{1,0:T(8,128)(2,1)S(1)} %get-tuple-element.31), channel_id=1, source_target_pairs={{0,1},{1,0},{2,3},{3,2},{4,5},{5,4},{6,7},{7,6},{8,9},{9,8},{10,11... | collective-permute-start | bytes 7077896 | tf_op jit(solution)/shard_map/ppermute | solution.py:435
  5.2 6.7 %collective-permute-start.1 = (bf16[64,1024]{1,0:T(8,128)(2,1)S(1)}, bf16[64,1024]{1,0:T(8,128)(2,1)S(1)}, u32[]{:S(2)}, u32[]{:S(2)}) collective-permute-start(bf16[64,1024]{1,0:T(8,128)(2,1)S(1)} %get-tuple-element.28.a_ref), channel_id=1, source_target_pairs={{0,2},{1,3},{2,0},{3,1},{4,6},{5,7},{6,4},{7,5},{8,10},{9,11},{10,... | collective-permute-start | bytes 393224 | tf_op jit(solution)/shard_map/ppermute | solution.py:435
  7.9 11.1 %collective-permute-start.8 = (bf16[128,2048]{1,0:T(8,128)(2,1)S(1)}, bf16[128,2048]{1,0:T(8,128)(2,1)S(1)}, u32[]{:S(2)}, u32[]{:S(2)}) collective-permute-start(bf16[128,2048]{1,0:T(8,128)(2,1)S(1)} %get-tuple-element.39), channel_id=1, source_target_pairs={{1,3},{2,0},{3,5},{4,2},{5,7},{6,4},{9,11},{10,8},{11,13},{12,10},... | collective-permute-start | bytes 1572872 | tf_op jit(solution)/shard_map/ppermute | solution.py:439
  13.6 10.3 %collective-permute-start.5 = (bf16[128,1024]{1,0:T(8,128)(2,1)S(1)}, bf16[128,1024]{1,0:T(8,128)(2,1)S(1)}, u32[]{:S(2)}, u32[]{:S(2)}) collective-permute-start(bf16[128,1024]{1,0:T(8,128)(2,1)S(1)} %get-tuple-element.36.a_ref), channel_id=1, source_target_pairs={{0,2},{1,3},{6,4},{7,5},{8,10},{9,11},{14,12},{15,13},{16,18},{17,... | collective-permute-start | bytes 786440 | tf_op jit(solution)/shard_map/ppermute | solution.py:442
  17.8 7.5 %collective-permute-start.2 = (bf16[64,1024]{1,0:T(8,128)(2,1)S(1)}, bf16[64,1024]{1,0:T(8,128)(2,1)S(1)}, u32[]{:S(2)}, u32[]{:S(2)}) collective-permute-start(bf16[64,1024]{1,0:T(8,128)(2,1)S(1)} %add_queries.1.q_a_ref), channel_id=1, source_target_pairs={{0,4},{1,5},{2,6},{3,7},{4,0},{5,1},{6,2},{7,3},{8,12},{9,13},{10,... | collective-permute-start | bytes 393224 | tf_op jit(solution)/shard_map/ppermute | solution.py:435
  19.0 19.1 %collective-permute-start.9 = (bf16[128,1024]{1,0:T(8,128)(2,1)S(1)}, bf16[128,1024]{1,0:T(8,128)(2,1)S(1)}, u32[]{:S(2)}, u32[]{:S(2)}) collective-permute-start(bf16[128,1024]{1,0:T(8,128)(2,1)S(1)} %split_edges.1), channel_id=1, source_target_pairs={{0,1},{1,0},{2,3},{3,2},{4,5},{5,4},{6,7},{7,6},{8,9},{9,8},{10,11... | collective-permute-start | bytes 786440 | tf_op jit(solution)/shard_map/ppermute | solution.py:435
  24.0 8.3 %collective-permute-start.6 = (bf16[128,1024]{1,0:T(8,128)(2,1)S(1)}, bf16[128,1024]{1,0:T(8,128)(2,1)S(1)}, u32[]{:S(2)}, u32[]{:S(2)}) collective-permute-start(bf16[128,1024]{1,0:T(8,128)(2,1)S(1)} %add_keys_values.2.a_ref), channel_id=1, source_target_pairs={{2,4},{3,5},{4,2},{5,3},{10,12},{11,13},{12,10},{13,11},{18,20},{1... | collective-permute-start | bytes 786440 | tf_op jit(solution)/shard_map/ppermute | solution.py:442
  25.3 12.8 %copy-start = (f32[2048]{0:T(1024)S(1)}, f32[2048]{0:T(1024)}, u32[]{:S(2)}) copy-start(f32[2048]{0:T(1024)} %param.9) | copy-start | bytes 24580
  25.3 12.8 %copy-start.1 = (s32[64]{0:T(128)S(1)}, s32[64]{0:T(128)}, u32[]{:S(2)}) copy-start(s32[64]{0:T(128)} %param.8) | copy-start | bytes 772
  26.7 8.7 %collective-permute-start.4 = (bf16[4,144,128]{2,1,0:T(8,128)(2,1)S(1)}, bf16[4,144,128]{2,1,0:T(8,128)(2,1)S(1)}, u32[]{:S(2)}, u32[]{:S(2)}) collective-permute-start(bf16[4,144,128]{2,1,0:T(8,128)(2,1)S(1)} %global_partial.1.a_ref), channel_id=1, source_target_pairs={{0,2},{1,3},{2,0},{3,1},{4,6},{5,7},{6,4},{7,5},{8,10},{9,11},{10,... | collective-permute-start | bytes 442376 | tf_op jit(solution)/shard_map/ppermute | solution.py:435
  32.3 12.0 %collective-permute-start.10 = (bf16[128,1024]{1,0:T(8,128)(2,1)S(1)}, bf16[128,1024]{1,0:T(8,128)(2,1)S(1)}, u32[]{:S(2)}, u32[]{:S(2)}) collective-permute-start(bf16[128,1024]{1,0:T(8,128)(2,1)S(1)} %add_keys_values.3.kv_a_ref), channel_id=1, source_target_pairs={{2,0},{3,1},{4,6},{5,7},{10,8},{11,9},{12,14},{13,15},{18,16},{19,... | collective-permute-start | bytes 786440 | tf_op jit(solution)/shard_map/ppermute | solution.py:442
  35.5 7.8 %collective-permute-start.7 = (bf16[4,144,128]{2,1,0:T(8,128)(2,1)S(1)}, bf16[4,144,128]{2,1,0:T(8,128)(2,1)S(1)}, u32[]{:S(2)}, u32[]{:S(2)}) collective-permute-start(bf16[4,144,128]{2,1,0:T(8,128)(2,1)S(1)} %merge_partial.1.a_ref), channel_id=1, source_target_pairs={{0,4},{1,5},{2,6},{3,7},{4,0},{5,1},{6,2},{7,3},{8,12},{9,13},{10,... | collective-permute-start | bytes 442376 | tf_op jit(solution)/shard_map/ppermute | solution.py:435
  46.8 1.2 %collective-permute-start.11 = (f32[2,3,128]{2,1,0:T(4,128)S(1)}, f32[2,3,128]{2,1,0:T(4,128)S(1)}, u32[]{:S(2)}, u32[]{:S(2)}) collective-permute-start(f32[2,3,128]{2,1,0:T(4,128)S(1)} %get-tuple-element.46), channel_id=1, source_target_pairs={{0,1},{1,0},{2,3},{3,2},{4,5},{5,4},{6,7},{7,6},{8,9},{9,8},{10,11... | collective-permute-start | bytes 9224 | tf_op jit(solution)/shard_map/ppermute | solution.py:435
